TPU v7x, 128 devices: a whole 4x4x4 slice. The times are simulated.
128 devices in a mesh: dom: 128 (over x, z, y, core).
Axes of the slice: x: 4, y: 4, z: 4, core: 2. Of those that a mesh axis runs over, the one named last changes fastest.
Arguments:
- features: bfloat16 [65536, 512], P('dom'), may hold values from -6 to 6
- weight_self: bfloat16 [512, 512], replicated, may hold values from -0.25 to 0.25
- weight_neigh: bfloat16 [512, 512], replicated, may hold values from -3 to 3
- local_weight: bfloat16 [65536, 512], P('dom'), may hold values from 0.049804688 to 1
- tile_cols: int32 [512, 4], P('dom'), may hold values from 0 to 3
- cut_weight: bfloat16 [65536, 512], P('dom'), may hold values from 0.049804688 to 1
- send_rows: int32 [16384, 4], P('dom'), may hold values from 0 to 255
- send_count: int32 [128, 128], P(None, 'dom'), may hold values from 0 to 4, as said below
- hub_rows: int32 [2048], P('dom'), may hold values from 0 to 255
- hub_edges: int32 [65536, 8], P('dom'), may hold values from 0 to 2047
- hub_weight: bfloat16 [65536, 8], P('dom'), may hold values from 1 to 16
- row_counts: int32 [128], P('dom'), may hold values from 256 to 512, as said below
- cotangent: bfloat16 [65536, 512], P('dom'), may hold values from -6 to 6
Outputs:
- activated: bfloat16 [65536, 512], P('dom')
- feature_grad: bfloat16 [65536, 512], P('dom')
- grad_self: float32 [512, 512], replicated
- grad_neigh: float32 [512, 512], replicated
Inputs may be any that keep to these rules, and one draw needn't show every extreme that they name: `send_count`: the used slots from one partition to another are the first ones; some partition receives all 4 slots from every partition. `row_counts`: the live rows of a partition are its leading rows; some partition has all rows live. `hub_rows`: hub h is owned by partition h // 16; its row there is live. `send_rows`: every sent row is live.
All inputs are finite; a program needn't handle non-finite values.
Results may differ from a plain program's by a relative error of at most 0.0056.
Values may be sent and summed in bfloat16 or wider, within the bound.
No kernel may reach another device: no remote copies, remote signals or barrier semaphores. Data moves between devices by JAX's collectives and lax.ppermute only.
A program may use at most 64 MiB of HBM per device.

v0:
```python
import jax
import jax.numpy as jnp
from jax import lax
from jax.experimental import pallas as pl
from jax.experimental.pallas import tpu as pltpu
from jax.sharding import Mesh
from jax.sharding import PartitionSpec as P


TILE = 128
TPR = 4
DOM = ("dom_0", "dom_1", "dom_2", "dom_3")
CHIPS = DOM[:3]
CORE = "dom_3"
BF = jnp.bfloat16
F32 = jnp.float32
REACH = 256


VM = pl.BlockSpec(memory_space=pltpu.VMEM)
SM = pl.BlockSpec(memory_space=pltpu.SMEM)
LIMIT = 8 << 20


def call(body, outs, specs, flops, *args, scratch=()):
    size = sum(a.size * a.dtype.itemsize for a in args)
    size += sum(o.size * o.dtype.itemsize for o in outs)
    return pl.pallas_call(
        body,
        out_shape=tuple(outs),
        in_specs=list(specs),
        out_specs=tuple([VM] * len(outs)),
        scratch_shapes=list(scratch),
        compiler_params=pltpu.CompilerParams(vmem_limit_bytes=LIMIT),
        cost_estimate=pl.CostEstimate(flops=flops, bytes_accessed=size, transcendentals=0),
    )(*args)


def mm(a, b):
    return jnp.dot(a, b, preferred_element_type=F32)


def mm_nt(a, b):
    return lax.dot_general(a, b, (((1,), (1,)), ((), ())), preferred_element_type=F32)


def mm_tn(a, b):
    return lax.dot_general(a, b, (((0,), (0,)), ((), ())), preferred_element_type=F32)


def pair(x):
    return lax.ppermute(x, CORE, [(0, 1), (1, 0)])


def over_chips(x):
    return lax.all_to_all(x, CHIPS, 0, 0, tiled=True)


def iota(shape, dim):
    return lax.broadcasted_iota(jnp.int32, shape, dim)


def ones_where(cond):
    return jnp.where(cond, 1.0, 0.0).astype(BF)


def small(ids):
    return ids.astype(F32).astype(BF)


def across(table, width):
    deep, peers = table.shape
    fan = ones_where(iota((peers, width), 0) == iota((peers, width), 1) // deep)
    wide = mm(small(table), fan)
    keep = iota((deep, width), 0) == iota((deep, width), 1) % deep
    return jnp.sum(jnp.where(keep, wide, 0.0), axis=0, keepdims=True)


def send(routes, hub_ids, feats, out):
    feat = feats.shape[1]
    deep, peers = routes.shape
    slots = deep * peers
    width = hub_ids.shape[1]
    same = iota((width, width), 0) == iota((width, width), 1)
    hub = jnp.sum(jnp.where(same, hub_ids[...].astype(F32), 0.0), axis=1, keepdims=True)
    slab = mm(ones_where(hub.astype(jnp.int32) == iota((width, REACH), 1)), feats[:REACH, :])
    out[:, :width, :] = jnp.broadcast_to(slab.astype(BF)[None], (out.shape[0], width, feat))
    fan = ones_where(iota((slots, peers), 1) == iota((slots, peers), 0) // deep)
    wide = mm_nt(fan, small(routes[...]))
    keep = iota((slots, deep), 1) == iota((slots, deep), 0) % deep
    row = jnp.sum(jnp.where(keep, wide, 0.0), axis=1, keepdims=True).astype(jnp.int32)
    rows = mm(ones_where(row == iota((slots, REACH), 1)), feats[:REACH, :])
    out[:, width:, :] = rows.astype(BF).reshape(out.shape[0], slots // out.shape[0], feat)


def ahead(
    cols,
    count,
    core,
    feats,
    lweight,
    cweight,
    counts,
    edges,
    hubw,
    wself,
    local_sum,
    self_term,
    degree,
    dense,
    flip_own,
    cut_own,
    wide_own,
    wide_far,
    feat_own,
    ship,
    masked,
    picked,
):
    rows, feat = feats.shape
    slots = cweight.shape[1]
    hubs = dense.shape[1]
    blocks = rows // TILE
    live = count[0]
    me = core[0]
    masked[...] = jnp.where(iota((rows, feat), 0) < live, feats[...], jnp.zeros_like(feats))
    self_term[...] = mm(masked[...], wself[...])
    deep = slots // counts.shape[1]
    fan = ones_where(iota((counts.shape[1], slots), 0) == iota((counts.shape[1], slots), 1) // deep)
    used = mm(small(counts[...]), fan)
    on = (iota((1, slots), 1) % deep).astype(F32) < used
    cut = cweight[...] * jnp.broadcast_to(ones_where(on), (rows, slots))
    edge_w = hubw[...]
    hub_deg = mm_tn(edge_w, jnp.ones((edge_w.shape[0], TILE), BF))[:, :1]
    degree[...] = hub_deg + jnp.sum(cut.astype(F32), axis=1, keepdims=True)
    lane = iota((TILE, TILE), 1)
    for r in range(blocks):
        part = jnp.zeros((TILE, 1), F32)
        at = pl.ds(r * TILE, TILE)
        for t in range(TPR):
            base = cols[r, t] * TILE
            picked[pl.ds(t * TILE, TILE), :] = masked[pl.ds(pl.multiple_of(base, TILE), TILE), :]
            vals = lweight[at, pl.ds(t * TILE, TILE)].astype(F32)
            part = part + jnp.sum(jnp.where(lane + base < live, vals, 0.0), axis=1, keepdims=True)
        local_sum[at, :] = mm(lweight[at, :], picked[...])
        degree[at, :] += part
    flip = jnp.transpose(cut)
    side = (iota((slots, rows), 0) // deep) % 2
    kept = jnp.where(side == me, flip, jnp.zeros_like(flip))
    tall = flip.astype(F32)
    up = pltpu.roll(tall, slots - deep, 0)
    down = pltpu.roll(tall, deep, 0)
    moved = jnp.where(side == me, jnp.where(me == 0, up, down), 0.0).astype(BF)
    cut_own[...] = kept
    wide_own[...] = jnp.transpose(kept)
    wide_far[...] = jnp.transpose(moved)
    half = feat // 2
    ship[hubs // 2 : hubs // 2 + slots, :] = moved
    feat_own[...] = jnp.transpose(jnp.where(me == 0, feats[:, :half], feats[:, half:]))
    ship[hubs // 2 + slots :, :] = jnp.transpose(
        jnp.where(me == 0, feats[:, half:], feats[:, :half])
    )
    width = hubs // (2 * (slots // (2 * deep)))
    owner = edges[...] // width
    place = ((owner % 2) ^ me) * (hubs // 2) + (owner // 2) * width + edges[...] % width
    weight = edge_w.astype(F32)
    step = 128

    def build(i, carry):
        base = pl.multiple_of(i * step, step)
        hub = iota((step, rows), 0) + base
        acc = jnp.zeros((step, rows), F32)
        for k in range(edges.shape[0]):
            acc = acc + jnp.where(place[k : k + 1, :] == hub, weight[k : k + 1, :], 0.0)
        flat = acc.astype(BF)
        dense[:, pl.ds(base, step)] = jnp.transpose(flat)

        @pl.when(base < hubs // 2)
        def _():
            flip_own[pl.ds(base, step), :] = flat

        @pl.when(base >= hubs // 2)
        def _():
            ship[pl.ds(pl.multiple_of(base - hubs // 2, step), step), :] = flat

        return carry

    lax.fori_loop(0, hubs // step, build, 0)


def sides(bundle, width, feat):
    peers, deep, _ = bundle.shape
    table = bundle[:, :width, :].reshape(peers * width, feat)
    return table, bundle[:, width:, :].reshape(peers * (deep - width), feat)


def near_sum(local_sum, wide_own, dense, bundle, out):
    _, feat = out.shape
    hubs = dense.shape[1] // 2
    table, cut = sides(bundle, hubs // bundle.shape[0], feat)
    out[...] = local_sum[...] + mm(wide_own[...], cut) + mm(dense[:, :hubs], table)


def forward(core, count, near, wide_far, dense, bundle, degree, self_term, wneigh, cot, act, mean_own, pack):
    rows, feat = near.shape
    hubs = dense.shape[1] // 2
    half = feat // 2
    me = core[0]
    table, cut = sides(bundle, hubs // bundle.shape[0], feat)
    total = near[...] + mm(wide_far[...], cut) + mm(dense[:, hubs:], table)
    mean = (total / degree[...]).astype(BF)
    mean_own[...] = jnp.transpose(jnp.where(me == 0, mean[:, :half], mean[:, half:]))
    pack[:half, :] = jnp.transpose(jnp.where(me == 0, mean[:, half:], mean[:, :half]))
    live = iota((rows, feat), 0) < count[0]
    pre = self_term[...] + mm(mean, wneigh[...])
    sig = jax.nn.sigmoid(pre)
    act[...] = jnp.where(live, pre * sig, 0.0).astype(BF)
    grad = cot[...].astype(F32) * sig * (1.0 + pre * (1.0 - sig))
    pack[half:, :] = jnp.where(live, grad, 0.0).astype(BF)


def back_near(pack, mean_own, feat_own, wneigh, degree, flip_own, cut_own, gmean, hub, cut, weight):
    half = feat_own.shape[0]
    grad = pack[half:, :]
    near = (mm_nt(grad, wneigh[...]) / degree[...]).astype(BF)
    gmean[...] = near
    hub[...] = mm(flip_own[...], near)
    cut[...] = mm(cut_own[...], near)
    weight[:half, :] = mm(feat_own[...], grad)
    weight[half:, :] = mm(mean_own[...], grad)


def back_far(pack, wneigh, degree, ship, hub, cut, weight, out):
    feat = wneigh.shape[0]
    half = feat // 2
    grad = pack[half:, :]
    hubs, slots = hub.shape[0], cut.shape[0]
    peers = out.shape[0]
    a, b = hubs // peers, (hubs + slots) // peers
    far = (mm_nt(grad, wneigh[...]) / degree[...]).astype(BF)
    first = hub[...] + mm(ship[:hubs, :], far)
    out[:, :a, :] = first.astype(BF).reshape(peers, a, feat)
    second = cut[...] + mm(ship[hubs : hubs + slots, :], far)
    out[:, a:b, :] = second.astype(BF).reshape(peers, b - a, feat)
    share = feat // peers
    low = weight[:half, :] + mm(ship[hubs + slots :, :], grad)
    high = weight[half:, :] + mm(pack[:half, :], grad)
    out[: peers // 2, b:, :] = low.astype(BF).reshape(peers // 2, share, feat)
    out[peers // 2 :, b:, :] = high.astype(BF).reshape(peers // 2, share, feat)


def row_terms(cols, pack, wself, lweight, gmean, out):
    rows, feat = out.shape
    out[...] = mm_nt(pack[feat // 2 :, :], wself[...])
    for r in range(rows // TILE):
        at = pl.ds(r * TILE, TILE)
        part = mm_tn(lweight[at, :], gmean[at, :])
        for t in range(TPR):
            base = pl.multiple_of(cols[r, t] * TILE, TILE)
            out[pl.ds(base, TILE), :] += part[t * TILE : (t + 1) * TILE, :]


def spread(bundle, out):
    share = out.shape[1]
    first = bundle.shape[1] - share
    total = jnp.sum(bundle[:, first:, :].astype(F32), axis=0)
    out[...] = jnp.broadcast_to(total.astype(BF)[None], out.shape)


def finish(count, rows_in, routes, hub_ids, bundle, out):
    rows, feat = rows_in.shape
    deep, peers = routes.shape
    slots = deep * peers
    chips = bundle.shape[0]
    width = hub_ids.shape[1]
    hubs = chips * width
    ids = across(routes[...], slots).astype(jnp.int32)
    cut = bundle[:, width : width + slots // chips, :].reshape(slots, feat)
    top = mm(ones_where(ids == iota((REACH, slots), 0)), cut)
    fan = ones_where(iota((width, hubs), 0) == iota((width, hubs), 1) % width)
    spots = mm(small(hub_ids[...]), fan).astype(jnp.int32)
    table = bundle[:, :width, :].reshape(hubs, feat)
    top = top + mm(ones_where(spots == iota((REACH, hubs), 0)), table)
    live = iota((rows, feat), 0) < count[0]
    out[:REACH, :] = jnp.where(live[:REACH], rows_in[:REACH, :] + top, 0.0).astype(BF)
    out[REACH:, :] = jnp.where(live[REACH:], rows_in[REACH:, :], 0.0).astype(BF)


def assemble(core, mine, other, first, second):
    peers, share, feat = mine.shape
    half = peers * share // 2
    me = core[0]
    for source, turn in ((mine, me), (other, 1 - me)):
        whole = source[...].reshape(peers * share, feat).astype(F32)
        at = pl.ds(pl.multiple_of(turn * half, half), half)
        first[at, :] = whole[:half, :]
        second[at, :] = whole[half:, :]


def per_device(
    features,
    weight_self,
    weight_neigh,
    local_weight,
    tile_cols,
    cut_weight,
    send_rows,
    send_count,
    hub_rows,
    hub_edges,
    hub_weight,
    row_counts,
    cotangent,
):
    rows, feat = features.shape
    core = lax.axis_index(CORE).astype(jnp.int32).reshape(1)
    chips = lax.axis_size(CHIPS)
    deep = send_rows.shape[1]
    width = hub_rows.shape[0]
    hubs = chips * 2 * width
    slots = chips * 2 * deep
    half = feat // 2
    share = feat // chips
    unit = 2 * 512 * 512 * 512

    def like(shape, kind=BF):
        return jax.ShapeDtypeStruct(shape, kind)

    routes = send_rows.T
    hub_ids = hub_rows.reshape(1, width)
    (bundle,) = call(
        send, [like((chips, width + 2 * deep, feat))], [VM] * 3, unit, routes, hub_ids, features
    )
    bundle = over_chips(bundle)
    (
        local_sum,
        self_term,
        degree,
        dense,
        flip_own,
        cut_own,
        wide_own,
        wide_far,
        feat_own,
        ship,
    ) = call(
        ahead,
        [
            like((rows, feat), F32),
            like((rows, feat), F32),
            like((rows, 1), F32),
            like((rows, hubs)),
            like((hubs // 2, rows)),
            like((slots, rows)),
            like((rows, slots)),
            like((rows, slots)),
            like((half, rows)),
            like((hubs // 2 + slots + half, rows)),
        ],
        [SM, SM, SM] + [VM] * 7,
        40 * unit,
        tile_cols,
        row_counts,
        core,
        features,
        local_weight,
        cut_weight,
        send_count.T,
        hub_edges.T,
        hub_weight.T,
        weight_self,
        scratch=[pltpu.VMEM((rows, feat), BF), pltpu.VMEM((TPR * TILE, feat), BF)],
    )
    degree_far = pair(degree)
    ship_far = pair(ship)

    bundle_far = pair(bundle)
    (near,) = call(near_sum, [like((rows, feat), F32)], [VM] * 4, 3 * unit, local_sum, wide_own, dense, bundle)
    activated, mean_own, pack = call(
        forward,
        [like((rows, feat)), like((half, rows)), like((half + rows, feat))],
        [SM, SM] + [VM] * 8,
        4 * unit,
        core,
        row_counts,
        near,
        wide_far,
        dense,
        bundle_far,
        degree,
        self_term,
        weight_neigh,
        cotangent,
    )
    pack_far = pair(pack)
    gmean, hub_part, cut_part, weight_part = call(
        back_near,
        [like((rows, feat)), like((hubs // 2, feat), F32), like((slots, feat), F32), like((feat, feat), F32)],
        [VM] * 7,
        5 * unit,
        pack,
        mean_own,
        feat_own,
        weight_neigh,
        degree,
        flip_own,
        cut_own,
    )
    (back,) = call(
        back_far,
        [like((chips, width + 2 * deep + share, feat))],
        [VM] * 7,
        5 * unit,
        pack_far,
        weight_neigh,
        degree_far,
        ship_far,
        hub_part,
        cut_part,
        weight_part,
    )
    back = over_chips(back)
    (row_sum,) = call(
        row_terms, [like((rows, feat), F32)], [SM] + [VM] * 4, 3 * unit, tile_cols, pack, weight_self, local_weight, gmean
    )
    (weight_sum,) = call(spread, [like((chips, share, feat))], [VM], 1 << 20, back)
    weight_all = over_chips(weight_sum)
    weight_pair = pair(weight_all)
    (feature_grad,) = call(
        finish,
        [like((rows, feat))],
        [SM] + [VM] * 4,
        2 * unit,
        row_counts,
        row_sum,
        routes,
        hub_ids,
        back,
    )
    grad_self, grad_neigh = call(
        assemble, [like((feat, feat), F32)] * 2, [SM, VM, VM], 1 << 20, core, weight_all, weight_pair
    )
    return activated, feature_grad, grad_self, grad_neigh


def solution(mesh):
    finer = Mesh(mesh.devices.reshape(4, 4, 4, 2), DOM)
    in_specs = (
        P(DOM, None),
        P(),
        P(),
        P(DOM, None),
        P(DOM, None),
        P(DOM, None),
        P(DOM, None),
        P(None, DOM),
        P(DOM),
        P(DOM, None),
        P(DOM, None),
        P(DOM),
        P(DOM, None),
    )
    out_specs = (P(DOM, None), P(DOM, None), P(), P())

    return jax.shard_map(
        per_device, mesh=finer, in_specs=in_specs, out_specs=out_specs, check_vma=False
    )
```

profile of v0, /device:TPU:1, one launch (start us, length us, event | category | flops | bytes accessed | tf_op | source)
XLA Modules:
  0.0 115.5 jit_solution(6331745649216262596)
XLA Ops:
  0.6 0.0 copy-start.2
  0.6 1.0 copy-done.2
  1.7 0.0 copy-start.6
  1.7 0.7 copy-done.6
  2.4 0.0 copy-start.9
  2.4 0.7 copy-done.9
  3.0 1.8 %shard_map.157 = bf16[64,24,512]{2,1,0:T(8,128)(2,1)} custom-call(s32[4,128]{1,0:T(4,128)S(1)} %bitcast.6, s32[1,16]{1,0:T(1,128)S(1)} %bitcast.8, bf16[512,512]{1,0:T(8,128)(2,1)S(1)} %copy-done.2), custom_call_target="tpu_custom_call" | custom-call | flops 268435456 | bytes 2099264 | tf_op jit(solution)/shard_map/pallas_call | solution.py:28
  4.8 0.0 copy-start.3
  4.8 0.0 copy-start.4
  4.8 0.0 copy-start.5
  4.8 0.0 copy-start.8
  4.8 0.0 copy-start.12
  4.8 0.0 copy-start.13
  4.8 0.0 copy-start.14
  4.8 12.1 %all-to-all-start = ((bf16[64,24,512]{2,1,0:T(8,128)(2,1)}), bf16[64,24,512]{2,1,0:T(8,128)(2,1)S(1)}, u32[]{:S(2)}, u32[]{:S(2)}) async-start(bf16[64,24,512]{2,1,0:T(8,128)(2,1)} %shard_map.157), calls=%async_computation | async-start | bytes 3145728 | tf_op jit(solution)/shard_map/all_to_all | solution.py:56
  17.6 21.3 %all-to-all-done.bundle = bf16[64,24,512]{2,1,0:T(8,128)(2,1)S(1)} async-done(((bf16[64,24,512]{2,1,0:T(8,128)(2,1)}), bf16[64,24,512]{2,1,0:T(8,128)(2,1)S(1)}, u32[]{:S(2)}, u32[]{:S(2)}) %all-to-all-start) | async-done | bytes 1572896 | tf_op jit(solution)/shard_map/all_to_all | solution.py:56
  38.9 3.2 %collective-permute-start = (bf16[64,24,512]{2,1,0:T(8,128)(2,1)S(1)}, bf16[64,24,512]{2,1,0:T(8,128)(2,1)S(1)}, u32[]{:S(2)}, u32[]{:S(2)}) collective-permute-start(bf16[64,24,512]{2,1,0:T(8,128)(2,1)S(1)} %all-to-all-done.bundle), channel_id=1, source_target_pairs={{0,1},{1,0},{2,3},{3,2},{4,5},{5,4},{6,7},{7,6},{8,9},{9,8},{10,11... | collective-permute-start | bytes 4718600 | tf_op jit(solution)/shard_map/ppermute | solution.py:52
  42.1 0.0 copy-done.3
  42.1 0.0 copy-done.4
  42.1 0.0 copy-done.5
  42.1 0.0 copy-done.8
  42.1 0.0 copy-done.12
  42.1 0.0 copy-done.13
  42.1 0.0 copy-done.14
  42.1 0.0 copy-start.11
  42.1 1.0 copy-done.11
  43.1 6.5 %shard_map.156 = (f32[512,512]{1,0:T(8,128)S(1)}, f32[512,512]{1,0:T(8,128)S(1)}, f32[512,1]{1,0:T(8,128)S(1)}, bf16[512,2048]{1,0:T(8,128)(2,1)S(1)}, bf16[1024...) custom-call(s32[4,4]{1,0:T(4,128)S(1)} %copy-done.8, ...), custom_call_target="tpu_custom_call" | custom-call | flops 10737418240 | bytes 11037256 | tf_op jit(solution)/shard_map/pallas_call | solution.py:28
  49.7 0.1 collective-permute-start.3
  49.8 0.0 copy-start
  49.8 0.0 copy-start.1
  49.8 1.0 shard_map.158.near
  50.8 0.0 collective-permute-done.bundle
  50.8 0.0 copy-done
  50.8 0.2 copy-done.1
  51.0 2.4 %shard_map.159 = (bf16[512,512]{1,0:T(8,128)(2,1)}, bf16[256,512]{1,0:T(8,128)(2,1)S(1)}, bf16[768,512]{1,0:T(8,128)(2,1)S(1)}) custom-call(s32[1]{0:T(128)} %bitcast.core, s32[1]{0:T(128)S(6)} %copy.17.count, f32[512,512]{1,0:T(8,128)S(1)} %shard_map.158.near, bf16[512,512]{1,0:T(8,128)(2,1)S(1)} %get-tuple-element.26.wide_far, ...), custom_call_target="tpu_custom_call" | custom-call | flops 1073741824 | bytes 8914952 | tf_op jit(solution)/shard_map/pallas_call | solution.py:28
  53.4 0.5 collective-permute-start.1
  53.9 0.0 collective-permute-start.2
  53.9 1.6 %shard_map.160 = (bf16[512,512]{1,0:T(8,128)(2,1)S(1)}, f32[1024,512]{1,0:T(8,128)S(1)}, f32[512,512]{1,0:T(8,128)S(1)}, f32[512,512]{1,0:T(8,128)S(1)}) custom-call(bf16[768,512]{1,0:T(8,128)(2,1)S(1)} %get-tuple-element.30.pack, bf16[256,512]{1,0:T(8,128)(2,1)S(1)} %get-tuple-element.31.mean_own, bf16[256,512]{1,0:T(8,128)(2,1)S(1)} %get-tuple-element.32.feat_own, ...), custom_call_target="tpu_custom_call" | custom-call | flops 1342177280 | bytes 8128512 | tf_op jit(solution)/shard_map/pallas_call | solution.py:28
  55.5 0.6 collective-permute-done.2.degree
  56.2 0.0 collective-permute-done.3.ship
  56.2 0.0 collective-permute-done.1.pack
  56.2 1.7 %shard_map.162 = bf16[64,32,512]{2,1,0:T(8,128)(2,1)S(1)} custom-call(bf16[768,512]{1,0:T(8,128)(2,1)S(1)} %collective-permute-done.1.pack, bf16[512,512]{1,0:T(8,128)(2,1)S(1)} %copy-done, f32[512,1]{1,0:T(8,128)S(1)} %collective-permute-done.2.degree, bf16[1792,512]{1,0:T(8,128)(2,1)S(1)} %collective-permute-done.3.ship, ...), custom_call_target="tpu_custom_call" | custom-call | flops 1342177280 | bytes 9439232 | tf_op jit(solution)/shard_map/pallas_call | solution.py:28
  57.8 31.8 %all_to_all.15.bundle = bf16[64,32,512]{2,1,0:T(8,128)(2,1)S(1)} all-to-all(bf16[64,32,512]{2,1,0:T(8,128)(2,1)S(1)} %shard_map.162), channel_id=1, replica_groups=mesh['dom_0'=4,'dom_1'=4,'dom_2'=4,'dom_3'=2] {'dom_0','dom_1','dom_2'}, dimensions={0} | all-to-all | bytes 4194304 | tf_op jit(solution)/shard_map/all_to_all | solution.py:56
  89.6 0.1 shard_map.164
  89.8 18.5 %all_to_all.16.mine = bf16[64,8,512]{2,1,0:T(8,128)(2,1)S(1)} all-to-all(bf16[64,8,512]{2,1,0:T(8,128)(2,1)S(1)} %shard_map.164), channel_id=1, replica_groups=mesh['dom_0'=4,'dom_1'=4,'dom_2'=4,'dom_3'=2] {'dom_0','dom_1','dom_2'}, dimensions={0} | all-to-all | bytes 1048576 | tf_op jit(solution)/shard_map/all_to_all | solution.py:56
  108.3 0.0 copy-start.7
  108.3 0.0 copy-start.10
  108.3 2.6 %collective-permute-start.4 = (bf16[64,8,512]{2,1,0:T(8,128)(2,1)S(1)}, bf16[64,8,512]{2,1,0:T(8,128)(2,1)S(1)}, u32[]{:S(2)}, u32[]{:S(2)}) collective-permute-start(bf16[64,8,512]{2,1,0:T(8,128)(2,1)S(1)} %all_to_all.16.mine), channel_id=1, source_target_pairs={{0,1},{1,0},{2,3},{3,2},{4,5},{5,4},{6,7},{7,6},{8,9},{9,8},{10,11... | collective-permute-start | bytes 1572872 | tf_op jit(solution)/shard_map/ppermute | solution.py:52
  110.9 1.6 %shard_map.161.rows_in = f32[512,512]{1,0:T(8,128)S(1)} custom-call(s32[4,4]{1,0:T(4,128)S(1)} %copy-done.8, bf16[768,512]{1,0:T(8,128)(2,1)S(1)} %get-tuple-element.30.pack, bf16[512,512]{1,0:T(8,128)(2,1)S(1)} %copy-done.5, bf16[512,512]{1,0:T(8,128)(2,1)S(1)} %copy-done.4, bf16[512,512]{1,0:T(8,128)(2,1)S(1)} %get-tuple-element.35.gmean), custom_call_target="tpu_custom_call" | custom-call | flops 805306368 | bytes 3407936 | tf_op jit(solution)/shard_map/pallas_call | solution.py:28
  112.6 0.0 copy-done.7
  112.6 0.0 copy-done.10
  112.6 1.5 %shard_map.163 = bf16[512,512]{1,0:T(8,128)(2,1)} custom-call(s32[1]{0:T(128)S(6)} %copy.17.count, f32[512,512]{1,0:T(8,128)S(1)} %shard_map.161.rows_in, s32[4,128]{1,0:T(4,128)S(1)} %bitcast.7, s32[1,16]{1,0:T(1,128)S(1)} %bitcast.9, bf16[64,32,512]{2,1,0:T(8,128)(2,1)S(1)} %all_to_all.15.bundle), custom_call_target="tpu_custom_call" | custom-call | flops 536870912 | bytes 3672132 | tf_op jit(solution)/shard_map/pallas_call | solution.py:28
  114.1 0.0 collective-permute-done.4.other
  114.1 1.4 %shard_map.165 = (f32[512,512]{1,0:T(8,128)}, f32[512,512]{1,0:T(8,128)}) custom-call(s32[1]{0:T(128)} %bitcast.core, bf16[64,8,512]{2,1,0:T(8,128)(2,1)S(1)} %all_to_all.16.mine, bf16[64,8,512]{2,1,0:T(8,128)(2,1)S(1)} %collective-permute-done.4.other), custom_call_target="tpu_custom_call" | custom-call | flops 1048576 | bytes 3145732 | tf_op jit(solution)/shard_map/pallas_call | solution.py:28
Async XLA Ops:
  0.6 1.0 copy-start.2
  1.7 0.7 copy-start.6
  2.4 0.7 copy-start.9
  4.8 37.3 %copy-start.3 = (bf16[512,512]{1,0:T(8,128)(2,1)S(1)}, bf16[512,512]{1,0:T(8,128)(2,1)}, u32[]{:S(2)}) copy-start(bf16[512,512]{1,0:T(8,128)(2,1)} %feats.3) | copy-start | bytes 1572868
  4.8 37.3 %copy-start.4 = (bf16[512,512]{1,0:T(8,128)(2,1)S(1)}, bf16[512,512]{1,0:T(8,128)(2,1)}, u32[]{:S(2)}) copy-start(bf16[512,512]{1,0:T(8,128)(2,1)} %lweight.3) | copy-start | bytes 1572868
  4.8 37.3 %copy-start.5 = (bf16[512,512]{1,0:T(8,128)(2,1)S(1)}, bf16[512,512]{1,0:T(8,128)(2,1)}, u32[]{:S(2)}) copy-start(bf16[512,512]{1,0:T(8,128)(2,1)} %wself.3) | copy-start | bytes 1572868
  4.8 37.3 %copy-start.8 = (s32[4,4]{1,0:T(4,128)S(1)}, s32[4,4]{1,0:T(4,128)}, u32[]{:S(2)}) copy-start(s32[4,4]{1,0:T(4,128)} %cols.3) | copy-start | bytes 196
  4.8 37.3 %copy-start.12 = (s32[512,8]{0,1:T(8,128)S(1)}, s32[512,8]{0,1:T(8,128)}, u32[]{:S(2)}) copy-start(s32[512,8]{0,1:T(8,128)} %param.22) | copy-start | bytes 49156
  4.8 37.3 %copy-start.13 = (bf16[512,8]{0,1:T(8,128)(2,1)S(1)}, bf16[512,8]{0,1:T(8,128)(2,1)}, u32[]{:S(2)}) copy-start(bf16[512,8]{0,1:T(8,128)(2,1)} %param.23) | copy-start | bytes 24580
  4.8 37.3 %copy-start.14 = (s32[128,1]{0,1:T(1,128)S(1)}, s32[128,1]{0,1:T(1,128)}, u32[]{:S(2)}) copy-start(s32[128,1]{0,1:T(1,128)} %param.20) | copy-start | bytes 1540
  4.8 34.1 %all-to-all-start = ((bf16[64,24,512]{2,1,0:T(8,128)(2,1)}), bf16[64,24,512]{2,1,0:T(8,128)(2,1)S(1)}, u32[]{:S(2)}, u32[]{:S(2)}) async-start(bf16[64,24,512]{2,1,0:T(8,128)(2,1)} %shard_map.157), calls=%async_computation | async-start | bytes 3145728 | tf_op jit(solution)/shard_map/all_to_all | solution.py:56
  38.9 11.9 %collective-permute-start = (bf16[64,24,512]{2,1,0:T(8,128)(2,1)S(1)}, bf16[64,24,512]{2,1,0:T(8,128)(2,1)S(1)}, u32[]{:S(2)}, u32[]{:S(2)}) collective-permute-start(bf16[64,24,512]{2,1,0:T(8,128)(2,1)S(1)} %all-to-all-done.bundle), channel_id=1, source_target_pairs={{0,1},{1,0},{2,3},{3,2},{4,5},{5,4},{6,7},{7,6},{8,9},{9,8},{10,11... | collective-permute-start | bytes 4718600 | tf_op jit(solution)/shard_map/ppermute | solution.py:52
  42.1 1.0 copy-start.11
  49.7 6.5 %collective-permute-start.3 = (bf16[1792,512]{1,0:T(8,128)(2,1)S(1)}, bf16[1792,512]{1,0:T(8,128)(2,1)S(1)}, u32[]{:S(2)}, u32[]{:S(2)}) collective-permute-start(bf16[1792,512]{1,0:T(8,128)(2,1)S(1)} %get-tuple-element.36), channel_id=1, source_target_pairs={{0,1},{1,0},{2,3},{3,2},{4,5},{5,4},{6,7},{7,6},{8,9},{9,8},{10,11... | collective-permute-start | bytes 5505032 | tf_op jit(solution)/shard_map/ppermute | solution.py:52
  49.8 1.0 copy-start
  49.8 1.2 %copy-start.1 = (bf16[512,512]{1,0:T(8,128)(2,1)S(1)}, bf16[512,512]{1,0:T(8,128)(2,1)}, u32[]{:S(2)}) copy-start(bf16[512,512]{1,0:T(8,128)(2,1)} %cot.1) | copy-start | bytes 1572868
  53.4 2.8 %collective-permute-start.1 = (bf16[768,512]{1,0:T(8,128)(2,1)S(1)}, bf16[768,512]{1,0:T(8,128)(2,1)S(1)}, u32[]{:S(2)}, u32[]{:S(2)}) collective-permute-start(bf16[768,512]{1,0:T(8,128)(2,1)S(1)} %get-tuple-element.30.pack), channel_id=1, source_target_pairs={{0,1},{1,0},{2,3},{3,2},{4,5},{5,4},{6,7},{7,6},{8,9},{9,8},{10,11... | collective-permute-start | bytes 2359304 | tf_op jit(solution)/shard_map/ppermute | solution.py:52
  53.9 2.3 %collective-permute-start.2 = (f32[512,1]{1,0:T(8,128)S(1)}, f32[512,1]{1,0:T(8,128)S(1)}, u32[]{:S(2)}, u32[]{:S(2)}) collective-permute-start(f32[512,1]{1,0:T(8,128)S(1)} %get-tuple-element.27.degree), channel_id=1, source_target_pairs={{0,1},{1,0},{2,3},{3,2},{4,5},{5,4},{6,7},{7,6},{8,9},{9,8},{10,11... | collective-permute-start | bytes 6152 | tf_op jit(solution)/shard_map/ppermute | solution.py:52
  108.3 4.3 %copy-start.7 = (s32[128,4]{0,1:T(4,128)S(1)}, s32[128,4]{0,1:T(4,128)}, u32[]{:S(2)}) copy-start(s32[128,4]{0,1:T(4,128)} %param.19) | copy-start | bytes 6148
  108.3 4.3 %copy-start.10 = (s32[16]{0:T(128)S(1)}, s32[16]{0:T(128)}, u32[]{:S(2)}) copy-start(s32[16]{0:T(128)} %param.21) | copy-start | bytes 196
  108.3 5.8 %collective-permute-start.4 = (bf16[64,8,512]{2,1,0:T(8,128)(2,1)S(1)}, bf16[64,8,512]{2,1,0:T(8,128)(2,1)S(1)}, u32[]{:S(2)}, u32[]{:S(2)}) collective-permute-start(bf16[64,8,512]{2,1,0:T(8,128)(2,1)S(1)} %all_to_all.16.mine), channel_id=1, source_target_pairs={{0,1},{1,0},{2,3},{3,2},{4,5},{5,4},{6,7},{7,6},{8,9},{9,8},{10,11... | collective-permute-start | bytes 1572872 | tf_op jit(solution)/shard_map/ppermute | solution.py:52
where the time goes:
time: 116 us
  blocking collectives  50.4 us (43%)
  waiting for transfers between devices  21.9 us (19%)
  Pallas kernels  19.6 us (17%)
  starting transfers between devices  18.5 us (16%)
  local copies, waits for them, and re-layouts  3.64 us (3%)
  between operations  1.45 us (1%)
    all_to_all x2, blocking collectives, over_chips(): return lax.all_to_all(x, CHIPS, 0, 0, tiled=True)  50.4 us
    all_to_all x1, waiting for transfers between devices, over_chips(): return lax.all_to_all(x, CHIPS, 0, 0, tiled=True)  21.3 us
    pallas_call x10, Pallas kernels, call(): pl.pallas_call(body, out_shape=tuple(outs), in_specs=list(specs), out_spe...  19.6 us
    all_to_all x1, starting transfers between devices, over_chips(): return lax.all_to_all(x, CHIPS, 0, 0, tiled=True)  12.1 us
    ppermute x5, starting transfers between devices, pair(): return lax.ppermute(x, CORE, [(0, 1), (1, 0)])  6.4 us
    unnamed x30, local copies, waits for them, and re-layouts  3.64 us
  transfers between devices with their start and end apart: 6, of which 2 were waited for; matrix products, arithmetic and copies ran while one was open for 0% of the time, Pallas kernels for 13%

commit v1 on v0

--- a/solution.py
+++ b/solution.py
@@ -19,18 +19,24 @@
 
 VM = pl.BlockSpec(memory_space=pltpu.VMEM)
 SM = pl.BlockSpec(memory_space=pltpu.SMEM)
+HB = pl.BlockSpec(memory_space=pltpu.MemorySpace.HBM)
+DMA = pltpu.SemaphoreType.DMA
 LIMIT = 8 << 20
 
 
-def call(body, outs, specs, flops, *args, scratch=()):
+def call(body, outs, specs, flops, *args, scratch=(), to=None, alias=None):
     size = sum(a.size * a.dtype.itemsize for a in args)
     size += sum(o.size * o.dtype.itemsize for o in outs)
+    spaces = to or [VM] * len(outs)
     return pl.pallas_call(
         body,
-        out_shape=tuple(outs),
+        out_shape=tuple(
+            pltpu.MemorySpace.HBM(o.shape, o.dtype) if p is HB else o for o, p in zip(outs, spaces)
+        ),
         in_specs=list(specs),
-        out_specs=tuple([VM] * len(outs)),
+        out_specs=tuple(spaces),
         scratch_shapes=list(scratch),
+        input_output_aliases=alias or {},
         compiler_params=pltpu.CompilerParams(vmem_limit_bytes=LIMIT),
         cost_estimate=pl.CostEstimate(flops=flops, bytes_accessed=size, transcendentals=0),
     )(*args)
@@ -76,21 +82,37 @@
     return jnp.sum(jnp.where(keep, wide, 0.0), axis=0, keepdims=True)
 
 
-def send(routes, hub_ids, feats, out):
-    feat = feats.shape[1]
+def send(routes_at, hub_ids_at, feats_at, out, routes, hub_ids, feats, hubs_out, cuts_out, sem):
+    reads = [
+        pltpu.make_async_copy(routes_at, routes, sem.at[0]),
+        pltpu.make_async_copy(hub_ids_at, hub_ids, sem.at[1]),
+        pltpu.make_async_copy(feats_at.at[pl.ds(0, REACH)], feats, sem.at[2]),
+    ]
+    for read in reads:
+        read.start()
+    for read in reads:
+        read.wait()
     deep, peers = routes.shape
     slots = deep * peers
     width = hub_ids.shape[1]
     same = iota((width, width), 0) == iota((width, width), 1)
     hub = jnp.sum(jnp.where(same, hub_ids[...].astype(F32), 0.0), axis=1, keepdims=True)
-    slab = mm(ones_where(hub.astype(jnp.int32) == iota((width, REACH), 1)), feats[:REACH, :])
-    out[:, :width, :] = jnp.broadcast_to(slab.astype(BF)[None], (out.shape[0], width, feat))
+    slab = mm(ones_where(hub.astype(jnp.int32) == iota((width, REACH), 1)), feats[...])
+    hubs_out[...] = jnp.broadcast_to(slab.astype(BF)[None], hubs_out.shape)
+    first = pltpu.make_async_copy(hubs_out, out.at[:, pl.ds(0, width), :], sem.at[3])
+    first.start()
     fan = ones_where(iota((slots, peers), 1) == iota((slots, peers), 0) // deep)
     wide = mm_nt(fan, small(routes[...]))
     keep = iota((slots, deep), 1) == iota((slots, deep), 0) % deep
     row = jnp.sum(jnp.where(keep, wide, 0.0), axis=1, keepdims=True).astype(jnp.int32)
-    rows = mm(ones_where(row == iota((slots, REACH), 1)), feats[:REACH, :])
-    out[:, width:, :] = rows.astype(BF).reshape(out.shape[0], slots // out.shape[0], feat)
+    rows = mm(ones_where(row == iota((slots, REACH), 1)), feats[...])
+    cuts_out[...] = rows.astype(BF).reshape(cuts_out.shape)
+    second = pltpu.make_async_copy(
+        cuts_out, out.at[:, pl.ds(width, cuts_out.shape[1]), :], sem.at[4]
+    )
+    second.start()
+    first.wait()
+    second.wait()
 
 
 def ahead(
@@ -108,6 +130,7 @@
     self_term,
     degree,
     dense,
+    dense_far,
     flip_own,
     cut_own,
     wide_own,
@@ -119,7 +142,7 @@
 ):
     rows, feat = feats.shape
     slots = cweight.shape[1]
-    hubs = dense.shape[1]
+    hubs = 2 * dense.shape[1]
     blocks = rows // TILE
     live = count[0]
     me = core[0]
@@ -173,15 +196,17 @@
         for k in range(edges.shape[0]):
             acc = acc + jnp.where(place[k : k + 1, :] == hub, weight[k : k + 1, :], 0.0)
         flat = acc.astype(BF)
-        dense[:, pl.ds(base, step)] = jnp.transpose(flat)
 
         @pl.when(base < hubs // 2)
         def _():
             flip_own[pl.ds(base, step), :] = flat
+            dense[:, pl.ds(base, step)] = jnp.transpose(flat)
 
         @pl.when(base >= hubs // 2)
         def _():
-            ship[pl.ds(pl.multiple_of(base - hubs // 2, step), step), :] = flat
+            spot = pl.multiple_of(base - hubs // 2, step)
+            ship[pl.ds(spot, step), :] = flat
+            dense_far[:, pl.ds(spot, step)] = jnp.transpose(flat)
 
         return carry
 
@@ -194,20 +219,20 @@
     return table, bundle[:, width:, :].reshape(peers * (deep - width), feat)
 
 
-def near_sum(local_sum, wide_own, dense, bundle, out):
+def near_sum(wide_own, dense, bundle, out):
     _, feat = out.shape
-    hubs = dense.shape[1] // 2
-    table, cut = sides(bundle, hubs // bundle.shape[0], feat)
-    out[...] = local_sum[...] + mm(wide_own[...], cut) + mm(dense[:, :hubs], table)
-
-
-def forward(core, count, near, wide_far, dense, bundle, degree, self_term, wneigh, cot, act, mean_own, pack):
+    table, cut = sides(bundle, dense.shape[1] // bundle.shape[0], feat)
+    out[...] = mm(wide_own[...], cut) + mm(dense[...], table)
+
+
+def forward(
+    core, count, near, local_sum, wide_far, dense, bundle, degree, self_term, wneigh, cot, act, mean_own, pack
+):
     rows, feat = near.shape
-    hubs = dense.shape[1] // 2
     half = feat // 2
     me = core[0]
-    table, cut = sides(bundle, hubs // bundle.shape[0], feat)
-    total = near[...] + mm(wide_far[...], cut) + mm(dense[:, hubs:], table)
+    table, cut = sides(bundle, dense.shape[1] // bundle.shape[0], feat)
+    total = local_sum[...] + near[...] + mm(wide_far[...], cut) + mm(dense[...], table)
     mean = (total / degree[...]).astype(BF)
     mean_own[...] = jnp.transpose(jnp.where(me == 0, mean[:, :half], mean[:, half:]))
     pack[:half, :] = jnp.transpose(jnp.where(me == 0, mean[:, half:], mean[:, :half]))
@@ -219,34 +244,48 @@
     pack[half:, :] = jnp.where(live, grad, 0.0).astype(BF)
 
 
-def back_near(pack, mean_own, feat_own, wneigh, degree, flip_own, cut_own, gmean, hub, cut, weight):
+def back_near(pack, wneigh, degree, flip_own, cut_own, gmean, hub, cut, near, sem):
+    half = wneigh.shape[0] // 2
+    near[...] = (mm_nt(pack[half:, :], wneigh[...]) / degree[...]).astype(BF)
+    away = pltpu.make_async_copy(near, gmean, sem)
+    away.start()
+    hub[...] = mm(flip_own[...], near[...])
+    cut[...] = mm(cut_own[...], near[...])
+    away.wait()
+
+
+def weight_near(pack, mean_own, feat_own, out):
     half = feat_own.shape[0]
     grad = pack[half:, :]
-    near = (mm_nt(grad, wneigh[...]) / degree[...]).astype(BF)
-    gmean[...] = near
-    hub[...] = mm(flip_own[...], near)
-    cut[...] = mm(cut_own[...], near)
-    weight[:half, :] = mm(feat_own[...], grad)
-    weight[half:, :] = mm(mean_own[...], grad)
-
-
-def back_far(pack, wneigh, degree, ship, hub, cut, weight, out):
+    out[:half, :] = mm(feat_own[...], grad)
+    out[half:, :] = mm(mean_own[...], grad)
+
+
+def back_far(pack, wneigh, degree, ship, hub, cut, weight, out, hubs_out, cuts_out, weights_out, sem):
     feat = wneigh.shape[0]
     half = feat // 2
+    hubs, slots = hub.shape[0], cut.shape[0]
+    width, deep, share = hubs_out.shape[1], cuts_out.shape[1], weights_out.shape[1]
+    peers = out.shape[0]
     grad = pack[half:, :]
-    hubs, slots = hub.shape[0], cut.shape[0]
-    peers = out.shape[0]
-    a, b = hubs // peers, (hubs + slots) // peers
     far = (mm_nt(grad, wneigh[...]) / degree[...]).astype(BF)
     first = hub[...] + mm(ship[:hubs, :], far)
-    out[:, :a, :] = first.astype(BF).reshape(peers, a, feat)
+    hubs_out[...] = first.astype(BF).reshape(hubs_out.shape)
+    one = pltpu.make_async_copy(hubs_out, out.at[:, pl.ds(0, width), :], sem.at[0])
+    one.start()
     second = cut[...] + mm(ship[hubs : hubs + slots, :], far)
-    out[:, a:b, :] = second.astype(BF).reshape(peers, b - a, feat)
-    share = feat // peers
+    cuts_out[...] = second.astype(BF).reshape(cuts_out.shape)
+    two = pltpu.make_async_copy(cuts_out, out.at[:, pl.ds(width, deep), :], sem.at[1])
+    two.start()
     low = weight[:half, :] + mm(ship[hubs + slots :, :], grad)
+    weights_out[: peers // 2] = low.astype(BF).reshape(peers // 2, share, feat)
     high = weight[half:, :] + mm(pack[:half, :], grad)
-    out[: peers // 2, b:, :] = low.astype(BF).reshape(peers // 2, share, feat)
-    out[peers // 2 :, b:, :] = high.astype(BF).reshape(peers // 2, share, feat)
+    weights_out[peers // 2 :] = high.astype(BF).reshape(peers // 2, share, feat)
+    three = pltpu.make_async_copy(weights_out, out.at[:, pl.ds(width + deep, share), :], sem.at[2])
+    three.start()
+    one.wait()
+    two.wait()
+    three.wait()
 
 
 def row_terms(cols, pack, wself, lweight, gmean, out):
@@ -260,11 +299,14 @@
             out[pl.ds(base, TILE), :] += part[t * TILE : (t + 1) * TILE, :]
 
 
-def spread(bundle, out):
-    share = out.shape[1]
-    first = bundle.shape[1] - share
-    total = jnp.sum(bundle[:, first:, :].astype(F32), axis=0)
-    out[...] = jnp.broadcast_to(total.astype(BF)[None], out.shape)
+def spread(parts, out, held, sem):
+    share = held.shape[1]
+    first = parts.shape[1] - share
+    total = jnp.sum(parts[:, first:, :].astype(F32), axis=0)
+    held[...] = jnp.broadcast_to(total.astype(BF)[None], held.shape)
+    away = pltpu.make_async_copy(held, out, sem)
+    away.start()
+    away.wait()
 
 
 def finish(count, rows_in, routes, hub_ids, bundle, out):
@@ -286,15 +328,26 @@
     out[REACH:, :] = jnp.where(live[REACH:], rows_in[REACH:, :], 0.0).astype(BF)
 
 
-def assemble(core, mine, other, first, second):
-    peers, share, feat = mine.shape
-    half = peers * share // 2
-    me = core[0]
-    for source, turn in ((mine, me), (other, 1 - me)):
-        whole = source[...].reshape(peers * share, feat).astype(F32)
-        at = pl.ds(pl.multiple_of(turn * half, half), half)
-        first[at, :] = whole[:half, :]
-        second[at, :] = whole[half:, :]
+def place_rows(turn, source, first, second, held, sem):
+    half, feat = held.shape[1:]
+    whole = source[...].reshape(2 * half, feat).astype(F32)
+    at = pl.ds(pl.multiple_of(turn * half, half), half)
+    held[0] = whole[:half, :]
+    one = pltpu.make_async_copy(held.at[0], first.at[at], sem.at[0])
+    one.start()
+    held[1] = whole[half:, :]
+    two = pltpu.make_async_copy(held.at[1], second.at[at], sem.at[1])
+    two.start()
+    one.wait()
+    two.wait()
+
+
+def place_own(core, source, first, second, held, sem):
+    place_rows(core[0], source, first, second, held, sem)
+
+
+def place_far(core, source, first_in, second_in, first, second, held, sem):
+    place_rows(1 - core[0], source, first, second, held, sem)
 
 
 def per_device(
@@ -329,7 +382,20 @@
     routes = send_rows.T
     hub_ids = hub_rows.reshape(1, width)
     (bundle,) = call(
-        send, [like((chips, width + 2 * deep, feat))], [VM] * 3, unit, routes, hub_ids, features
+        send,
+        [like((chips, width + 2 * deep, feat))],
+        [HB] * 3,
+        unit,
+        *[pltpu.with_memory_space_constraint(x, pltpu.MemorySpace.HBM) for x in (routes, hub_ids, features)],
+        to=[HB],
+        scratch=[
+            pltpu.VMEM(routes.shape, routes.dtype),
+            pltpu.VMEM(hub_ids.shape, hub_ids.dtype),
+            pltpu.VMEM((REACH, feat), BF),
+            pltpu.VMEM((chips, width, feat), BF),
+            pltpu.VMEM((chips, 2 * deep, feat), BF),
+            DMA((5,)),
+        ],
     )
     bundle = over_chips(bundle)
     (
@@ -337,6 +403,7 @@
         self_term,
         degree,
         dense,
+        dense_far,
         flip_own,
         cut_own,
         wide_own,
@@ -349,7 +416,8 @@
             like((rows, feat), F32),
             like((rows, feat), F32),
             like((rows, 1), F32),
-            like((rows, hubs)),
+            like((rows, hubs // 2)),
+            like((rows, hubs // 2)),
             like((hubs // 2, rows)),
             like((slots, rows)),
             like((rows, slots)),
@@ -375,17 +443,18 @@
     ship_far = pair(ship)
 
     bundle_far = pair(bundle)
-    (near,) = call(near_sum, [like((rows, feat), F32)], [VM] * 4, 3 * unit, local_sum, wide_own, dense, bundle)
+    (near,) = call(near_sum, [like((rows, feat), F32)], [VM] * 3, 3 * unit, wide_own, dense, bundle)
     activated, mean_own, pack = call(
         forward,
         [like((rows, feat)), like((half, rows)), like((half + rows, feat))],
-        [SM, SM] + [VM] * 8,
+        [SM, SM] + [VM] * 9,
         4 * unit,
         core,
         row_counts,
         near,
+        local_sum,
         wide_far,
-        dense,
+        dense_far,
         bundle_far,
         degree,
         self_term,
@@ -393,19 +462,20 @@
         cotangent,
     )
     pack_far = pair(pack)
-    gmean, hub_part, cut_part, weight_part = call(
+    gmean, hub_part, cut_part = call(
         back_near,
-        [like((rows, feat)), like((hubs // 2, feat), F32), like((slots, feat), F32), like((feat, feat), F32)],
-        [VM] * 7,
-        5 * unit,
+        [like((rows, feat)), like((hubs // 2, feat), F32), like((slots, feat), F32)],
+        [VM] * 5,
+        4 * unit,
         pack,
-        mean_own,
-        feat_own,
         weight_neigh,
         degree,
         flip_own,
         cut_own,
-    )
+        to=[HB, VM, VM],
+        scratch=[pltpu.VMEM((rows, feat), BF), DMA],
+    )
+    (weight_part,) = call(weight_near, [like((feat, feat), F32)], [VM] * 3, unit, pack, mean_own, feat_own)
     (back,) = call(
         back_far,
         [like((chips, width + 2 * deep + share, feat))],
@@ -418,12 +488,27 @@
         hub_part,
         cut_part,
         weight_part,
+        to=[HB],
+        scratch=[
+            pltpu.VMEM((chips, width, feat), BF),
+            pltpu.VMEM((chips, 2 * deep, feat), BF),
+            pltpu.VMEM((chips, share, feat), BF),
+            DMA((3,)),
+        ],
     )
     back = over_chips(back)
     (row_sum,) = call(
         row_terms, [like((rows, feat), F32)], [SM] + [VM] * 4, 3 * unit, tile_cols, pack, weight_self, local_weight, gmean
     )
-    (weight_sum,) = call(spread, [like((chips, share, feat))], [VM], 1 << 20, back)
+    (weight_sum,) = call(
+        spread,
+        [like((chips, share, feat))],
+        [VM],
+        1 << 20,
+        back,
+        to=[HB],
+        scratch=[pltpu.VMEM((chips, share, feat), BF), DMA],
+    )
     weight_all = over_chips(weight_sum)
     weight_pair = pair(weight_all)
     (feature_grad,) = call(
@@ -437,8 +522,20 @@
         hub_ids,
         back,
     )
+    grads = [like((feat, feat), F32)] * 2
+    held = [pltpu.VMEM((2, half, feat), F32), DMA((2,))]
+    halfway = call(place_own, grads, [SM, VM], 1 << 20, core, weight_all, to=[HB, HB], scratch=held)
     grad_self, grad_neigh = call(
-        assemble, [like((feat, feat), F32)] * 2, [SM, VM, VM], 1 << 20, core, weight_all, weight_pair
+        place_far,
+        grads,
+        [SM, VM, HB, HB],
+        1 << 20,
+        core,
+        weight_pair,
+        *halfway,
+        to=[HB, HB],
+        scratch=held,
+        alias={2: 0, 3: 1},
     )
     return activated, feature_grad, grad_self, grad_neigh
 

time: 116 us -> 119 us (1.026)
  Pallas kernels: 19.6 us -> 24.1 us
  local copies, waits for them, and re-layouts: 3.64 us -> 1.28 us
    pallas_call x10 -> x12, Pallas kernels: 19.6 us -> 24.1 us  [call(): pl.pallas_call(body, out_shape=tuple((pltpu.MemorySpace.HBM(o.shape, o.dt...]
    unnamed x30 -> x26, local copies, waits for them, and re-layouts: 3.64 us -> 1.28 us
  transfers between devices with their start and end apart: 6 -> 6, of which waited for: 2 -> 2; matrix products, arithmetic and copies ran while one was open for 0% -> 0% of each run, Pallas kernels for 13% -> 14%
where the time goes in v1:
time: 119 us
  blocking collectives  51.5 us (43%)
  Pallas kernels  24.1 us (20%)
  waiting for transfers between devices  21.8 us (18%)
  starting transfers between devices  18.5 us (16%)
  between operations  1.51 us (1%)
  local copies, waits for them, and re-layouts  1.28 us (1%)
    all_to_all x2, blocking collectives, over_chips(): return lax.all_to_all(x, CHIPS, 0, 0, tiled=True)  51.5 us
    pallas_call x12, Pallas kernels, call(): pl.pallas_call(body, out_shape=tuple((pltpu.MemorySpace.HBM(o.shape, o.dt...  24.1 us
    all_to_all x1, waiting for transfers between devices, over_chips(): return lax.all_to_all(x, CHIPS, 0, 0, tiled=True)  21.3 us
    all_to_all x1, starting transfers between devices, over_chips(): return lax.all_to_all(x, CHIPS, 0, 0, tiled=True)  12.1 us
    ppermute x5, starting transfers between devices, pair(): return lax.ppermute(x, CORE, [(0, 1), (1, 0)])  6.36 us
  transfers between devices with their start and end apart: 6, of which 2 were waited for; matrix products, arithmetic and copies ran while one was open for 0% of the time, Pallas kernels for 14%

profile of v1, /device:TPU:1, one launch (start us, length us, event | category | flops | bytes accessed | tf_op | source)
XLA Modules:
  0.0 118.6 jit_solution(15787475321565595314)
XLA Ops:
  0.6 2.6 %shard_map.157 = bf16[64,24,512]{2,1,0:T(8,128)(2,1)} custom-call(s32[4,128]{1,0:T(4,128)} %bitcast.6, s32[1,16]{1,0:T(1,128)} %bitcast.8, bf16[512,512]{1,0:T(8,128)(2,1)} %feats_at.1), custom_call_target="tpu_custom_call" | custom-call | flops 268435456 | bytes 2099264 | tf_op jit(solution)/shard_map/pallas_call | solution.py:31
  3.2 0.0 copy-start.2
  3.2 0.0 copy-start.3
  3.2 0.0 copy-start.4
  3.3 0.0 copy-start.7
  3.3 0.0 copy-start.10
  3.3 0.0 copy-start.11
  3.3 0.0 copy-start.12
  3.3 12.1 %all-to-all-start = ((bf16[64,24,512]{2,1,0:T(8,128)(2,1)}), bf16[64,24,512]{2,1,0:T(8,128)(2,1)S(1)}, u32[]{:S(2)}, u32[]{:S(2)}) async-start(bf16[64,24,512]{2,1,0:T(8,128)(2,1)} %shard_map.157), calls=%async_computation | async-start | bytes 3145728 | tf_op jit(solution)/shard_map/all_to_all | solution.py:62
  16.1 21.3 %all-to-all-done.bundle = bf16[64,24,512]{2,1,0:T(8,128)(2,1)S(1)} async-done(((bf16[64,24,512]{2,1,0:T(8,128)(2,1)}), bf16[64,24,512]{2,1,0:T(8,128)(2,1)S(1)}, u32[]{:S(2)}, u32[]{:S(2)}) %all-to-all-start) | async-done | bytes 1572896 | tf_op jit(solution)/shard_map/all_to_all | solution.py:62
  37.4 3.2 %collective-permute-start = (bf16[64,24,512]{2,1,0:T(8,128)(2,1)S(1)}, bf16[64,24,512]{2,1,0:T(8,128)(2,1)S(1)}, u32[]{:S(2)}, u32[]{:S(2)}) collective-permute-start(bf16[64,24,512]{2,1,0:T(8,128)(2,1)S(1)} %all-to-all-done.bundle), channel_id=1, source_target_pairs={{0,1},{1,0},{2,3},{3,2},{4,5},{5,4},{6,7},{7,6},{8,9},{9,8},{10,11... | collective-permute-start | bytes 4718600 | tf_op jit(solution)/shard_map/ppermute | solution.py:58
  40.5 0.0 copy-done.2
  40.5 0.0 copy-done.3
  40.5 0.0 copy-done.4
  40.5 0.0 copy-done.7
  40.5 0.0 copy-done.10
  40.6 0.0 copy-done.11
  40.6 0.0 copy-done.12
  40.6 0.0 copy-start.9
  40.6 1.0 copy-done.9
  41.6 7.8 %shard_map.156 = (f32[512,512]{1,0:T(8,128)S(1)}, f32[512,512]{1,0:T(8,128)S(1)}, f32[512,1]{1,0:T(8,128)S(1)}, bf16[512,1024]{1,0:T(8,128)(2,1)S(1)}, bf16[512,...) custom-call(s32[4,4]{1,0:T(4,128)S(1)} %copy-done.7, ...), custom_call_target="tpu_custom_call" | custom-call | flops 10737418240 | bytes 11037256 | tf_op jit(solution)/shard_map/pallas_call | solution.py:31
  49.4 0.1 collective-permute-start.3
  49.5 0.0 copy-start
  49.5 0.0 copy-start.1
  49.5 1.0 shard_map.158.near
  50.5 0.0 collective-permute-done.bundle
  50.5 0.0 copy-done
  50.6 0.2 copy-done.1
  50.7 2.4 %shard_map.159 = (bf16[512,512]{1,0:T(8,128)(2,1)}, bf16[256,512]{1,0:T(8,128)(2,1)S(1)}, bf16[768,512]{1,0:T(8,128)(2,1)S(1)}) custom-call(s32[1]{0:T(128)} %bitcast.core, s32[1]{0:T(128)S(6)} %copy.21.count, f32[512,512]{1,0:T(8,128)S(1)} %shard_map.158.near, f32[512,512]{1,0:T(8,128)S(1)} %get-tuple-element.27.local_sum, ...), custom_call_target="tpu_custom_call" | custom-call | flops 1073741824 | bytes 8914952 | tf_op jit(solution)/shard_map/pallas_call | solution.py:31
  53.1 0.5 collective-permute-start.1
  53.6 0.0 collective-permute-start.2
  53.6 1.4 %shard_map.160 = (bf16[512,512]{1,0:T(8,128)(2,1)}, f32[1024,512]{1,0:T(8,128)S(1)}, f32[512,512]{1,0:T(8,128)S(1)}) custom-call(bf16[768,512]{1,0:T(8,128)(2,1)S(1)} %get-tuple-element.33.pack, bf16[512,512]{1,0:T(8,128)(2,1)S(1)} %copy-done, f32[512,1]{1,0:T(8,128)S(1)} %get-tuple-element.30.degree, bf16[1024,512]{1,0:T(8,128)(2,1)S(1)} %get-tuple-element.34.flip_own, ...), custom_call_target="tpu_custom_call" | custom-call | flops 1073741824 | bytes 6555648 | tf_op jit(solution)/shard_map/pallas_call | solution.py:31
  55.0 0.4 shard_map.162.weight
  55.5 0.5 collective-permute-done.2.degree
  55.9 0.0 collective-permute-done.3.ship
  55.9 0.0 collective-permute-done.1.pack
  55.9 2.5 %shard_map.163 = bf16[64,32,512]{2,1,0:T(8,128)(2,1)} custom-call(bf16[768,512]{1,0:T(8,128)(2,1)S(1)} %collective-permute-done.1.pack, bf16[512,512]{1,0:T(8,128)(2,1)S(1)} %copy-done, f32[512,1]{1,0:T(8,128)S(1)} %collective-permute-done.2.degree, bf16[1792,512]{1,0:T(8,128)(2,1)S(1)} %collective-permute-done.3.ship, ...), custom_call_target="tpu_custom_call" | custom-call | flops 1342177280 | bytes 9439232 | tf_op jit(solution)/shard_map/pallas_call | solution.py:31
  58.4 32.6 %all_to_all.15.bundle.parts = bf16[64,32,512]{2,1,0:T(8,128)(2,1)S(1)} all-to-all(bf16[64,32,512]{2,1,0:T(8,128)(2,1)} %shard_map.163), channel_id=1, replica_groups=mesh['dom_0'=4,'dom_1'=4,'dom_2'=4,'dom_3'=2] {'dom_0','dom_1','dom_2'}, dimensions={0} | all-to-all | bytes 4194304 | tf_op jit(solution)/shard_map/all_to_all | solution.py:62
  91.1 0.0 copy-start.5
  91.1 0.9 shard_map.165
  92.0 18.8 %all_to_all.16.source = bf16[64,8,512]{2,1,0:T(8,128)(2,1)S(1)} all-to-all(bf16[64,8,512]{2,1,0:T(8,128)(2,1)} %shard_map.165), channel_id=1, replica_groups=mesh['dom_0'=4,'dom_1'=4,'dom_2'=4,'dom_3'=2] {'dom_0','dom_1','dom_2'}, dimensions={0} | all-to-all | bytes 1048576 | tf_op jit(solution)/shard_map/all_to_all | solution.py:62
  110.8 0.0 copy-start.6
  110.8 0.0 copy-start.8
  110.8 2.6 %collective-permute-start.4 = (bf16[64,8,512]{2,1,0:T(8,128)(2,1)S(1)}, bf16[64,8,512]{2,1,0:T(8,128)(2,1)S(1)}, u32[]{:S(2)}, u32[]{:S(2)}) collective-permute-start(bf16[64,8,512]{2,1,0:T(8,128)(2,1)S(1)} %all_to_all.16.source), channel_id=1, source_target_pairs={{0,1},{1,0},{2,3},{3,2},{4,5},{5,4},{6,7},{7,6},{8,9},{9,8},{10,11... | collective-permute-start | bytes 1572872 | tf_op jit(solution)/shard_map/ppermute | solution.py:58
  113.4 0.0 copy-done.5
  113.4 1.6 %shard_map.161.rows_in = f32[512,512]{1,0:T(8,128)S(1)} custom-call(s32[4,4]{1,0:T(4,128)S(1)} %copy-done.7, bf16[768,512]{1,0:T(8,128)(2,1)S(1)} %get-tuple-element.33.pack, bf16[512,512]{1,0:T(8,128)(2,1)S(1)} %copy-done.4, bf16[512,512]{1,0:T(8,128)(2,1)S(1)} %copy-done.3, bf16[512,512]{1,0:T(8,128)(2,1)S(1)} %copy-done.5), custom_call_target="tpu_custom_call" | custom-call | flops 805306368 | bytes 3407936 | tf_op jit(solution)/shard_map/pallas_call | solution.py:31
  115.0 0.0 copy-done.6
  115.0 0.0 copy-done.8
  115.0 1.5 %shard_map.164 = bf16[512,512]{1,0:T(8,128)(2,1)} custom-call(s32[1]{0:T(128)S(6)} %copy.21.count, f32[512,512]{1,0:T(8,128)S(1)} %shard_map.161.rows_in, s32[4,128]{1,0:T(4,128)S(1)} %bitcast.7, s32[1,16]{1,0:T(1,128)S(1)} %bitcast.9, bf16[64,32,512]{2,1,0:T(8,128)(2,1)S(1)} %all_to_all.15.bundle.parts), custom_call_target="tpu_custom_call" | custom-call | flops 536870912 | bytes 3672132 | tf_op jit(solution)/shard_map/pallas_call | solution.py:31
  116.6 1.0 shard_map.166
  117.6 0.0 collective-permute-done.4.source
  117.6 1.0 shard_map.167
Async XLA Ops:
  3.2 37.3 %copy-start.2 = (bf16[512,512]{1,0:T(8,128)(2,1)S(1)}, bf16[512,512]{1,0:T(8,128)(2,1)}, u32[]{:S(2)}) copy-start(bf16[512,512]{1,0:T(8,128)(2,1)} %feats_at.1) | copy-start | bytes 1572868
  3.2 37.3 %copy-start.3 = (bf16[512,512]{1,0:T(8,128)(2,1)S(1)}, bf16[512,512]{1,0:T(8,128)(2,1)}, u32[]{:S(2)}) copy-start(bf16[512,512]{1,0:T(8,128)(2,1)} %lweight.3) | copy-start | bytes 1572868
  3.2 37.3 %copy-start.4 = (bf16[512,512]{1,0:T(8,128)(2,1)S(1)}, bf16[512,512]{1,0:T(8,128)(2,1)}, u32[]{:S(2)}) copy-start(bf16[512,512]{1,0:T(8,128)(2,1)} %wself.3) | copy-start | bytes 1572868
  3.3 37.3 %copy-start.7 = (s32[4,4]{1,0:T(4,128)S(1)}, s32[4,4]{1,0:T(4,128)}, u32[]{:S(2)}) copy-start(s32[4,4]{1,0:T(4,128)} %cols.3) | copy-start | bytes 196
  3.3 37.3 %copy-start.10 = (s32[512,8]{0,1:T(8,128)S(1)}, s32[512,8]{0,1:T(8,128)}, u32[]{:S(2)}) copy-start(s32[512,8]{0,1:T(8,128)} %param.22) | copy-start | bytes 49156
  3.3 37.3 %copy-start.11 = (bf16[512,8]{0,1:T(8,128)(2,1)S(1)}, bf16[512,8]{0,1:T(8,128)(2,1)}, u32[]{:S(2)}) copy-start(bf16[512,8]{0,1:T(8,128)(2,1)} %param.23) | copy-start | bytes 24580
  3.3 37.3 %copy-start.12 = (s32[128,1]{0,1:T(1,128)S(1)}, s32[128,1]{0,1:T(1,128)}, u32[]{:S(2)}) copy-start(s32[128,1]{0,1:T(1,128)} %param.20) | copy-start | bytes 1540
  3.3 34.1 %all-to-all-start = ((bf16[64,24,512]{2,1,0:T(8,128)(2,1)}), bf16[64,24,512]{2,1,0:T(8,128)(2,1)S(1)}, u32[]{:S(2)}, u32[]{:S(2)}) async-start(bf16[64,24,512]{2,1,0:T(8,128)(2,1)} %shard_map.157), calls=%async_computation | async-start | bytes 3145728 | tf_op jit(solution)/shard_map/all_to_all | solution.py:62
  37.4 13.2 %collective-permute-start = (bf16[64,24,512]{2,1,0:T(8,128)(2,1)S(1)}, bf16[64,24,512]{2,1,0:T(8,128)(2,1)S(1)}, u32[]{:S(2)}, u32[]{:S(2)}) collective-permute-start(bf16[64,24,512]{2,1,0:T(8,128)(2,1)S(1)} %all-to-all-done.bundle), channel_id=1, source_target_pairs={{0,1},{1,0},{2,3},{3,2},{4,5},{5,4},{6,7},{7,6},{8,9},{9,8},{10,11... | collective-permute-start | bytes 4718600 | tf_op jit(solution)/shard_map/ppermute | solution.py:58
  40.6 1.0 copy-start.9
  49.4 6.5 %collective-permute-start.3 = (bf16[1792,512]{1,0:T(8,128)(2,1)S(1)}, bf16[1792,512]{1,0:T(8,128)(2,1)S(1)}, u32[]{:S(2)}, u32[]{:S(2)}) collective-permute-start(bf16[1792,512]{1,0:T(8,128)(2,1)S(1)} %get-tuple-element.37), channel_id=1, source_target_pairs={{0,1},{1,0},{2,3},{3,2},{4,5},{5,4},{6,7},{7,6},{8,9},{9,8},{10,11... | collective-permute-start | bytes 5505032 | tf_op jit(solution)/shard_map/ppermute | solution.py:58
  49.5 1.0 copy-start
  49.5 1.2 %copy-start.1 = (bf16[512,512]{1,0:T(8,128)(2,1)S(1)}, bf16[512,512]{1,0:T(8,128)(2,1)}, u32[]{:S(2)}) copy-start(bf16[512,512]{1,0:T(8,128)(2,1)} %cot.1) | copy-start | bytes 1572868
  53.1 2.8 %collective-permute-start.1 = (bf16[768,512]{1,0:T(8,128)(2,1)S(1)}, bf16[768,512]{1,0:T(8,128)(2,1)S(1)}, u32[]{:S(2)}, u32[]{:S(2)}) collective-permute-start(bf16[768,512]{1,0:T(8,128)(2,1)S(1)} %get-tuple-element.33.pack), channel_id=1, source_target_pairs={{0,1},{1,0},{2,3},{3,2},{4,5},{5,4},{6,7},{7,6},{8,9},{9,8},{10,11... | collective-permute-start | bytes 2359304 | tf_op jit(solution)/shard_map/ppermute | solution.py:58
  53.6 2.3 %collective-permute-start.2 = (f32[512,1]{1,0:T(8,128)S(1)}, f32[512,1]{1,0:T(8,128)S(1)}, u32[]{:S(2)}, u32[]{:S(2)}) collective-permute-start(f32[512,1]{1,0:T(8,128)S(1)} %get-tuple-element.30.degree), channel_id=1, source_target_pairs={{0,1},{1,0},{2,3},{3,2},{4,5},{5,4},{6,7},{7,6},{8,9},{9,8},{10,11... | collective-permute-start | bytes 6152 | tf_op jit(solution)/shard_map/ppermute | solution.py:58
  91.1 22.4 %copy-start.5 = (bf16[512,512]{1,0:T(8,128)(2,1)S(1)}, bf16[512,512]{1,0:T(8,128)(2,1)}, u32[]{:S(2)}) copy-start(bf16[512,512]{1,0:T(8,128)(2,1)} %get-tuple-element.36.gmean) | copy-start | bytes 1572868
  110.8 4.2 %copy-start.6 = (s32[128,4]{0,1:T(4,128)S(1)}, s32[128,4]{0,1:T(4,128)}, u32[]{:S(2)}) copy-start(s32[128,4]{0,1:T(4,128)} %param.19) | copy-start | bytes 6148
  110.8 4.2 %copy-start.8 = (s32[16]{0:T(128)S(1)}, s32[16]{0:T(128)}, u32[]{:S(2)}) copy-start(s32[16]{0:T(128)} %param.21) | copy-start | bytes 196
  110.8 6.8 %collective-permute-start.4 = (bf16[64,8,512]{2,1,0:T(8,128)(2,1)S(1)}, bf16[64,8,512]{2,1,0:T(8,128)(2,1)S(1)}, u32[]{:S(2)}, u32[]{:S(2)}) collective-permute-start(bf16[64,8,512]{2,1,0:T(8,128)(2,1)S(1)} %all_to_all.16.source), channel_id=1, source_target_pairs={{0,1},{1,0},{2,3},{3,2},{4,5},{5,4},{6,7},{7,6},{8,9},{9,8},{10,11... | collective-permute-start | bytes 1572872 | tf_op jit(solution)/shard_map/ppermute | solution.py:58

commit v2 on v1

--- a/solution.py
+++ b/solution.py
@@ -56,6 +56,14 @@
 
 def pair(x):
     return lax.ppermute(x, CORE, [(0, 1), (1, 0)])
+
+
+def round_ring(x, axis):
+    size = lax.axis_size(axis)
+    return [
+        lax.ppermute(x, axis, [(i, (i + shift) % size) for i in range(size)])
+        for shift in range(1, size)
+    ]
 
 
 def over_chips(x):
@@ -145,7 +153,7 @@
     hubs = 2 * dense.shape[1]
     blocks = rows // TILE
     live = count[0]
-    me = core[0]
+    me = core[0] % 2
     masked[...] = jnp.where(iota((rows, feat), 0) < live, feats[...], jnp.zeros_like(feats))
     self_term[...] = mm(masked[...], wself[...])
     deep = slots // counts.shape[1]
@@ -230,7 +238,7 @@
 ):
     rows, feat = near.shape
     half = feat // 2
-    me = core[0]
+    me = core[0] % 2
     table, cut = sides(bundle, dense.shape[1] // bundle.shape[0], feat)
     total = local_sum[...] + near[...] + mm(wide_far[...], cut) + mm(dense[...], table)
     mean = (total / degree[...]).astype(BF)
@@ -254,21 +262,25 @@
     away.wait()
 
 
-def weight_near(pack, mean_own, feat_own, out):
-    half = feat_own.shape[0]
-    grad = pack[half:, :]
-    out[:half, :] = mm(feat_own[...], grad)
-    out[half:, :] = mm(mean_own[...], grad)
-
-
-def back_far(pack, wneigh, degree, ship, hub, cut, weight, out, hubs_out, cuts_out, weights_out, sem):
+def weight_terms(pack, pack_far, mean_own, feat_own, ship, out, terms, sem):
+    half, _ = feat_own.shape
+    start = ship.shape[0] - half
+    peers, share, feat = out.shape
+    mine, other = pack[half:, :], pack_far[half:, :]
+    low = mm(feat_own[...], mine) + mm(ship[start:, :], other)
+    terms[: peers // 2] = low.astype(BF).reshape(peers // 2, share, feat)
+    high = mm(mean_own[...], mine) + mm(pack_far[:half, :], other)
+    terms[peers // 2 :] = high.astype(BF).reshape(peers // 2, share, feat)
+    away = pltpu.make_async_copy(terms, out, sem)
+    away.start()
+    away.wait()
+
+
+def back_far(pack, wneigh, degree, ship, hub, cut, out, hubs_out, cuts_out, sem):
     feat = wneigh.shape[0]
-    half = feat // 2
     hubs, slots = hub.shape[0], cut.shape[0]
-    width, deep, share = hubs_out.shape[1], cuts_out.shape[1], weights_out.shape[1]
-    peers = out.shape[0]
-    grad = pack[half:, :]
-    far = (mm_nt(grad, wneigh[...]) / degree[...]).astype(BF)
+    width, deep = hubs_out.shape[1], cuts_out.shape[1]
+    far = (mm_nt(pack[feat // 2 :, :], wneigh[...]) / degree[...]).astype(BF)
     first = hub[...] + mm(ship[:hubs, :], far)
     hubs_out[...] = first.astype(BF).reshape(hubs_out.shape)
     one = pltpu.make_async_copy(hubs_out, out.at[:, pl.ds(0, width), :], sem.at[0])
@@ -277,15 +289,8 @@
     cuts_out[...] = second.astype(BF).reshape(cuts_out.shape)
     two = pltpu.make_async_copy(cuts_out, out.at[:, pl.ds(width, deep), :], sem.at[1])
     two.start()
-    low = weight[:half, :] + mm(ship[hubs + slots :, :], grad)
-    weights_out[: peers // 2] = low.astype(BF).reshape(peers // 2, share, feat)
-    high = weight[half:, :] + mm(pack[:half, :], grad)
-    weights_out[peers // 2 :] = high.astype(BF).reshape(peers // 2, share, feat)
-    three = pltpu.make_async_copy(weights_out, out.at[:, pl.ds(width + deep, share), :], sem.at[2])
-    three.start()
     one.wait()
     two.wait()
-    three.wait()
 
 
 def row_terms(cols, pack, wself, lweight, gmean, out):
@@ -299,14 +304,14 @@
             out[pl.ds(base, TILE), :] += part[t * TILE : (t + 1) * TILE, :]
 
 
-def spread(parts, out, held, sem):
-    share = held.shape[1]
-    first = parts.shape[1] - share
-    total = jnp.sum(parts[:, first:, :].astype(F32), axis=0)
-    held[...] = jnp.broadcast_to(total.astype(BF)[None], held.shape)
-    away = pltpu.make_async_copy(held, out, sem)
-    away.start()
-    away.wait()
+def own_sum(parts, out):
+    out[...] = jnp.sum(parts[...].astype(F32), axis=0).astype(BF)
+
+
+def join_four(a, b, c, d, out):
+    rows = a.shape[0]
+    for i, part in enumerate((a, b, c, d)):
+        out[i * rows : (i + 1) * rows, :] = part[...]
 
 
 def finish(count, rows_in, routes, hub_ids, bundle, out):
@@ -328,26 +333,34 @@
     out[REACH:, :] = jnp.where(live[REACH:], rows_in[REACH:, :], 0.0).astype(BF)
 
 
-def place_rows(turn, source, first, second, held, sem):
-    half, feat = held.shape[1:]
-    whole = source[...].reshape(2 * half, feat).astype(F32)
-    at = pl.ds(pl.multiple_of(turn * half, half), half)
-    held[0] = whole[:half, :]
-    one = pltpu.make_async_copy(held.at[0], first.at[at], sem.at[0])
+def place_rows(spot, turn, parts, first, second, held, sem):
+    rows, _ = held.shape
+    half = rows // 2
+    size = len(parts)
+    share = parts[0].shape[0] // (size * size)
+    x, z, y = spot // 32, (spot // 8) % 4, (spot // 2) % 4
+    for i, part in enumerate(parts):
+        wide = part[...].astype(F32)
+        for k in range(size):
+            for j in range(size):
+                chip = ((x - i + size) % size * size + (z - k + size) % size) * size + (y - j + size) % size
+                at = (k * size + j) * share
+                held[pl.ds(pl.multiple_of(chip * share, share), share), :] = wide[at : at + share, :]
+    to = pl.ds(pl.multiple_of(turn * half, half), half)
+    one = pltpu.make_async_copy(held.at[pl.ds(0, half)], first.at[to], sem.at[0])
+    two = pltpu.make_async_copy(held.at[pl.ds(half, half)], second.at[to], sem.at[1])
     one.start()
-    held[1] = whole[half:, :]
-    two = pltpu.make_async_copy(held.at[1], second.at[at], sem.at[1])
     two.start()
     one.wait()
     two.wait()
 
 
-def place_own(core, source, first, second, held, sem):
-    place_rows(core[0], source, first, second, held, sem)
-
-
-def place_far(core, source, first_in, second_in, first, second, held, sem):
-    place_rows(1 - core[0], source, first, second, held, sem)
+def place_own(spot, a, b, c, d, first, second, held, sem):
+    place_rows(spot[0], spot[0] % 2, (a, b, c, d), first, second, held, sem)
+
+
+def place_far(spot, a, b, c, d, first_in, second_in, first, second, held, sem):
+    place_rows(spot[0], 1 - spot[0] % 2, (a, b, c, d), first, second, held, sem)
 
 
 def per_device(
@@ -366,7 +379,7 @@
     cotangent,
 ):
     rows, feat = features.shape
-    core = lax.axis_index(CORE).astype(jnp.int32).reshape(1)
+    core = lax.axis_index(DOM).astype(jnp.int32).reshape(1)
     chips = lax.axis_size(CHIPS)
     deep = send_rows.shape[1]
     width = hub_rows.shape[0]
@@ -475,42 +488,49 @@
         to=[HB, VM, VM],
         scratch=[pltpu.VMEM((rows, feat), BF), DMA],
     )
-    (weight_part,) = call(weight_near, [like((feat, feat), F32)], [VM] * 3, unit, pack, mean_own, feat_own)
+    (terms,) = call(
+        weight_terms,
+        [like((chips, share, feat))],
+        [VM] * 5,
+        2 * unit,
+        pack,
+        pack_far,
+        mean_own,
+        feat_own,
+        ship_far,
+        to=[HB],
+        scratch=[pltpu.VMEM((chips, share, feat), BF), DMA],
+    )
+    terms = over_chips(terms)
     (back,) = call(
         back_far,
-        [like((chips, width + 2 * deep + share, feat))],
-        [VM] * 7,
-        5 * unit,
+        [like((chips, width + 2 * deep, feat))],
+        [VM] * 6,
+        4 * unit,
         pack_far,
         weight_neigh,
         degree_far,
         ship_far,
         hub_part,
         cut_part,
-        weight_part,
         to=[HB],
         scratch=[
             pltpu.VMEM((chips, width, feat), BF),
             pltpu.VMEM((chips, 2 * deep, feat), BF),
-            pltpu.VMEM((chips, share, feat), BF),
-            DMA((3,)),
+            DMA((2,)),
         ],
     )
     back = over_chips(back)
     (row_sum,) = call(
         row_terms, [like((rows, feat), F32)], [SM] + [VM] * 4, 3 * unit, tile_cols, pack, weight_self, local_weight, gmean
     )
-    (weight_sum,) = call(
-        spread,
-        [like((chips, share, feat))],
-        [VM],
-        1 << 20,
-        back,
-        to=[HB],
-        scratch=[pltpu.VMEM((chips, share, feat), BF), DMA],
-    )
-    weight_all = over_chips(weight_sum)
-    weight_pair = pair(weight_all)
+    (stage,) = call(own_sum, [like((share, feat))], [VM], 1 << 20, terms)
+    for axis in CHIPS[:0:-1]:
+        parts = [stage] + round_ring(stage, axis)
+        (stage,) = call(
+            join_four, [like((4 * stage.shape[0], feat))], [VM] * 4, 1 << 20, *parts
+        )
+    parts = [stage] + round_ring(stage, CHIPS[0])
     (feature_grad,) = call(
         finish,
         [like((rows, feat))],
@@ -523,19 +543,19 @@
         back,
     )
     grads = [like((feat, feat), F32)] * 2
-    held = [pltpu.VMEM((2, half, feat), F32), DMA((2,))]
-    halfway = call(place_own, grads, [SM, VM], 1 << 20, core, weight_all, to=[HB, HB], scratch=held)
+    held = [pltpu.VMEM((feat, feat), F32), DMA((2,))]
+    halfway = call(place_own, grads, [SM] + [VM] * 4, 1 << 20, core, *parts, to=[HB, HB], scratch=held)
     grad_self, grad_neigh = call(
         place_far,
         grads,
-        [SM, VM, HB, HB],
+        [SM] + [VM] * 4 + [HB, HB],
         1 << 20,
         core,
-        weight_pair,
+        *[pair(p) for p in parts],
         *halfway,
         to=[HB, HB],
         scratch=held,
-        alias={2: 0, 3: 1},
+        alias={5: 0, 6: 1},
     )
     return activated, feature_grad, grad_self, grad_neigh
 

time: 119 us -> 129 us (1.084)
  blocking collectives: 51.5 us -> 0 us
  starting transfers between devices: 18.5 us -> 51.1 us
  waiting for transfers between devices: 21.8 us -> 40.8 us
  local copies, waits for them, and re-layouts: 1.28 us -> 9.2 us
  Pallas kernels: 24.1 us -> 25.6 us
    all_to_all x2 -> x0, blocking collectives: 51.5 us -> none  [over_chips(): return lax.all_to_all(x, CHIPS, 0, 0, tiled=True)]
    ppermute x0 -> x9, starting transfers between devices: none -> 17.5 us  [round_ring(): lax.ppermute(x, axis, [(i, (i + shift) % size) for i in range(size)])]
    ppermute x0 -> x9, waiting for transfers between devices: none -> 13.2 us  [round_ring(): lax.ppermute(x, axis, [(i, (i + shift) % size) for i in range(size)])]
    all_to_all x1 -> x3, starting transfers between devices: 12.1 us -> 23.6 us  [over_chips(): return lax.all_to_all(x, CHIPS, 0, 0, tiled=True)]
    unnamed x26 -> x46, local copies, waits for them, and re-layouts: 1.28 us -> 9.2 us
    all_to_all x1 -> x3, waiting for transfers between devices: 21.3 us -> 25.3 us  [over_chips(): return lax.all_to_all(x, CHIPS, 0, 0, tiled=True)]
    ppermute x5 -> x8, starting transfers between devices: 6.36 us -> 10 us  [pair(): return lax.ppermute(x, CORE, [(0, 1), (1, 0)])]
    ppermute x5 -> x8, waiting for transfers between devices: 0.46 us -> 2.3 us  [pair(): return lax.ppermute(x, CORE, [(0, 1), (1, 0)])]
  transfers between devices with their start and end apart: 6 -> 20, of which waited for: 2 -> 7; matrix products, arithmetic and copies ran while one was open for 0% -> 0% of each run, Pallas kernels for 14% -> 16%
where the time goes in v2:
time: 129 us; the launch traced here: 128 us
  starting transfers between devices  51.1 us (40%)
  waiting for transfers between devices  40.8 us (32%)
  Pallas kernels  25.6 us (20%)
  local copies, waits for them, and re-layouts  9.2 us (7%)
  between operations  1.66 us (1%)
    pallas_call x14, Pallas kernels, call(): pl.pallas_call(body, out_shape=tuple((pltpu.MemorySpace.HBM(o.shape, o.dt...  25.6 us
    all_to_all x3, waiting for transfers between devices, over_chips(): return lax.all_to_all(x, CHIPS, 0, 0, tiled=True)  25.3 us
    all_to_all x3, starting transfers between devices, over_chips(): return lax.all_to_all(x, CHIPS, 0, 0, tiled=True)  23.6 us
    ppermute x9, starting transfers between devices, round_ring(): lax.ppermute(x, axis, [(i, (i + shift) % size) for i in range(size)])  17.5 us
    ppermute x9, waiting for transfers between devices, round_ring(): lax.ppermute(x, axis, [(i, (i + shift) % size) for i in range(size)])  13.2 us
    ppermute x8, starting transfers between devices, pair(): return lax.ppermute(x, CORE, [(0, 1), (1, 0)])  10 us
    unnamed x46, local copies, waits for them, and re-layouts  9.2 us
  transfers between devices with their start and end apart: 20, of which 7 were waited for; matrix products, arithmetic and copies ran while one was open for 0% of the time, Pallas kernels for 16%

profile of v2, /device:TPU:1, one launch (start us, length us, event | category | flops | bytes accessed | tf_op | source)
XLA Modules:
  0.0 128.4 jit_solution(14402311019704494019)
XLA Ops:
  0.6 2.6 %shard_map.157 = bf16[64,24,512]{2,1,0:T(8,128)(2,1)} custom-call(s32[4,128]{1,0:T(4,128)} %bitcast.6, s32[1,16]{1,0:T(1,128)} %bitcast.8, bf16[512,512]{1,0:T(8,128)(2,1)} %feats_at.1), custom_call_target="tpu_custom_call" | custom-call | flops 268435456 | bytes 2099264 | tf_op jit(solution)/shard_map/pallas_call | solution.py:31
  3.2 0.0 copy-start.4
  3.2 0.0 copy-start.5
  3.2 0.0 copy-start.7
  3.2 0.0 copy-start.13
  3.2 0.0 copy-start.16
  3.2 0.0 copy-start.17
  3.3 0.0 copy-start.18
  3.3 12.1 %all-to-all-start = ((bf16[64,24,512]{2,1,0:T(8,128)(2,1)}), bf16[64,24,512]{2,1,0:T(8,128)(2,1)S(1)}, u32[]{:S(2)}, u32[]{:S(2)}) async-start(bf16[64,24,512]{2,1,0:T(8,128)(2,1)} %shard_map.157), calls=%async_computation | async-start | bytes 3145728 | tf_op jit(solution)/shard_map/all_to_all | solution.py:70
  16.0 21.3 %all-to-all-done.bundle = bf16[64,24,512]{2,1,0:T(8,128)(2,1)S(1)} async-done(((bf16[64,24,512]{2,1,0:T(8,128)(2,1)}), bf16[64,24,512]{2,1,0:T(8,128)(2,1)S(1)}, u32[]{:S(2)}, u32[]{:S(2)}) %all-to-all-start) | async-done | bytes 1572896 | tf_op jit(solution)/shard_map/all_to_all | solution.py:70
  37.3 3.2 %collective-permute-start = (bf16[64,24,512]{2,1,0:T(8,128)(2,1)S(1)}, bf16[64,24,512]{2,1,0:T(8,128)(2,1)S(1)}, u32[]{:S(2)}, u32[]{:S(2)}) collective-permute-start(bf16[64,24,512]{2,1,0:T(8,128)(2,1)S(1)} %all-to-all-done.bundle), channel_id=1, source_target_pairs={{0,1},{1,0},{2,3},{3,2},{4,5},{5,4},{6,7},{7,6},{8,9},{9,8},{10,11... | collective-permute-start | bytes 4718600 | tf_op jit(solution)/shard_map/ppermute | solution.py:58
  40.5 0.0 copy-start.15
  40.5 1.0 copy-done.15
  41.6 7.8 %shard_map.156 = (f32[512,512]{1,0:T(8,128)S(1)}, f32[512,512]{1,0:T(8,128)S(1)}, f32[512,1]{1,0:T(8,128)S(1)}, bf16[512,1024]{1,0:T(8,128)(2,1)S(1)}, bf16[512,...) custom-call(s32[4,4]{1,0:T(4,128)S(1)} %copy-done.13, ...), custom_call_target="tpu_custom_call" | custom-call | flops 10737418240 | bytes 11037256 | tf_op jit(solution)/shard_map/pallas_call | solution.py:31
  49.4 0.0 copy-start.19
  49.4 0.0 copy-start.21
  49.4 0.1 collective-permute-start.3
  49.5 0.0 copy-start.3
  49.5 1.0 shard_map.158.near
  50.6 0.0 collective-permute-done.bundle
  50.6 0.1 copy-done.10
  50.6 0.4 copy-done
  51.0 0.3 copy-done.3
  51.3 2.4 %shard_map.159 = (bf16[512,512]{1,0:T(8,128)(2,1)}, bf16[256,512]{1,0:T(8,128)(2,1)S(1)}, bf16[768,512]{1,0:T(8,128)(2,1)S(1)}) custom-call(s32[1]{0:T(128)} %bitcast.core.spot, s32[1]{0:T(128)S(6)} %copy.21.count, f32[512,512]{1,0:T(8,128)S(1)} %shard_map.158.near, f32[512,512]{1,0:T(8,128)S(1)} %get-tuple-element.27.local_sum, ...), custom_call_target="tpu_custom_call" | custom-call | flops 1073741824 | bytes 8914952 | tf_op jit(solution)/shard_map/pallas_call | solution.py:31
  53.7 0.0 collective-permute-start.1
  53.7 0.0 collective-permute-done.3.ship
  53.7 2.3 %collective-permute-done.1.pack.pack_far = bf16[768,512]{1,0:T(8,128)(2,1)S(1)} collective-permute-done((bf16[768,512]{1,0:T(8,128)(2,1)S(1)}, bf16[768,512]{1,0:T(8,128)(2,1)S(1)}, u32[]{:S(2)}, u32[]{:S(2)}) %collective-permute-start.1) | collective-permute-done | bytes 786464 | tf_op jit(solution)/shard_map/ppermute | solution.py:58
  56.0 1.5 %shard_map.164 = bf16[64,8,512]{2,1,0:T(8,128)(2,1)} custom-call(bf16[768,512]{1,0:T(8,128)(2,1)S(1)} %get-tuple-element.33.pack, bf16[768,512]{1,0:T(8,128)(2,1)S(1)} %collective-permute-done.1.pack.pack_far, bf16[256,512]{1,0:T(8,128)(2,1)S(1)} %get-tuple-element.40.mean_own, bf16[256,512]{1,0:T(8,128)(2,1)S(1)} %get-tuple-element.41.feat_own, ...), custom_call_target="tpu_custom_call" | custom-call | flops 536870912 | bytes 4456448 | tf_op jit(solution)/shard_map/pallas_call | solution.py:31
  57.5 5.5 %all-to-all-start.2 = ((bf16[64,8,512]{2,1,0:T(8,128)(2,1)}), bf16[64,8,512]{2,1,0:T(8,128)(2,1)}, u32[]{:S(2)}, u32[]{:S(2)}) async-start(bf16[64,8,512]{2,1,0:T(8,128)(2,1)} %shard_map.164), calls=%async_computation.2 | async-start | bytes 1048576 | tf_op jit(solution)/shard_map/all_to_all | solution.py:70
  63.0 0.2 collective-permute-start.2
  63.2 1.0 copy-done.1
  64.3 0.9 copy-done.11
  65.2 1.2 copy-done.20
  66.4 1.0 copy-done.22
  67.5 1.4 %shard_map.160 = (bf16[512,512]{1,0:T(8,128)(2,1)}, f32[1024,512]{1,0:T(8,128)S(1)}, f32[512,512]{1,0:T(8,128)S(1)}) custom-call(bf16[768,512]{1,0:T(8,128)(2,1)S(1)} %get-tuple-element.33.pack, bf16[512,512]{1,0:T(8,128)(2,1)S(1)} %copy-done.1, f32[512,1]{1,0:T(8,128)S(1)} %copy-done.11, bf16[1024,512]{1,0:T(8,128)(2,1)S(1)} %copy-done.20, ...), custom_call_target="tpu_custom_call" | custom-call | flops 1073741824 | bytes 6555648 | tf_op jit(solution)/shard_map/pallas_call | solution.py:31
  68.9 2.3 %shard_map.162 = bf16[64,24,512]{2,1,0:T(8,128)(2,1)} custom-call(bf16[768,512]{1,0:T(8,128)(2,1)S(1)} %collective-permute-done.1.pack.pack_far, bf16[512,512]{1,0:T(8,128)(2,1)S(1)} %copy-done.2, f32[512,1]{1,0:T(8,128)S(1)} %collective-permute-done.2.degree, bf16[1792,512]{1,0:T(8,128)(2,1)S(1)} %collective-permute-done.3.ship, ...), custom_call_target="tpu_custom_call" | custom-call | flops 1073741824 | bytes 7866368 | tf_op jit(solution)/shard_map/pallas_call | solution.py:31
  71.2 4.0 %all-to-all-done.2.parts = bf16[64,8,512]{2,1,0:T(8,128)(2,1)} async-done(((bf16[64,8,512]{2,1,0:T(8,128)(2,1)}), bf16[64,8,512]{2,1,0:T(8,128)(2,1)}, u32[]{:S(2)}, u32[]{:S(2)}) %all-to-all-start.2) | async-done | bytes 524320 | tf_op jit(solution)/shard_map/all_to_all | solution.py:70
  75.2 6.0 %all-to-all-start.1 = ((bf16[64,24,512]{2,1,0:T(8,128)(2,1)}), bf16[64,24,512]{2,1,0:T(8,128)(2,1)S(1)}, u32[]{:S(2)}, u32[]{:S(2)}) async-start(bf16[64,24,512]{2,1,0:T(8,128)(2,1)} %shard_map.162), calls=%async_computation.1 | async-start | bytes 3145728 | tf_op jit(solution)/shard_map/all_to_all | solution.py:70
  81.2 1.1 shard_map.165.a
  82.4 1.1 collective-permute-start.4
  83.4 2.4 %collective-permute-start.5 = (bf16[8,512]{1,0:T(8,128)(2,1)S(1)}, bf16[8,512]{1,0:T(8,128)(2,1)S(1)}, u32[]{:S(2)}, u32[]{:S(2)}) collective-permute-start(bf16[8,512]{1,0:T(8,128)(2,1)S(1)} %shard_map.165.a), channel_id=1, source_target_pairs={{0,4},{2,6},{4,0},{6,2},{1,5},{3,7},{5,1},{7,3},{8,12},{10,14},{12... | collective-permute-start | bytes 24584 | tf_op jit(solution)/shard_map/ppermute | solution.py:64
  85.8 1.2 collective-permute-start.6
  87.0 5.6 %collective-permute-done.4.b = bf16[8,512]{1,0:T(8,128)(2,1)S(1)} collective-permute-done((bf16[8,512]{1,0:T(8,128)(2,1)S(1)}, bf16[8,512]{1,0:T(8,128)(2,1)S(1)}, u32[]{:S(2)}, u32[]{:S(2)}) %collective-permute-start.4) | collective-permute-done | bytes 8224 | tf_op jit(solution)/shard_map/ppermute | solution.py:64
  92.6 4.1 %collective-permute-done.5.c = bf16[8,512]{1,0:T(8,128)(2,1)S(1)} collective-permute-done((bf16[8,512]{1,0:T(8,128)(2,1)S(1)}, bf16[8,512]{1,0:T(8,128)(2,1)S(1)}, u32[]{:S(2)}, u32[]{:S(2)}) %collective-permute-start.5) | collective-permute-done | bytes 8224 | tf_op jit(solution)/shard_map/ppermute | solution.py:64
  96.7 0.0 collective-permute-start.7
  96.8 3.6 %collective-permute-start.8 = (bf16[32,512]{1,0:T(8,128)(2,1)S(1)}, bf16[32,512]{1,0:T(8,128)(2,1)S(1)}, u32[]{:S(2)}, u32[]{:S(2)}) collective-permute-start(bf16[32,512]{1,0:T(8,128)(2,1)S(1)} %shard_map.166.a), channel_id=1, source_target_pairs={{0,16},{8,24},{16,0},{24,8},{1,17},{9,25},{17,1},{25,9},{2,18},{10... | collective-permute-start | bytes 98312 | tf_op jit(solution)/shard_map/ppermute | solution.py:64
  100.4 2.3 %collective-permute-done.7.b = bf16[32,512]{1,0:T(8,128)(2,1)S(1)} collective-permute-done((bf16[32,512]{1,0:T(8,128)(2,1)S(1)}, bf16[32,512]{1,0:T(8,128)(2,1)S(1)}, u32[]{:S(2)}, u32[]{:S(2)}) %collective-permute-start.7) | collective-permute-done | bytes 32800 | tf_op jit(solution)/shard_map/ppermute | solution.py:64
  102.7 1.1 collective-permute-done.9.d
  103.9 4.0 %collective-permute-start.11 = (bf16[128,512]{1,0:T(8,128)(2,1)S(1)}, bf16[128,512]{1,0:T(8,128)(2,1)S(1)}, u32[]{:S(2)}, u32[]{:S(2)}) collective-permute-start(bf16[128,512]{1,0:T(8,128)(2,1)S(1)} %shard_map.167.a), channel_id=1, source_target_pairs={{0,32},{32,64},{64,96},{96,0},{1,33},{33,65},{65,97},{97,1},{2,34}... | collective-permute-start | bytes 393224 | tf_op jit(solution)/shard_map/ppermute | solution.py:64
  107.8 4.0 %collective-permute-start.13 = (bf16[128,512]{1,0:T(8,128)(2,1)S(1)}, bf16[128,512]{1,0:T(8,128)(2,1)S(1)}, u32[]{:S(2)}, u32[]{:S(2)}) collective-permute-start(bf16[128,512]{1,0:T(8,128)(2,1)S(1)} %shard_map.167.a), channel_id=1, source_target_pairs={{0,64},{32,96},{64,0},{96,32},{1,65},{33,97},{65,1},{97,33},{2,66}... | collective-permute-start | bytes 393224 | tf_op jit(solution)/shard_map/ppermute | solution.py:64
  111.8 1.3 %collective-permute-start.15 = (bf16[128,512]{1,0:T(8,128)(2,1)S(1)}, bf16[128,512]{1,0:T(8,128)(2,1)S(1)}, u32[]{:S(2)}, u32[]{:S(2)}) collective-permute-start(bf16[128,512]{1,0:T(8,128)(2,1)S(1)} %shard_map.167.a), channel_id=1, source_target_pairs={{0,96},{32,0},{64,32},{96,64},{1,97},{33,1},{65,33},{97,65},{2,98}... | collective-permute-start | bytes 393224 | tf_op jit(solution)/shard_map/ppermute | solution.py:64
  113.1 3.4 %collective-permute-start.10 = (bf16[128,512]{1,0:T(8,128)(2,1)S(1)}, bf16[128,512]{1,0:T(8,128)(2,1)S(1)}, u32[]{:S(2)}, u32[]{:S(2)}) collective-permute-start(bf16[128,512]{1,0:T(8,128)(2,1)S(1)} %shard_map.167.a), channel_id=1, source_target_pairs={{0,1},{1,0},{2,3},{3,2},{4,5},{5,4},{6,7},{7,6},{8,9},{9,8},{10,11... | collective-permute-start | bytes 393224 | tf_op jit(solution)/shard_map/ppermute | solution.py:58
  116.5 1.1 collective-permute-start.12
  117.6 1.5 %collective-permute-start.14 = (bf16[128,512]{1,0:T(8,128)(2,1)S(1)}, bf16[128,512]{1,0:T(8,128)(2,1)S(1)}, u32[]{:S(2)}, u32[]{:S(2)}) collective-permute-start(bf16[128,512]{1,0:T(8,128)(2,1)S(1)} %collective-permute-done.13.c), channel_id=1, source_target_pairs={{0,1},{1,0},{2,3},{3,2},{4,5},{5,4},{6,7},{7,6},{8,9},{9,8},{10,11... | collective-permute-start | bytes 393224 | tf_op jit(solution)/shard_map/ppermute | solution.py:58
  119.1 0.6 collective-permute-start.16
  119.7 1.0 copy-done.6
  120.7 1.0 copy-done.8
  121.8 1.0 copy-done.9
  122.8 1.6 %shard_map.161.rows_in = f32[512,512]{1,0:T(8,128)S(1)} custom-call(s32[4,4]{1,0:T(4,128)S(1)} %copy-done.13, bf16[768,512]{1,0:T(8,128)(2,1)S(1)} %get-tuple-element.33.pack, bf16[512,512]{1,0:T(8,128)(2,1)S(1)} %copy-done.8, bf16[512,512]{1,0:T(8,128)(2,1)S(1)} %copy-done.6, bf16[512,512]{1,0:T(8,128)(2,1)S(1)} %copy-done.9), custom_call_target="tpu_custom_call" | custom-call | flops 805306368 | bytes 3407936 | tf_op jit(solution)/shard_map/pallas_call | solution.py:31
  124.4 0.0 copy-start.12
  124.4 0.0 copy-start.14
  124.4 1.2 shard_map.168
  125.7 1.2 shard_map.169
  126.9 1.5 %shard_map.163 = bf16[512,512]{1,0:T(8,128)(2,1)} custom-call(s32[1]{0:T(128)S(6)} %copy.21.count, f32[512,512]{1,0:T(8,128)S(1)} %shard_map.161.rows_in, s32[4,128]{1,0:T(4,128)S(1)} %bitcast.7, s32[1,16]{1,0:T(1,128)S(1)} %bitcast.9, bf16[64,24,512]{2,1,0:T(8,128)(2,1)S(1)} %all-to-all-done.1.bundle), custom_call_target="tpu_custom_call" | custom-call | flops 536870912 | bytes 3147844 | tf_op jit(solution)/shard_map/pallas_call | solution.py:31
  (36 shorter events, 0.1 us)
Async XLA Ops:
  3.2 37.3 %copy-start.4 = (bf16[512,512]{1,0:T(8,128)(2,1)S(1)}, bf16[512,512]{1,0:T(8,128)(2,1)}, u32[]{:S(2)}) copy-start(bf16[512,512]{1,0:T(8,128)(2,1)} %feats_at.1) | copy-start | bytes 1572868
  3.2 37.3 %copy-start.5 = (bf16[512,512]{1,0:T(8,128)(2,1)S(1)}, bf16[512,512]{1,0:T(8,128)(2,1)}, u32[]{:S(2)}) copy-start(bf16[512,512]{1,0:T(8,128)(2,1)} %lweight.3) | copy-start | bytes 1572868
  3.2 37.3 %copy-start.7 = (bf16[512,512]{1,0:T(8,128)(2,1)S(1)}, bf16[512,512]{1,0:T(8,128)(2,1)}, u32[]{:S(2)}) copy-start(bf16[512,512]{1,0:T(8,128)(2,1)} %wself.3) | copy-start | bytes 1572868
  3.2 37.3 %copy-start.13 = (s32[4,4]{1,0:T(4,128)S(1)}, s32[4,4]{1,0:T(4,128)}, u32[]{:S(2)}) copy-start(s32[4,4]{1,0:T(4,128)} %cols.3) | copy-start | bytes 196
  3.2 37.3 %copy-start.16 = (s32[512,8]{0,1:T(8,128)S(1)}, s32[512,8]{0,1:T(8,128)}, u32[]{:S(2)}) copy-start(s32[512,8]{0,1:T(8,128)} %param.22) | copy-start | bytes 49156
  3.2 37.3 %copy-start.17 = (bf16[512,8]{0,1:T(8,128)(2,1)S(1)}, bf16[512,8]{0,1:T(8,128)(2,1)}, u32[]{:S(2)}) copy-start(bf16[512,8]{0,1:T(8,128)(2,1)} %param.23) | copy-start | bytes 24580
  3.3 37.3 %copy-start.18 = (s32[128,1]{0,1:T(1,128)S(1)}, s32[128,1]{0,1:T(1,128)}, u32[]{:S(2)}) copy-start(s32[128,1]{0,1:T(1,128)} %param.20) | copy-start | bytes 1540
  3.3 34.1 %all-to-all-start = ((bf16[64,24,512]{2,1,0:T(8,128)(2,1)}), bf16[64,24,512]{2,1,0:T(8,128)(2,1)S(1)}, u32[]{:S(2)}, u32[]{:S(2)}) async-start(bf16[64,24,512]{2,1,0:T(8,128)(2,1)} %shard_map.157), calls=%async_computation | async-start | bytes 3145728 | tf_op jit(solution)/shard_map/all_to_all | solution.py:70
  37.3 13.2 %collective-permute-start = (bf16[64,24,512]{2,1,0:T(8,128)(2,1)S(1)}, bf16[64,24,512]{2,1,0:T(8,128)(2,1)S(1)}, u32[]{:S(2)}, u32[]{:S(2)}) collective-permute-start(bf16[64,24,512]{2,1,0:T(8,128)(2,1)S(1)} %all-to-all-done.bundle), channel_id=1, source_target_pairs={{0,1},{1,0},{2,3},{3,2},{4,5},{5,4},{6,7},{7,6},{8,9},{9,8},{10,11... | collective-permute-start | bytes 4718600 | tf_op jit(solution)/shard_map/ppermute | solution.py:58
  40.5 1.0 copy-start.15
  49.4 1.1 copy-start.19
  49.4 1.1 copy-start.21
  49.4 1.2 copy-start.10
  49.4 4.3 %collective-permute-start.3 = (bf16[1792,512]{1,0:T(8,128)(2,1)S(1)}, bf16[1792,512]{1,0:T(8,128)(2,1)S(1)}, u32[]{:S(2)}, u32[]{:S(2)}) collective-permute-start(bf16[1792,512]{1,0:T(8,128)(2,1)S(1)} %get-tuple-element.37), channel_id=1, source_target_pairs={{0,1},{1,0},{2,3},{3,2},{4,5},{5,4},{6,7},{7,6},{8,9},{9,8},{10,11... | collective-permute-start | bytes 5505032 | tf_op jit(solution)/shard_map/ppermute | solution.py:58
  49.5 1.4 %copy-start = (bf16[512,512]{1,0:T(8,128)(2,1)S(1)}, bf16[512,512]{1,0:T(8,128)(2,1)}, u32[]{:S(2)}) copy-start(bf16[512,512]{1,0:T(8,128)(2,1)} %wneigh.5) | copy-start | bytes 1572868
  49.5 1.7 %copy-start.3 = (bf16[512,512]{1,0:T(8,128)(2,1)S(1)}, bf16[512,512]{1,0:T(8,128)(2,1)}, u32[]{:S(2)}) copy-start(bf16[512,512]{1,0:T(8,128)(2,1)} %cot.1) | copy-start | bytes 1572868
  53.7 2.3 %collective-permute-start.1 = (bf16[768,512]{1,0:T(8,128)(2,1)S(1)}, bf16[768,512]{1,0:T(8,128)(2,1)S(1)}, u32[]{:S(2)}, u32[]{:S(2)}) collective-permute-start(bf16[768,512]{1,0:T(8,128)(2,1)S(1)} %get-tuple-element.33.pack), channel_id=1, source_target_pairs={{0,1},{1,0},{2,3},{3,2},{4,5},{5,4},{6,7},{7,6},{8,9},{9,8},{10,11... | collective-permute-start | bytes 2359304 | tf_op jit(solution)/shard_map/ppermute | solution.py:58
  57.5 17.7 %all-to-all-start.2 = ((bf16[64,8,512]{2,1,0:T(8,128)(2,1)}), bf16[64,8,512]{2,1,0:T(8,128)(2,1)}, u32[]{:S(2)}, u32[]{:S(2)}) async-start(bf16[64,8,512]{2,1,0:T(8,128)(2,1)} %shard_map.164), calls=%async_computation.2 | async-start | bytes 1048576 | tf_op jit(solution)/shard_map/all_to_all | solution.py:70
  63.0 5.9 %collective-permute-start.2 = (f32[512,1]{1,0:T(8,128)}, f32[512,1]{1,0:T(8,128)S(1)}, u32[]{:S(2)}, u32[]{:S(2)}) collective-permute-start(f32[512,1]{1,0:T(8,128)} %copy-done.10), channel_id=1, source_target_pairs={{0,1},{1,0},{2,3},{3,2},{4,5},{5,4},{6,7},{7,6},{8,9},{9,8},{10,11... | collective-permute-start | bytes 6152 | tf_op jit(solution)/shard_map/ppermute | solution.py:58
  63.2 1.0 copy-start.1
  64.3 0.9 copy-start.11
  65.2 1.2 copy-start.20
  66.4 1.0 copy-start.22
  67.5 1.4 %copy-start.2 = (bf16[512,512]{1,0:T(8,128)(2,1)S(1)}, bf16[512,512]{1,0:T(8,128)(2,1)}, u32[]{:S(2)}) copy-start(bf16[512,512]{1,0:T(8,128)(2,1)} %wneigh.5) | copy-start | bytes 1572868
  75.2 51.6 %all-to-all-start.1 = ((bf16[64,24,512]{2,1,0:T(8,128)(2,1)}), bf16[64,24,512]{2,1,0:T(8,128)(2,1)S(1)}, u32[]{:S(2)}, u32[]{:S(2)}) async-start(bf16[64,24,512]{2,1,0:T(8,128)(2,1)} %shard_map.162), calls=%async_computation.1 | async-start | bytes 3145728 | tf_op jit(solution)/shard_map/all_to_all | solution.py:70
  82.4 10.3 %collective-permute-start.4 = (bf16[8,512]{1,0:T(8,128)(2,1)S(1)}, bf16[8,512]{1,0:T(8,128)(2,1)S(1)}, u32[]{:S(2)}, u32[]{:S(2)}) collective-permute-start(bf16[8,512]{1,0:T(8,128)(2,1)S(1)} %shard_map.165.a), channel_id=1, source_target_pairs={{0,2},{2,4},{4,6},{6,0},{1,3},{3,5},{5,7},{7,1},{8,10},{10,12},{12... | collective-permute-start | bytes 24584 | tf_op jit(solution)/shard_map/ppermute | solution.py:64
  83.4 13.3 %collective-permute-start.5 = (bf16[8,512]{1,0:T(8,128)(2,1)S(1)}, bf16[8,512]{1,0:T(8,128)(2,1)S(1)}, u32[]{:S(2)}, u32[]{:S(2)}) collective-permute-start(bf16[8,512]{1,0:T(8,128)(2,1)S(1)} %shard_map.165.a), channel_id=1, source_target_pairs={{0,4},{2,6},{4,0},{6,2},{1,5},{3,7},{5,1},{7,3},{8,12},{10,14},{12... | collective-permute-start | bytes 24584 | tf_op jit(solution)/shard_map/ppermute | solution.py:64
  85.8 10.9 %collective-permute-start.6 = (bf16[8,512]{1,0:T(8,128)(2,1)S(1)}, bf16[8,512]{1,0:T(8,128)(2,1)S(1)}, u32[]{:S(2)}, u32[]{:S(2)}) collective-permute-start(bf16[8,512]{1,0:T(8,128)(2,1)S(1)} %shard_map.165.a), channel_id=1, source_target_pairs={{0,6},{2,0},{4,2},{6,4},{1,7},{3,1},{5,3},{7,5},{8,14},{10,8},{12,... | collective-permute-start | bytes 24584 | tf_op jit(solution)/shard_map/ppermute | solution.py:64
  96.7 6.0 %collective-permute-start.7 = (bf16[32,512]{1,0:T(8,128)(2,1)S(1)}, bf16[32,512]{1,0:T(8,128)(2,1)S(1)}, u32[]{:S(2)}, u32[]{:S(2)}) collective-permute-start(bf16[32,512]{1,0:T(8,128)(2,1)S(1)} %shard_map.166.a), channel_id=1, source_target_pairs={{0,8},{8,16},{16,24},{24,0},{1,9},{9,17},{17,25},{25,1},{2,10},{10... | collective-permute-start | bytes 98312 | tf_op jit(solution)/shard_map/ppermute | solution.py:64
  96.8 6.0 %collective-permute-start.8 = (bf16[32,512]{1,0:T(8,128)(2,1)S(1)}, bf16[32,512]{1,0:T(8,128)(2,1)S(1)}, u32[]{:S(2)}, u32[]{:S(2)}) collective-permute-start(bf16[32,512]{1,0:T(8,128)(2,1)S(1)} %shard_map.166.a), channel_id=1, source_target_pairs={{0,16},{8,24},{16,0},{24,8},{1,17},{9,25},{17,1},{25,9},{2,18},{10... | collective-permute-start | bytes 98312 | tf_op jit(solution)/shard_map/ppermute | solution.py:64
  100.4 3.5 %collective-permute-start.9 = (bf16[32,512]{1,0:T(8,128)(2,1)S(1)}, bf16[32,512]{1,0:T(8,128)(2,1)S(1)}, u32[]{:S(2)}, u32[]{:S(2)}) collective-permute-start(bf16[32,512]{1,0:T(8,128)(2,1)S(1)} %shard_map.166.a), channel_id=1, source_target_pairs={{0,24},{8,0},{16,8},{24,16},{1,25},{9,1},{17,9},{25,17},{2,26},{10... | collective-permute-start | bytes 98312 | tf_op jit(solution)/shard_map/ppermute | solution.py:64
  103.9 12.6 %collective-permute-start.11 = (bf16[128,512]{1,0:T(8,128)(2,1)S(1)}, bf16[128,512]{1,0:T(8,128)(2,1)S(1)}, u32[]{:S(2)}, u32[]{:S(2)}) collective-permute-start(bf16[128,512]{1,0:T(8,128)(2,1)S(1)} %shard_map.167.a), channel_id=1, source_target_pairs={{0,32},{32,64},{64,96},{96,0},{1,33},{33,65},{65,97},{97,1},{2,34}... | collective-permute-start | bytes 393224 | tf_op jit(solution)/shard_map/ppermute | solution.py:64
  107.8 9.8 %collective-permute-start.13 = (bf16[128,512]{1,0:T(8,128)(2,1)S(1)}, bf16[128,512]{1,0:T(8,128)(2,1)S(1)}, u32[]{:S(2)}, u32[]{:S(2)}) collective-permute-start(bf16[128,512]{1,0:T(8,128)(2,1)S(1)} %shard_map.167.a), channel_id=1, source_target_pairs={{0,64},{32,96},{64,0},{96,32},{1,65},{33,97},{65,1},{97,33},{2,66}... | collective-permute-start | bytes 393224 | tf_op jit(solution)/shard_map/ppermute | solution.py:64
  111.8 7.3 %collective-permute-start.15 = (bf16[128,512]{1,0:T(8,128)(2,1)S(1)}, bf16[128,512]{1,0:T(8,128)(2,1)S(1)}, u32[]{:S(2)}, u32[]{:S(2)}) collective-permute-start(bf16[128,512]{1,0:T(8,128)(2,1)S(1)} %shard_map.167.a), channel_id=1, source_target_pairs={{0,96},{32,0},{64,32},{96,64},{1,97},{33,1},{65,33},{97,65},{2,98}... | collective-permute-start | bytes 393224 | tf_op jit(solution)/shard_map/ppermute | solution.py:64
  113.1 12.5 %collective-permute-start.10 = (bf16[128,512]{1,0:T(8,128)(2,1)S(1)}, bf16[128,512]{1,0:T(8,128)(2,1)S(1)}, u32[]{:S(2)}, u32[]{:S(2)}) collective-permute-start(bf16[128,512]{1,0:T(8,128)(2,1)S(1)} %shard_map.167.a), channel_id=1, source_target_pairs={{0,1},{1,0},{2,3},{3,2},{4,5},{5,4},{6,7},{7,6},{8,9},{9,8},{10,11... | collective-permute-start | bytes 393224 | tf_op jit(solution)/shard_map/ppermute | solution.py:58
  116.5 9.2 %collective-permute-start.12 = (bf16[128,512]{1,0:T(8,128)(2,1)S(1)}, bf16[128,512]{1,0:T(8,128)(2,1)S(1)}, u32[]{:S(2)}, u32[]{:S(2)}) collective-permute-start(bf16[128,512]{1,0:T(8,128)(2,1)S(1)} %collective-permute-done.11.b), channel_id=1, source_target_pairs={{0,1},{1,0},{2,3},{3,2},{4,5},{5,4},{6,7},{7,6},{8,9},{9,8},{10,11... | collective-permute-start | bytes 393224 | tf_op jit(solution)/shard_map/ppermute | solution.py:58
  117.6 8.1 %collective-permute-start.14 = (bf16[128,512]{1,0:T(8,128)(2,1)S(1)}, bf16[128,512]{1,0:T(8,128)(2,1)S(1)}, u32[]{:S(2)}, u32[]{:S(2)}) collective-permute-start(bf16[128,512]{1,0:T(8,128)(2,1)S(1)} %collective-permute-done.13.c), channel_id=1, source_target_pairs={{0,1},{1,0},{2,3},{3,2},{4,5},{5,4},{6,7},{7,6},{8,9},{9,8},{10,11... | collective-permute-start | bytes 393224 | tf_op jit(solution)/shard_map/ppermute | solution.py:58
  119.1 6.5 %collective-permute-start.16 = (bf16[128,512]{1,0:T(8,128)(2,1)S(1)}, bf16[128,512]{1,0:T(8,128)(2,1)S(1)}, u32[]{:S(2)}, u32[]{:S(2)}) collective-permute-start(bf16[128,512]{1,0:T(8,128)(2,1)S(1)} %collective-permute-done.15.d), channel_id=1, source_target_pairs={{0,1},{1,0},{2,3},{3,2},{4,5},{5,4},{6,7},{7,6},{8,9},{9,8},{10,11... | collective-permute-start | bytes 393224 | tf_op jit(solution)/shard_map/ppermute | solution.py:58
  119.7 1.0 copy-start.6
  120.7 1.0 copy-start.8
  121.8 1.0 copy-start.9
  124.4 2.5 %copy-start.12 = (s32[128,4]{0,1:T(4,128)S(1)}, s32[128,4]{0,1:T(4,128)}, u32[]{:S(2)}) copy-start(s32[128,4]{0,1:T(4,128)} %param.19) | copy-start | bytes 6148
  124.4 2.4 %copy-start.14 = (s32[16]{0:T(128)S(1)}, s32[16]{0:T(128)}, u32[]{:S(2)}) copy-start(s32[16]{0:T(128)} %param.21) | copy-start | bytes 196

commit v3 on v1

--- a/solution.py
+++ b/solution.py
@@ -24,7 +24,7 @@
 LIMIT = 8 << 20
 
 
-def call(body, outs, specs, flops, *args, scratch=(), to=None, alias=None):
+def call(body, outs, specs, flops, *args, scratch=(), to=None, alias=None, limit=LIMIT):
     size = sum(a.size * a.dtype.itemsize for a in args)
     size += sum(o.size * o.dtype.itemsize for o in outs)
     spaces = to or [VM] * len(outs)
@@ -37,7 +37,7 @@
         out_specs=tuple(spaces),
         scratch_shapes=list(scratch),
         input_output_aliases=alias or {},
-        compiler_params=pltpu.CompilerParams(vmem_limit_bytes=LIMIT),
+        compiler_params=pltpu.CompilerParams(vmem_limit_bytes=limit),
         cost_estimate=pl.CostEstimate(flops=flops, bytes_accessed=size, transcendentals=0),
     )(*args)
 
@@ -56,6 +56,10 @@
 
 def pair(x):
     return lax.ppermute(x, CORE, [(0, 1), (1, 0)])
+
+
+def in_hbm(x):
+    return pltpu.with_memory_space_constraint(x, pltpu.MemorySpace.HBM)
 
 
 def over_chips(x):
@@ -119,43 +123,120 @@
     cols,
     count,
     core,
+    feats_at,
+    lweight_at,
+    cweight_at,
+    wself_at,
+    counts,
+    edges,
+    hubw,
+    local_sum_at,
+    self_term_at,
+    dense_at,
+    flip_own_at,
+    cut_own_at,
+    wide_own_at,
+    feat_own_at,
+    degree,
+    ship,
+    ship_wide,
     feats,
     lweight,
     cweight,
-    counts,
-    edges,
-    hubw,
     wself,
     local_sum,
     self_term,
-    degree,
     dense,
-    dense_far,
     flip_own,
     cut_own,
     wide_own,
-    wide_far,
     feat_own,
-    ship,
     masked,
     picked,
+    sem,
 ):
+    reads = [
+        pltpu.make_async_copy(src, dst, sem.at[i])
+        for i, (src, dst) in enumerate(
+            ((cweight_at, cweight), (feats_at, feats), (lweight_at, lweight), (wself_at, wself))
+        )
+    ]
+    for read in reads:
+        read.start()
+    writes = []
+
+    def put(src, dst):
+        write = pltpu.make_async_copy(src, dst, sem.at[4 + len(writes)])
+        write.start()
+        writes.append(write)
+
     rows, feat = feats.shape
     slots = cweight.shape[1]
-    hubs = 2 * dense.shape[1]
+    hubs = 2 * flip_own.shape[0]
     blocks = rows // TILE
     live = count[0]
     me = core[0]
-    masked[...] = jnp.where(iota((rows, feat), 0) < live, feats[...], jnp.zeros_like(feats))
-    self_term[...] = mm(masked[...], wself[...])
+    edge_w = hubw[...]
     deep = slots // counts.shape[1]
+    width = hubs // (2 * (slots // (2 * deep)))
+    owner = edges[...] // width
+    place = ((owner % 2) ^ me) * (hubs // 2) + (owner // 2) * width + edges[...] % width
+    weight = edge_w.astype(F32)
+    step = 128
+
+    def build(i, carry):
+        base = pl.multiple_of(i * step, step)
+        hub = iota((step, rows), 0) + base
+        acc = jnp.zeros((step, rows), F32)
+        for k in range(edges.shape[0]):
+            acc = acc + jnp.where(place[k : k + 1, :] == hub, weight[k : k + 1, :], 0.0)
+        flat = acc.astype(BF)
+
+        @pl.when(base < hubs // 2)
+        def _():
+            flip_own[pl.ds(base, step), :] = flat
+            dense[:, pl.ds(base, step)] = jnp.transpose(flat)
+
+        @pl.when(base >= hubs // 2)
+        def _():
+            spot = pl.multiple_of(base - hubs // 2, step)
+            ship[pl.ds(spot, step), :] = flat
+            ship_wide[:, pl.ds(spot, step)] = jnp.transpose(flat)
+
+        return carry
+
+    lax.fori_loop(0, hubs // step, build, 0)
+    put(flip_own, flip_own_at)
+    put(dense, dense_at)
     fan = ones_where(iota((counts.shape[1], slots), 0) == iota((counts.shape[1], slots), 1) // deep)
     used = mm(small(counts[...]), fan)
     on = (iota((1, slots), 1) % deep).astype(F32) < used
+    reads[0].wait()
     cut = cweight[...] * jnp.broadcast_to(ones_where(on), (rows, slots))
-    edge_w = hubw[...]
     hub_deg = mm_tn(edge_w, jnp.ones((edge_w.shape[0], TILE), BF))[:, :1]
     degree[...] = hub_deg + jnp.sum(cut.astype(F32), axis=1, keepdims=True)
+    flip = jnp.transpose(cut)
+    side = (iota((slots, rows), 0) // deep) % 2
+    kept = jnp.where(side == me, flip, jnp.zeros_like(flip))
+    tall = flip.astype(F32)
+    up = pltpu.roll(tall, slots - deep, 0)
+    down = pltpu.roll(tall, deep, 0)
+    moved = jnp.where(side == me, jnp.where(me == 0, up, down), 0.0).astype(BF)
+    cut_own[...] = kept
+    put(cut_own, cut_own_at)
+    wide_own[...] = jnp.transpose(kept)
+    put(wide_own, wide_own_at)
+    ship[hubs // 2 : hubs // 2 + slots, :] = moved
+    ship_wide[:, hubs // 2 :] = jnp.transpose(moved)
+    reads[1].wait()
+    half = feat // 2
+    feat_own[...] = jnp.transpose(jnp.where(me == 0, feats[:, :half], feats[:, half:]))
+    put(feat_own, feat_own_at)
+    ship[hubs // 2 + slots :, :] = jnp.transpose(
+        jnp.where(me == 0, feats[:, half:], feats[:, :half])
+    )
+    masked[...] = jnp.where(iota((rows, feat), 0) < live, feats[...], jnp.zeros_like(feats))
+    reads[2].wait()
     lane = iota((TILE, TILE), 1)
     for r in range(blocks):
         part = jnp.zeros((TILE, 1), F32)
@@ -167,50 +248,12 @@
             part = part + jnp.sum(jnp.where(lane + base < live, vals, 0.0), axis=1, keepdims=True)
         local_sum[at, :] = mm(lweight[at, :], picked[...])
         degree[at, :] += part
-    flip = jnp.transpose(cut)
-    side = (iota((slots, rows), 0) // deep) % 2
-    kept = jnp.where(side == me, flip, jnp.zeros_like(flip))
-    tall = flip.astype(F32)
-    up = pltpu.roll(tall, slots - deep, 0)
-    down = pltpu.roll(tall, deep, 0)
-    moved = jnp.where(side == me, jnp.where(me == 0, up, down), 0.0).astype(BF)
-    cut_own[...] = kept
-    wide_own[...] = jnp.transpose(kept)
-    wide_far[...] = jnp.transpose(moved)
-    half = feat // 2
-    ship[hubs // 2 : hubs // 2 + slots, :] = moved
-    feat_own[...] = jnp.transpose(jnp.where(me == 0, feats[:, :half], feats[:, half:]))
-    ship[hubs // 2 + slots :, :] = jnp.transpose(
-        jnp.where(me == 0, feats[:, half:], feats[:, :half])
-    )
-    width = hubs // (2 * (slots // (2 * deep)))
-    owner = edges[...] // width
-    place = ((owner % 2) ^ me) * (hubs // 2) + (owner // 2) * width + edges[...] % width
-    weight = edge_w.astype(F32)
-    step = 128
-
-    def build(i, carry):
-        base = pl.multiple_of(i * step, step)
-        hub = iota((step, rows), 0) + base
-        acc = jnp.zeros((step, rows), F32)
-        for k in range(edges.shape[0]):
-            acc = acc + jnp.where(place[k : k + 1, :] == hub, weight[k : k + 1, :], 0.0)
-        flat = acc.astype(BF)
-
-        @pl.when(base < hubs // 2)
-        def _():
-            flip_own[pl.ds(base, step), :] = flat
-            dense[:, pl.ds(base, step)] = jnp.transpose(flat)
-
-        @pl.when(base >= hubs // 2)
-        def _():
-            spot = pl.multiple_of(base - hubs // 2, step)
-            ship[pl.ds(spot, step), :] = flat
-            dense_far[:, pl.ds(spot, step)] = jnp.transpose(flat)
-
-        return carry
-
-    lax.fori_loop(0, hubs // step, build, 0)
+    put(local_sum, local_sum_at)
+    reads[3].wait()
+    self_term[...] = mm(masked[...], wself[...])
+    put(self_term, self_term_at)
+    for write in writes:
+        write.wait()
 
 
 def sides(bundle, width, feat):
@@ -219,20 +262,48 @@
     return table, bundle[:, width:, :].reshape(peers * (deep - width), feat)
 
 
-def near_sum(wide_own, dense, bundle, out):
-    _, feat = out.shape
-    table, cut = sides(bundle, dense.shape[1] // bundle.shape[0], feat)
-    out[...] = mm(wide_own[...], cut) + mm(dense[...], table)
-
-
-def forward(
-    core, count, near, local_sum, wide_far, dense, bundle, degree, self_term, wneigh, cot, act, mean_own, pack
-):
+def settle(ship_in, wide_in, degree_in, ship, wide, degree):
+    pass
+
+
+def fetched_sum(bundle, cut_at, dense_at, cut_w, dense_w, sem):
+    feat = bundle.shape[2]
+    hubs = dense_w.shape[1]
+    part = hubs // 2
+    reads = [pltpu.make_async_copy(cut_at, cut_w, sem.at[0])]
+    for i in range(2):
+        span = pl.ds(i * part, part)
+        reads.append(
+            pltpu.make_async_copy(dense_at.at[:, span], dense_w.at[:, span], sem.at[1 + i])
+        )
+    for read in reads:
+        read.start()
+    table, cut = sides(bundle, hubs // bundle.shape[0], feat)
+    reads[0].wait()
+    total = mm(cut_w[...], cut)
+    reads[1].wait()
+    total = total + mm(dense_w[:, :part], table[:part])
+    reads[2].wait()
+    return total + mm(dense_w[:, part:], table[part:])
+
+
+def far_sum(wide, bundle, out, cut_w, dense_w, sem):
+    hubs = dense_w.shape[1]
+    slots = cut_w.shape[1]
+    out[...] = fetched_sum(
+        bundle, wide.at[:, pl.ds(hubs, slots)], wide.at[:, pl.ds(0, hubs)], cut_w, dense_w, sem
+    ).astype(BF)
+
+
+def near_sum(wide_own, dense, bundle, out, cut_w, dense_w, sem):
+    out[...] = fetched_sum(bundle, wide_own, dense, cut_w, dense_w, sem)
+
+
+def forward(core, count, near, far, local_sum, degree, self_term, wneigh, cot, act, mean_own, pack):
     rows, feat = near.shape
     half = feat // 2
     me = core[0]
-    table, cut = sides(bundle, dense.shape[1] // bundle.shape[0], feat)
-    total = local_sum[...] + near[...] + mm(wide_far[...], cut) + mm(dense[...], table)
+    total = local_sum[...] + near[...] + far[...].astype(F32)
     mean = (total / degree[...]).astype(BF)
     mean_own[...] = jnp.transpose(jnp.where(me == 0, mean[:, :half], mean[:, half:]))
     pack[:half, :] = jnp.transpose(jnp.where(me == 0, mean[:, half:], mean[:, :half]))
@@ -386,7 +457,7 @@
         [like((chips, width + 2 * deep, feat))],
         [HB] * 3,
         unit,
-        *[pltpu.with_memory_space_constraint(x, pltpu.MemorySpace.HBM) for x in (routes, hub_ids, features)],
+        *[in_hbm(x) for x in (routes, hub_ids, features)],
         to=[HB],
         scratch=[
             pltpu.VMEM(routes.shape, routes.dtype),
@@ -398,64 +469,73 @@
         ],
     )
     bundle = over_chips(bundle)
-    (
-        local_sum,
-        self_term,
-        degree,
-        dense,
-        dense_far,
-        flip_own,
-        cut_own,
-        wide_own,
-        wide_far,
-        feat_own,
-        ship,
-    ) = call(
+    held = [
+        like((rows, feat), F32),
+        like((rows, feat), F32),
+        like((rows, hubs // 2)),
+        like((hubs // 2, rows)),
+        like((slots, rows)),
+        like((rows, slots)),
+        like((half, rows)),
+    ]
+    sources = (features, local_weight, cut_weight, weight_self)
+    local_sum, self_term, dense, flip_own, cut_own, wide_own, feat_own, degree, ship, ship_wide = call(
         ahead,
-        [
-            like((rows, feat), F32),
-            like((rows, feat), F32),
+        held
+        + [
             like((rows, 1), F32),
-            like((rows, hubs // 2)),
-            like((rows, hubs // 2)),
-            like((hubs // 2, rows)),
-            like((slots, rows)),
-            like((rows, slots)),
-            like((rows, slots)),
-            like((half, rows)),
             like((hubs // 2 + slots + half, rows)),
+            like((rows, hubs // 2 + slots)),
         ],
-        [SM, SM, SM] + [VM] * 7,
+        [SM, SM, SM] + [HB] * 4 + [VM] * 3,
         40 * unit,
         tile_cols,
         row_counts,
         core,
-        features,
-        local_weight,
-        cut_weight,
+        *[in_hbm(x) for x in sources],
         send_count.T,
         hub_edges.T,
         hub_weight.T,
-        weight_self,
-        scratch=[pltpu.VMEM((rows, feat), BF), pltpu.VMEM((TPR * TILE, feat), BF)],
-    )
-    degree_far = pair(degree)
-    ship_far = pair(ship)
-
-    bundle_far = pair(bundle)
-    (near,) = call(near_sum, [like((rows, feat), F32)], [VM] * 3, 3 * unit, wide_own, dense, bundle)
+        to=[HB] * len(held) + [VM] * 3,
+        scratch=[pltpu.VMEM(x.shape, x.dtype) for x in (*sources, *held)]
+        + [pltpu.VMEM((rows, feat), BF), pltpu.VMEM((TPR * TILE, feat), BF), DMA((4 + len(held),))],
+        limit=20 << 20,
+    )
+    pairs = [in_hbm(pair(x)) for x in (ship, ship_wide, degree)]
+    ship_far, wide_far, degree_far = call(
+        settle,
+        [like(x.shape, x.dtype) for x in (ship, ship_wide, degree)],
+        [HB] * 3,
+        1 << 20,
+        *pairs,
+        to=[HB] * 3,
+        alias={0: 0, 1: 1, 2: 2},
+    )
+    weights = [pltpu.VMEM((rows, slots), BF), pltpu.VMEM((rows, hubs // 2), BF), DMA((3,))]
+    (far,) = call(
+        far_sum, [like((rows, feat))], [HB, VM], 3 * unit, in_hbm(wide_far), bundle, scratch=weights
+    )
+    far = pair(far)
+    (near,) = call(
+        near_sum,
+        [like((rows, feat), F32)],
+        [HB, HB, VM],
+        3 * unit,
+        in_hbm(wide_own),
+        in_hbm(dense),
+        bundle,
+        scratch=weights,
+    )
     activated, mean_own, pack = call(
         forward,
         [like((rows, feat)), like((half, rows)), like((half + rows, feat))],
-        [SM, SM] + [VM] * 9,
-        4 * unit,
+        [SM, SM] + [VM] * 7,
+        unit,
         core,
         row_counts,
         near,
+        far,
         local_sum,
-        wide_far,
-        dense_far,
-        bundle_far,
         degree,
         self_term,
         weight_neigh,
@@ -523,8 +603,8 @@
         back,
     )
     grads = [like((feat, feat), F32)] * 2
-    held = [pltpu.VMEM((2, half, feat), F32), DMA((2,))]
-    halfway = call(place_own, grads, [SM, VM], 1 << 20, core, weight_all, to=[HB, HB], scratch=held)
+    wide = [pltpu.VMEM((2, half, feat), F32), DMA((2,))]
+    halfway = call(place_own, grads, [SM, VM], 1 << 20, core, weight_all, to=[HB, HB], scratch=wide)
     grad_self, grad_neigh = call(
         place_far,
         grads,
@@ -534,7 +614,7 @@
         weight_pair,
         *halfway,
         to=[HB, HB],
-        scratch=held,
+        scratch=wide,
         alias={2: 0, 3: 1},
     )
     return activated, feature_grad, grad_self, grad_neigh

time: 119 us -> 131 us (1.10)
  Pallas kernels: 24.1 us -> 30.5 us
  local copies, waits for them, and re-layouts: 1.28 us -> 6.59 us
  waiting for transfers between devices: 21.8 us -> 19.4 us
  blocking collectives: 51.5 us -> 53.4 us
    pallas_call x12 -> x14, Pallas kernels: 24.1 us -> 30.5 us  [call(): pl.pallas_call(body, out_shape=tuple((pltpu.MemorySpace.HBM(o.shape, o.dt...]
    unnamed x26 -> x46, local copies, waits for them, and re-layouts: 1.28 us -> 6.59 us
    all_to_all x1, waiting for transfers between devices: 21.3 us -> 18 us  [over_chips(): return lax.all_to_all(x, CHIPS, 0, 0, tiled=True)]
    all_to_all x2, blocking collectives: 51.5 us -> 53.4 us  [over_chips(): return lax.all_to_all(x, CHIPS, 0, 0, tiled=True)]
    ppermute x5 -> x6, starting transfers between devices: 6.36 us -> 7.54 us  [pair(): return lax.ppermute(x, CORE, [(0, 1), (1, 0)])]
  transfers between devices with their start and end apart: 6 -> 7, of which waited for: 2 -> 2; matrix products, arithmetic and copies ran while one was open for 0% -> 0% of each run, Pallas kernels for 14% -> 8%
where the time goes in v3:
time: 131 us; the launch traced here: 130 us
  blocking collectives  53.4 us (41%)
  Pallas kernels  30.5 us (23%)
  waiting for transfers between devices  19.4 us (15%)
  starting transfers between devices  18.8 us (14%)
  local copies, waits for them, and re-layouts  6.59 us (5%)
  between operations  1.51 us (1%)
    all_to_all x2, blocking collectives, over_chips(): return lax.all_to_all(x, CHIPS, 0, 0, tiled=True)  53.4 us
    pallas_call x14, Pallas kernels, call(): pl.pallas_call(body, out_shape=tuple((pltpu.MemorySpace.HBM(o.shape, o.dt...  30.5 us
    all_to_all x1, waiting for transfers between devices, over_chips(): return lax.all_to_all(x, CHIPS, 0, 0, tiled=True)  18 us
    all_to_all x1, starting transfers between devices, over_chips(): return lax.all_to_all(x, CHIPS, 0, 0, tiled=True)  11.3 us
    ppermute x6, starting transfers between devices, pair(): return lax.ppermute(x, CORE, [(0, 1), (1, 0)])  7.54 us
    unnamed x46, local copies, waits for them, and re-layouts  6.59 us
  transfers between devices with their start and end apart: 7, of which 2 were waited for; matrix products, arithmetic and copies ran while one was open for 0% of the time, Pallas kernels for 8%

profile of v3, /device:TPU:1, one launch (start us, length us, event | category | flops | bytes accessed | tf_op | source)
XLA Modules:
  0.0 130.2 jit_solution(6904108646358954763)
XLA Ops:
  1.3 0.0 copy-start.15
  1.3 0.7 copy-done.15
  2.0 0.0 copy-start.18
  2.0 0.7 copy-done.18
  2.7 0.0 copy-start.19
  2.7 0.7 copy-done.19
  3.4 0.0 copy-start.20
  3.4 0.7 copy-done.20
  4.0 11.2 %shard_map.156 = (f32[512,512]{1,0:T(8,128)}, f32[512,512]{1,0:T(8,128)}, bf16[512,1024]{1,0:T(8,128)(2,1)}, bf16[1024,512]{1,0:T(8,128)(2,1)}, bf16[512,512]{1,...) custom-call(s32[4,4]{1,0:T(4,128)S(1)} %copy-done.15, ...), custom_call_target="tpu_custom_call" | custom-call | flops 10737418240 | bytes 11037256 | tf_op jit(solution)/shard_map/pallas_call | solution.py:31
  15.3 0.0 copy-start.12
  15.3 0.7 copy-done.12
  15.9 1.4 %collective-permute-start = (bf16[1792,512]{1,0:T(8,128)(2,1)}, bf16[1792,512]{1,0:T(8,128)(2,1)S(1)}, u32[]{:S(2)}, u32[]{:S(2)}) collective-permute-start(bf16[1792,512]{1,0:T(8,128)(2,1)} %get-tuple-element.29), channel_id=1, source_target_pairs={{0,1},{1,0},{2,3},{3,2},{4,5},{5,4},{6,7},{7,6},{8,9},{9,8},{10,11... | collective-permute-start | bytes 5505032 | tf_op jit(solution)/shard_map/ppermute | solution.py:58
  17.3 0.0 collective-permute-start.1
  17.3 2.6 %shard_map.157 = bf16[64,24,512]{2,1,0:T(8,128)(2,1)} custom-call(s32[4,128]{1,0:T(4,128)} %bitcast.6, s32[1,16]{1,0:T(1,128)} %bitcast.8, bf16[512,512]{1,0:T(8,128)(2,1)} %feats_at.3), custom_call_target="tpu_custom_call" | custom-call | flops 268435456 | bytes 2099264 | tf_op jit(solution)/shard_map/pallas_call | solution.py:31
  19.9 11.3 %all-to-all-start = ((bf16[64,24,512]{2,1,0:T(8,128)(2,1)}), bf16[64,24,512]{2,1,0:T(8,128)(2,1)S(1)}, u32[]{:S(2)}, u32[]{:S(2)}) async-start(bf16[64,24,512]{2,1,0:T(8,128)(2,1)} %shard_map.157), calls=%async_computation | async-start | bytes 3145728 | tf_op jit(solution)/shard_map/all_to_all | solution.py:66
  31.2 0.9 collective-permute-start.2
  32.0 1.4 %collective-permute-done.2.degree_in = f32[512,1]{1,0:T(8,128)S(1)} collective-permute-done((f32[512,1]{1,0:T(8,128)}, f32[512,1]{1,0:T(8,128)S(1)}, u32[]{:S(2)}, u32[]{:S(2)}) %collective-permute-start.2) | collective-permute-done | bytes 2080 | tf_op jit(solution)/shard_map/ppermute | solution.py:58
  33.4 0.0 collective-permute-done.1.wide_in
  33.4 0.0 collective-permute-done.ship_in
  33.4 0.7 copy-done.3
  34.1 1.2 copy-done
  35.4 18.0 %all-to-all-done.bundle = bf16[64,24,512]{2,1,0:T(8,128)(2,1)S(1)} async-done(((bf16[64,24,512]{2,1,0:T(8,128)(2,1)}), bf16[64,24,512]{2,1,0:T(8,128)(2,1)S(1)}, u32[]{:S(2)}, u32[]{:S(2)}) %all-to-all-start) | async-done | bytes 1572896 | tf_op jit(solution)/shard_map/all_to_all | solution.py:66
  53.3 2.3 %shard_map.160 = bf16[512,512]{1,0:T(8,128)(2,1)S(1)} custom-call(bf16[512,1536]{1,0:T(8,128)(2,1)} %get-tuple-element.32.wide, bf16[64,24,512]{2,1,0:T(8,128)(2,1)S(1)} %all-to-all-done.bundle), custom_call_target="tpu_custom_call" | custom-call | flops 805306368 | bytes 3670016 | tf_op jit(solution)/shard_map/pallas_call | solution.py:31
  55.6 3.0 %collective-permute-start.3 = (bf16[512,512]{1,0:T(8,128)(2,1)S(1)}, bf16[512,512]{1,0:T(8,128)(2,1)S(1)}, u32[]{:S(2)}, u32[]{:S(2)}) collective-permute-start(bf16[512,512]{1,0:T(8,128)(2,1)S(1)} %shard_map.160), channel_id=1, source_target_pairs={{0,1},{1,0},{2,3},{3,2},{4,5},{5,4},{6,7},{7,6},{8,9},{9,8},{10,11... | collective-permute-start | bytes 1572872 | tf_op jit(solution)/shard_map/ppermute | solution.py:58
  58.6 0.0 copy-start.2
  58.6 0.0 copy-start.5
  58.6 0.0 copy-start.6
  58.6 0.0 copy-start.13
  58.7 2.4 %shard_map.158.near = f32[512,512]{1,0:T(8,128)S(1)} custom-call(bf16[512,512]{1,0:T(8,128)(2,1)} %get-tuple-element.27.wide_own, bf16[512,1024]{1,0:T(8,128)(2,1)} %get-tuple-element.28.dense, bf16[64,24,512]{2,1,0:T(8,128)(2,1)S(1)} %all-to-all-done.bundle), custom_call_target="tpu_custom_call" | custom-call | flops 805306368 | bytes 4194304 | tf_op jit(solution)/shard_map/pallas_call | solution.py:31
  61.1 0.0 collective-permute-done.3.far
  61.1 0.0 copy-done.2
  61.1 0.0 copy-done.5
  61.1 0.0 copy-done.6
  61.1 0.0 copy-done.10
  61.1 0.0 copy-done.13
  61.1 0.0 copy-start.11
  61.1 1.6 %shard_map.161 = (bf16[512,512]{1,0:T(8,128)(2,1)}, bf16[256,512]{1,0:T(8,128)(2,1)S(1)}, bf16[768,512]{1,0:T(8,128)(2,1)S(1)}) custom-call(s32[1]{0:T(128)} %bitcast.core, s32[1]{0:T(128)S(6)} %copy.27.count, f32[512,512]{1,0:T(8,128)S(1)} %shard_map.158.near, bf16[512,512]{1,0:T(8,128)(2,1)S(1)} %collective-permute-done.3.far, f32[512,512]{1,0:T(8,128)S(1)} %copy-done.5, ...), custom_call_target="tpu_custom_call" | custom-call | flops 268435456 | bytes 6293512 | tf_op jit(solution)/shard_map/pallas_call | solution.py:31
  62.8 0.0 copy-start.21
  62.8 0.0 copy-start.22
  62.8 0.1 collective-permute-start.4
  62.9 0.0 copy-done.11
  62.9 0.4 shard_map.164.weight
  63.3 0.7 copy-done.21
  64.0 0.1 copy-done.22
  64.2 1.4 %shard_map.162 = (bf16[512,512]{1,0:T(8,128)(2,1)}, f32[1024,512]{1,0:T(8,128)S(1)}, f32[512,512]{1,0:T(8,128)S(1)}) custom-call(bf16[768,512]{1,0:T(8,128)(2,1)S(1)} %get-tuple-element.36.pack, bf16[512,512]{1,0:T(8,128)(2,1)S(1)} %copy-done.2, f32[512,1]{1,0:T(8,128)S(1)} %copy-done.13, bf16[1024,512]{1,0:T(8,128)(2,1)S(1)} %copy-done.21, ...), custom_call_target="tpu_custom_call" | custom-call | flops 1073741824 | bytes 6555648 | tf_op jit(solution)/shard_map/pallas_call | solution.py:31
  65.5 0.0 collective-permute-done.4.pack
  65.5 0.2 copy-done.1
  65.7 0.1 copy-done.4
  65.8 2.5 %shard_map.165 = bf16[64,32,512]{2,1,0:T(8,128)(2,1)} custom-call(bf16[768,512]{1,0:T(8,128)(2,1)S(1)} %collective-permute-done.4.pack, bf16[512,512]{1,0:T(8,128)(2,1)S(1)} %copy-done.2, f32[512,1]{1,0:T(8,128)S(1)} %copy-done.4, bf16[1792,512]{1,0:T(8,128)(2,1)S(1)} %copy-done.1, f32[1024,512]{1,0:T(8,128)S(1)} %get-tuple-element.42.hub, ...), custom_call_target="tpu_custom_call" | custom-call | flops 1342177280 | bytes 9439232 | tf_op jit(solution)/shard_map/pallas_call | solution.py:31
  68.4 33.9 %all_to_all.15.bundle.parts = bf16[64,32,512]{2,1,0:T(8,128)(2,1)S(1)} all-to-all(bf16[64,32,512]{2,1,0:T(8,128)(2,1)} %shard_map.165), channel_id=1, replica_groups=mesh['dom_0'=4,'dom_1'=4,'dom_2'=4,'dom_3'=2] {'dom_0','dom_1','dom_2'}, dimensions={0} | all-to-all | bytes 4194304 | tf_op jit(solution)/shard_map/all_to_all | solution.py:66
  102.2 0.9 shard_map.167
  103.2 19.6 %all_to_all.16.source = bf16[64,8,512]{2,1,0:T(8,128)(2,1)S(1)} all-to-all(bf16[64,8,512]{2,1,0:T(8,128)(2,1)} %shard_map.167), channel_id=1, replica_groups=mesh['dom_0'=4,'dom_1'=4,'dom_2'=4,'dom_3'=2] {'dom_0','dom_1','dom_2'}, dimensions={0} | all-to-all | bytes 1048576 | tf_op jit(solution)/shard_map/all_to_all | solution.py:66
  122.7 2.2 %collective-permute-start.5 = (bf16[64,8,512]{2,1,0:T(8,128)(2,1)S(1)}, bf16[64,8,512]{2,1,0:T(8,128)(2,1)S(1)}, u32[]{:S(2)}, u32[]{:S(2)}) collective-permute-start(bf16[64,8,512]{2,1,0:T(8,128)(2,1)S(1)} %all_to_all.16.source), channel_id=1, source_target_pairs={{0,1},{1,0},{2,3},{3,2},{4,5},{5,4},{6,7},{7,6},{8,9},{9,8},{10,11... | collective-permute-start | bytes 1572872 | tf_op jit(solution)/shard_map/ppermute | solution.py:58
  125.0 0.0 copy-done.7
  125.0 0.0 copy-done.8
  125.0 0.0 copy-done.9
  125.0 0.0 copy-done.16
  125.0 1.6 %shard_map.163.rows_in = f32[512,512]{1,0:T(8,128)S(1)} custom-call(s32[4,4]{1,0:T(4,128)S(1)} %copy-done.16, bf16[768,512]{1,0:T(8,128)(2,1)S(1)} %get-tuple-element.36.pack, bf16[512,512]{1,0:T(8,128)(2,1)S(1)} %copy-done.8, bf16[512,512]{1,0:T(8,128)(2,1)S(1)} %copy-done.7, bf16[512,512]{1,0:T(8,128)(2,1)S(1)} %copy-done.9), custom_call_target="tpu_custom_call" | custom-call | flops 805306368 | bytes 3407936 | tf_op jit(solution)/shard_map/pallas_call | solution.py:31
  126.6 0.0 copy-done.14
  126.6 0.0 copy-done.17
  126.6 1.5 %shard_map.166 = bf16[512,512]{1,0:T(8,128)(2,1)} custom-call(s32[1]{0:T(128)S(6)} %copy.27.count, f32[512,512]{1,0:T(8,128)S(1)} %shard_map.163.rows_in, s32[4,128]{1,0:T(4,128)S(1)} %bitcast.7, s32[1,16]{1,0:T(1,128)S(1)} %bitcast.9, bf16[64,32,512]{2,1,0:T(8,128)(2,1)S(1)} %all_to_all.15.bundle.parts), custom_call_target="tpu_custom_call" | custom-call | flops 536870912 | bytes 3672132 | tf_op jit(solution)/shard_map/pallas_call | solution.py:31
  128.1 1.0 shard_map.168
  129.1 0.0 collective-permute-done.5.source
  129.2 1.0 shard_map.169
  (12 shorter events, 0.0 us)
Async XLA Ops:
  1.3 0.7 copy-start.15
  2.0 0.7 copy-start.18
  2.7 0.7 copy-start.19
  3.4 0.7 copy-start.20
  15.3 0.7 copy-start.12
  15.9 17.5 %collective-permute-start = (bf16[1792,512]{1,0:T(8,128)(2,1)}, bf16[1792,512]{1,0:T(8,128)(2,1)S(1)}, u32[]{:S(2)}, u32[]{:S(2)}) collective-permute-start(bf16[1792,512]{1,0:T(8,128)(2,1)} %get-tuple-element.29), channel_id=1, source_target_pairs={{0,1},{1,0},{2,3},{3,2},{4,5},{5,4},{6,7},{7,6},{8,9},{9,8},{10,11... | collective-permute-start | bytes 5505032 | tf_op jit(solution)/shard_map/ppermute | solution.py:58
  17.3 16.1 %collective-permute-start.1 = (bf16[512,1536]{1,0:T(8,128)(2,1)}, bf16[512,1536]{1,0:T(8,128)(2,1)}, u32[]{:S(2)}, u32[]{:S(2)}) collective-permute-start(bf16[512,1536]{1,0:T(8,128)(2,1)} %get-tuple-element.30), channel_id=1, source_target_pairs={{0,1},{1,0},{2,3},{3,2},{4,5},{5,4},{6,7},{7,6},{8,9},{9,8},{10,11... | collective-permute-start | bytes 4718600 | tf_op jit(solution)/shard_map/ppermute | solution.py:58
  19.9 33.4 %all-to-all-start = ((bf16[64,24,512]{2,1,0:T(8,128)(2,1)}), bf16[64,24,512]{2,1,0:T(8,128)(2,1)S(1)}, u32[]{:S(2)}, u32[]{:S(2)}) async-start(bf16[64,24,512]{2,1,0:T(8,128)(2,1)} %shard_map.157), calls=%async_computation | async-start | bytes 3145728 | tf_op jit(solution)/shard_map/all_to_all | solution.py:66
  31.2 2.2 %collective-permute-start.2 = (f32[512,1]{1,0:T(8,128)}, f32[512,1]{1,0:T(8,128)S(1)}, u32[]{:S(2)}, u32[]{:S(2)}) collective-permute-start(f32[512,1]{1,0:T(8,128)} %copy-done.12), channel_id=1, source_target_pairs={{0,1},{1,0},{2,3},{3,2},{4,5},{5,4},{6,7},{7,6},{8,9},{9,8},{10,11... | collective-permute-start | bytes 6152 | tf_op jit(solution)/shard_map/ppermute | solution.py:58
  33.4 0.7 copy-start.3
  34.1 1.2 copy-start
  55.6 5.5 %collective-permute-start.3 = (bf16[512,512]{1,0:T(8,128)(2,1)S(1)}, bf16[512,512]{1,0:T(8,128)(2,1)S(1)}, u32[]{:S(2)}, u32[]{:S(2)}) collective-permute-start(bf16[512,512]{1,0:T(8,128)(2,1)S(1)} %shard_map.160), channel_id=1, source_target_pairs={{0,1},{1,0},{2,3},{3,2},{4,5},{5,4},{6,7},{7,6},{8,9},{9,8},{10,11... | collective-permute-start | bytes 1572872 | tf_op jit(solution)/shard_map/ppermute | solution.py:58
  58.6 2.5 %copy-start.2 = (bf16[512,512]{1,0:T(8,128)(2,1)S(1)}, bf16[512,512]{1,0:T(8,128)(2,1)}, u32[]{:S(2)}) copy-start(bf16[512,512]{1,0:T(8,128)(2,1)} %wneigh.5) | copy-start | bytes 1572868
  58.6 2.5 %copy-start.5 = (f32[512,512]{1,0:T(8,128)S(1)}, f32[512,512]{1,0:T(8,128)}, u32[]{:S(2)}) copy-start(f32[512,512]{1,0:T(8,128)} %get-tuple-element.33.local_sum) | copy-start | bytes 3145732
  58.6 2.5 %copy-start.6 = (f32[512,512]{1,0:T(8,128)S(1)}, f32[512,512]{1,0:T(8,128)}, u32[]{:S(2)}) copy-start(f32[512,512]{1,0:T(8,128)} %get-tuple-element.34.self_term) | copy-start | bytes 3145732
  58.6 2.5 %copy-start.10 = (bf16[512,512]{1,0:T(8,128)(2,1)S(1)}, bf16[512,512]{1,0:T(8,128)(2,1)}, u32[]{:S(2)}) copy-start(bf16[512,512]{1,0:T(8,128)(2,1)} %cot.1) | copy-start | bytes 1572868
  58.6 2.5 %copy-start.13 = (f32[512,1]{1,0:T(8,128)S(1)}, f32[512,1]{1,0:T(8,128)}, u32[]{:S(2)}) copy-start(f32[512,1]{1,0:T(8,128)} %copy-done.12) | copy-start | bytes 6148
  61.1 1.7 %copy-start.11 = (bf16[256,512]{1,0:T(8,128)(2,1)S(1)}, bf16[256,512]{1,0:T(8,128)(2,1)}, u32[]{:S(2)}) copy-start(bf16[256,512]{1,0:T(8,128)(2,1)} %get-tuple-element.45.feat_own) | copy-start | bytes 786436
  62.8 1.2 copy-start.21
  62.8 1.4 %copy-start.22 = (bf16[512,512]{1,0:T(8,128)(2,1)S(1)}, bf16[512,512]{1,0:T(8,128)(2,1)}, u32[]{:S(2)}) copy-start(bf16[512,512]{1,0:T(8,128)(2,1)} %get-tuple-element.38.cut_own) | copy-start | bytes 1572868
  62.8 2.7 %collective-permute-start.4 = (bf16[768,512]{1,0:T(8,128)(2,1)S(1)}, bf16[768,512]{1,0:T(8,128)(2,1)S(1)}, u32[]{:S(2)}, u32[]{:S(2)}) collective-permute-start(bf16[768,512]{1,0:T(8,128)(2,1)S(1)} %get-tuple-element.36.pack), channel_id=1, source_target_pairs={{0,1},{1,0},{2,3},{3,2},{4,5},{5,4},{6,7},{7,6},{8,9},{9,8},{10,11... | collective-permute-start | bytes 2359304 | tf_op jit(solution)/shard_map/ppermute | solution.py:58
  64.2 1.6 %copy-start.1 = (bf16[1792,512]{1,0:T(8,128)(2,1)S(1)}, bf16[1792,512]{1,0:T(8,128)(2,1)}, u32[]{:S(2)}) copy-start(bf16[1792,512]{1,0:T(8,128)(2,1)} %get-tuple-element.41.ship) | copy-start | bytes 5505028
  64.2 1.7 %copy-start.4 = (f32[512,1]{1,0:T(8,128)S(1)}, f32[512,1]{1,0:T(8,128)}, u32[]{:S(2)}) copy-start(f32[512,1]{1,0:T(8,128)} %get-tuple-element.40.degree) | copy-start | bytes 6148
  102.2 22.7 %copy-start.7 = (bf16[512,512]{1,0:T(8,128)(2,1)S(1)}, bf16[512,512]{1,0:T(8,128)(2,1)}, u32[]{:S(2)}) copy-start(bf16[512,512]{1,0:T(8,128)(2,1)} %lweight.1) | copy-start | bytes 1572868
  102.2 22.7 %copy-start.8 = (bf16[512,512]{1,0:T(8,128)(2,1)S(1)}, bf16[512,512]{1,0:T(8,128)(2,1)}, u32[]{:S(2)}) copy-start(bf16[512,512]{1,0:T(8,128)(2,1)} %wself.1) | copy-start | bytes 1572868
  102.2 22.7 %copy-start.9 = (bf16[512,512]{1,0:T(8,128)(2,1)S(1)}, bf16[512,512]{1,0:T(8,128)(2,1)}, u32[]{:S(2)}) copy-start(bf16[512,512]{1,0:T(8,128)(2,1)} %get-tuple-element.39.gmean) | copy-start | bytes 1572868
  102.2 22.7 %copy-start.16 = (s32[4,4]{1,0:T(4,128)S(1)}, s32[4,4]{1,0:T(4,128)}, u32[]{:S(2)}) copy-start(s32[4,4]{1,0:T(4,128)} %cols.3) | copy-start | bytes 196
  122.7 3.8 %copy-start.14 = (s32[128,4]{0,1:T(4,128)S(1)}, s32[128,4]{0,1:T(4,128)}, u32[]{:S(2)}) copy-start(s32[128,4]{0,1:T(4,128)} %param.19) | copy-start | bytes 6148
  122.7 3.9 %copy-start.17 = (s32[16]{0:T(128)S(1)}, s32[16]{0:T(128)}, u32[]{:S(2)}) copy-start(s32[16]{0:T(128)} %param.21) | copy-start | bytes 196
  122.7 6.4 %collective-permute-start.5 = (bf16[64,8,512]{2,1,0:T(8,128)(2,1)S(1)}, bf16[64,8,512]{2,1,0:T(8,128)(2,1)S(1)}, u32[]{:S(2)}, u32[]{:S(2)}) collective-permute-start(bf16[64,8,512]{2,1,0:T(8,128)(2,1)S(1)} %all_to_all.16.source), channel_id=1, source_target_pairs={{0,1},{1,0},{2,3},{3,2},{4,5},{5,4},{6,7},{7,6},{8,9},{9,8},{10,11... | collective-permute-start | bytes 1572872 | tf_op jit(solution)/shard_map/ppermute | solution.py:58

commit v4 on v3

--- a/solution.py
+++ b/solution.py
@@ -137,9 +137,10 @@
     cut_own_at,
     wide_own_at,
     feat_own_at,
-    degree,
+    dense_far_at,
+    wide_far_at,
+    degree_at,
     ship,
-    ship_wide,
     feats,
     lweight,
     cweight,
@@ -151,6 +152,9 @@
     cut_own,
     wide_own,
     feat_own,
+    dense_far,
+    wide_far,
+    degree,
     masked,
     picked,
     sem,
@@ -201,13 +205,14 @@
         def _():
             spot = pl.multiple_of(base - hubs // 2, step)
             ship[pl.ds(spot, step), :] = flat
-            ship_wide[:, pl.ds(spot, step)] = jnp.transpose(flat)
+            dense_far[:, pl.ds(spot, step)] = jnp.transpose(flat)
 
         return carry
 
     lax.fori_loop(0, hubs // step, build, 0)
     put(flip_own, flip_own_at)
     put(dense, dense_at)
+    put(dense_far, dense_far_at)
     fan = ones_where(iota((counts.shape[1], slots), 0) == iota((counts.shape[1], slots), 1) // deep)
     used = mm(small(counts[...]), fan)
     on = (iota((1, slots), 1) % deep).astype(F32) < used
@@ -227,7 +232,8 @@
     wide_own[...] = jnp.transpose(kept)
     put(wide_own, wide_own_at)
     ship[hubs // 2 : hubs // 2 + slots, :] = moved
-    ship_wide[:, hubs // 2 :] = jnp.transpose(moved)
+    wide_far[...] = jnp.transpose(moved)
+    put(wide_far, wide_far_at)
     reads[1].wait()
     half = feat // 2
     feat_own[...] = jnp.transpose(jnp.where(me == 0, feats[:, :half], feats[:, half:]))
@@ -249,6 +255,7 @@
         local_sum[at, :] = mm(lweight[at, :], picked[...])
         degree[at, :] += part
     put(local_sum, local_sum_at)
+    put(degree, degree_at)
     reads[3].wait()
     self_term[...] = mm(masked[...], wself[...])
     put(self_term, self_term_at)
@@ -262,48 +269,101 @@
     return table, bundle[:, width:, :].reshape(peers * (deep - width), feat)
 
 
-def settle(ship_in, wide_in, degree_in, ship, wide, degree):
+def settle(ship_in, degree_in, ship, degree):
     pass
 
 
-def fetched_sum(bundle, cut_at, dense_at, cut_w, dense_w, sem):
-    feat = bundle.shape[2]
-    hubs = dense_w.shape[1]
-    part = hubs // 2
-    reads = [pltpu.make_async_copy(cut_at, cut_w, sem.at[0])]
-    for i in range(2):
-        span = pl.ds(i * part, part)
-        reads.append(
-            pltpu.make_async_copy(dense_at.at[:, span], dense_w.at[:, span], sem.at[1 + i])
-        )
+def near_sum(
+    wide_at,
+    dense_at,
+    local_at,
+    dense_far_at,
+    wide_far_at,
+    self_at,
+    degree_at,
+    cot_at,
+    wneigh_at,
+    bundle,
+    out,
+    dense_far,
+    wide_far,
+    self_term,
+    degree,
+    cot,
+    wneigh,
+    wide,
+    dense,
+    local,
+    sem,
+):
+    pairs = (
+        (wide_at, wide),
+        (dense_at, dense),
+        (local_at, local),
+        (wide_far_at, wide_far),
+        (dense_far_at, dense_far),
+        (self_at, self_term),
+        (degree_at, degree),
+        (wneigh_at, wneigh),
+        (cot_at, cot),
+    )
+    reads = [pltpu.make_async_copy(src, dst, sem.at[i]) for i, (src, dst) in enumerate(pairs)]
     for read in reads:
         read.start()
-    table, cut = sides(bundle, hubs // bundle.shape[0], feat)
+    _, feat = out.shape
+    table, cut = sides(bundle, dense.shape[1] // bundle.shape[0], feat)
     reads[0].wait()
-    total = mm(cut_w[...], cut)
+    total = mm(wide[...], cut)
     reads[1].wait()
-    total = total + mm(dense_w[:, :part], table[:part])
+    total = total + mm(dense[...], table)
     reads[2].wait()
-    return total + mm(dense_w[:, part:], table[part:])
-
-
-def far_sum(wide, bundle, out, cut_w, dense_w, sem):
-    hubs = dense_w.shape[1]
-    slots = cut_w.shape[1]
-    out[...] = fetched_sum(
-        bundle, wide.at[:, pl.ds(hubs, slots)], wide.at[:, pl.ds(0, hubs)], cut_w, dense_w, sem
-    ).astype(BF)
-
-
-def near_sum(wide_own, dense, bundle, out, cut_w, dense_w, sem):
-    out[...] = fetched_sum(bundle, wide_own, dense, cut_w, dense_w, sem)
-
-
-def forward(core, count, near, far, local_sum, degree, self_term, wneigh, cot, act, mean_own, pack):
+    out[...] = total + local[...]
+    for read in reads[3:]:
+        read.wait()
+
+
+def forward(
+    core,
+    count,
+    flip_at,
+    cut_at,
+    feat_at,
+    ship_at,
+    degree_far_at,
+    near,
+    wide_far,
+    dense,
+    bundle,
+    degree,
+    self_term,
+    wneigh,
+    cot,
+    act_at,
+    mean_own,
+    pack,
+    flip,
+    cut_own,
+    feat_own,
+    ship,
+    degree_far,
+    act,
+    sem,
+):
+    pairs = (
+        (flip_at, flip),
+        (cut_at, cut_own),
+        (feat_at, feat_own),
+        (ship_at, ship),
+        (degree_far_at, degree_far),
+    )
+    reads = [pltpu.make_async_copy(src, dst, sem.at[i]) for i, (src, dst) in enumerate(pairs)]
+    for read in reads:
+        read.start()
     rows, feat = near.shape
     half = feat // 2
     me = core[0]
-    total = local_sum[...] + near[...] + far[...].astype(F32)
+    table, cut = sides(bundle, dense.shape[1] // bundle.shape[0], feat)
+    total = near[...] + mm(wide_far[...], cut) + mm(dense[...], table)
     mean = (total / degree[...]).astype(BF)
     mean_own[...] = jnp.transpose(jnp.where(me == 0, mean[:, :half], mean[:, half:]))
     pack[:half, :] = jnp.transpose(jnp.where(me == 0, mean[:, half:], mean[:, :half]))
@@ -311,8 +371,13 @@
     pre = self_term[...] + mm(mean, wneigh[...])
     sig = jax.nn.sigmoid(pre)
     act[...] = jnp.where(live, pre * sig, 0.0).astype(BF)
+    away = pltpu.make_async_copy(act, act_at, sem.at[len(reads)])
+    away.start()
     grad = cot[...].astype(F32) * sig * (1.0 + pre * (1.0 - sig))
     pack[half:, :] = jnp.where(live, grad, 0.0).astype(BF)
+    for read in reads:
+        read.wait()
+    away.wait()
 
 
 def back_near(pack, wneigh, degree, flip_own, cut_own, gmean, hub, cut, near, sem):
@@ -477,16 +542,26 @@
         like((slots, rows)),
         like((rows, slots)),
         like((half, rows)),
+        like((rows, hubs // 2)),
+        like((rows, slots)),
+        like((rows, 1), F32),
     ]
     sources = (features, local_weight, cut_weight, weight_self)
-    local_sum, self_term, dense, flip_own, cut_own, wide_own, feat_own, degree, ship, ship_wide = call(
+    (
+        local_sum,
+        self_term,
+        dense,
+        flip_own,
+        cut_own,
+        wide_own,
+        feat_own,
+        dense_far,
+        wide_far,
+        degree,
+        ship,
+    ) = call(
         ahead,
-        held
-        + [
-            like((rows, 1), F32),
-            like((hubs // 2 + slots + half, rows)),
-            like((rows, hubs // 2 + slots)),
-        ],
+        held + [like((hubs // 2 + slots + half, rows))],
         [SM, SM, SM] + [HB] * 4 + [VM] * 3,
         40 * unit,
         tile_cols,
@@ -496,50 +571,52 @@
         send_count.T,
         hub_edges.T,
         hub_weight.T,
-        to=[HB] * len(held) + [VM] * 3,
+        to=[HB] * len(held) + [VM],
         scratch=[pltpu.VMEM(x.shape, x.dtype) for x in (*sources, *held)]
         + [pltpu.VMEM((rows, feat), BF), pltpu.VMEM((TPR * TILE, feat), BF), DMA((4 + len(held),))],
         limit=20 << 20,
     )
-    pairs = [in_hbm(pair(x)) for x in (ship, ship_wide, degree)]
-    ship_far, wide_far, degree_far = call(
+    ship_far, degree_far = call(
         settle,
-        [like(x.shape, x.dtype) for x in (ship, ship_wide, degree)],
-        [HB] * 3,
+        [like(ship.shape), like(degree.shape, F32)],
+        [HB] * 2,
         1 << 20,
-        *pairs,
-        to=[HB] * 3,
-        alias={0: 0, 1: 1, 2: 2},
-    )
-    weights = [pltpu.VMEM((rows, slots), BF), pltpu.VMEM((rows, hubs // 2), BF), DMA((3,))]
-    (far,) = call(
-        far_sum, [like((rows, feat))], [HB, VM], 3 * unit, in_hbm(wide_far), bundle, scratch=weights
-    )
-    far = pair(far)
-    (near,) = call(
+        in_hbm(pair(ship)),
+        in_hbm(pair(degree)),
+        to=[HB] * 2,
+        alias={0: 0, 1: 1},
+    )
+    bundle_far = pair(bundle)
+    following = [dense_far, wide_far, self_term, degree, cotangent, weight_neigh]
+    near, dense_far, wide_far, self_term, degree, cotangent, weight_neigh = call(
         near_sum,
-        [like((rows, feat), F32)],
-        [HB, HB, VM],
+        [like((rows, feat), F32)] + [like(x.shape, x.dtype) for x in following],
+        [HB] * 9 + [VM],
         3 * unit,
-        in_hbm(wide_own),
-        in_hbm(dense),
+        *[in_hbm(x) for x in (wide_own, dense, local_sum, *following)],
         bundle,
-        scratch=weights,
-    )
-    activated, mean_own, pack = call(
+        scratch=[pltpu.VMEM(x.shape, x.dtype) for x in (wide_own, dense, local_sum)] + [DMA((9,))],
+    )
+    following = [flip_own, cut_own, feat_own, ship_far, degree_far]
+    activated, mean_own, pack, flip_own, cut_own, feat_own, ship_far, degree_far = call(
         forward,
-        [like((rows, feat)), like((half, rows)), like((half + rows, feat))],
-        [SM, SM] + [VM] * 7,
-        unit,
+        [like((rows, feat)), like((half, rows)), like((half + rows, feat))]
+        + [like(x.shape, x.dtype) for x in following],
+        [SM, SM] + [HB] * 5 + [VM] * 8,
+        4 * unit,
         core,
         row_counts,
+        *[in_hbm(x) for x in following],
         near,
-        far,
-        local_sum,
+        wide_far,
+        dense_far,
+        bundle_far,
         degree,
         self_term,
         weight_neigh,
         cotangent,
+        to=[HB] + [VM] * 7,
+        scratch=[pltpu.VMEM((rows, feat), BF), DMA((6,))],
     )
     pack_far = pair(pack)
     gmean, hub_part, cut_part = call(

time: 131 us -> 113 us (0.86)
  waiting for transfers between devices: 19.4 us -> 11.3 us
  local copies, waits for them, and re-layouts: 6.59 us -> 0.74 us
  Pallas kernels: 30.5 us -> 28.4 us
  blocking collectives: 53.4 us -> 51.5 us
    all_to_all x1, waiting for transfers between devices: 18 us -> 10.7 us  [over_chips(): return lax.all_to_all(x, CHIPS, 0, 0, tiled=True)]
    unnamed x46 -> x20, local copies, waits for them, and re-layouts: 6.59 us -> 0.74 us
    pallas_call x14 -> x13, Pallas kernels: 30.5 us -> 28.4 us  [call(): pl.pallas_call(body, out_shape=tuple((pltpu.MemorySpace.HBM(o.shape, o.dt...]
    all_to_all x2, blocking collectives: 53.4 us -> 51.5 us  [over_chips(): return lax.all_to_all(x, CHIPS, 0, 0, tiled=True)]
    ppermute x6 -> x5, starting transfers between devices: 7.54 us -> 7.26 us  [pair(): return lax.ppermute(x, CORE, [(0, 1), (1, 0)])]
  transfers between devices with their start and end apart: 7 -> 6, of which waited for: 2 -> 3; matrix products, arithmetic and copies ran while one was open for 0% -> 0% of each run, Pallas kernels for 8% -> 16%
where the time goes in v4:
time: 113 us
  blocking collectives  51.5 us (46%)
  Pallas kernels  28.4 us (25%)
  starting transfers between devices  19.4 us (17%)
  waiting for transfers between devices  11.3 us (10%)
  between operations  1.47 us (1%)
    all_to_all x2, blocking collectives, over_chips(): return lax.all_to_all(x, CHIPS, 0, 0, tiled=True)  51.5 us
    pallas_call x13, Pallas kernels, call(): pl.pallas_call(body, out_shape=tuple((pltpu.MemorySpace.HBM(o.shape, o.dt...  28.4 us
    all_to_all x1, starting transfers between devices, over_chips(): return lax.all_to_all(x, CHIPS, 0, 0, tiled=True)  12.1 us
    all_to_all x1, waiting for transfers between devices, over_chips(): return lax.all_to_all(x, CHIPS, 0, 0, tiled=True)  10.7 us
    ppermute x5, starting transfers between devices, pair(): return lax.ppermute(x, CORE, [(0, 1), (1, 0)])  7.26 us
  transfers between devices with their start and end apart: 6, of which 3 were waited for; matrix products, arithmetic and copies ran while one was open for 0% of the time, Pallas kernels for 16%

profile of v4, /device:TPU:1, one launch (start us, length us, event | category | flops | bytes accessed | tf_op | source)
XLA Modules:
  0.0 112.8 jit_solution(4070092849315538074)
XLA Ops:
  0.6 2.5 %shard_map.158 = bf16[64,24,512]{2,1,0:T(8,128)(2,1)} custom-call(s32[4,128]{1,0:T(4,128)} %bitcast.6, s32[1,16]{1,0:T(1,128)} %bitcast.8, bf16[512,512]{1,0:T(8,128)(2,1)} %feats_at.3), custom_call_target="tpu_custom_call" | custom-call | flops 268435456 | bytes 2099264 | tf_op jit(solution)/shard_map/pallas_call | solution.py:31
  3.2 0.0 copy-start.4
  3.2 0.0 copy-start.6
  3.2 0.0 copy-start.7
  3.2 0.0 copy-start.8
  3.2 12.1 %all-to-all-start = ((bf16[64,24,512]{2,1,0:T(8,128)(2,1)}), bf16[64,24,512]{2,1,0:T(8,128)(2,1)S(1)}, u32[]{:S(2)}, u32[]{:S(2)}) async-start(bf16[64,24,512]{2,1,0:T(8,128)(2,1)} %shard_map.158), calls=%async_computation | async-start | bytes 3145728 | tf_op jit(solution)/shard_map/all_to_all | solution.py:66
  16.0 0.0 copy-done.4
  16.0 0.0 copy-done.6
  16.0 0.0 copy-done.7
  16.0 0.0 copy-done.8
  16.0 9.5 %shard_map.156 = (f32[512,512]{1,0:T(8,128)}, f32[512,512]{1,0:T(8,128)}, bf16[512,1024]{1,0:T(8,128)(2,1)}, bf16[1024,512]{1,0:T(8,128)(2,1)}, bf16[512,512]{1,...) custom-call(s32[4,4]{1,0:T(4,128)S(1)} %copy-done.4, ...), custom_call_target="tpu_custom_call" | custom-call | flops 10737418240 | bytes 11037256 | tf_op jit(solution)/shard_map/pallas_call | solution.py:31
  25.5 1.0 collective-permute-start
  26.6 10.7 %all-to-all-done.bundle = bf16[64,24,512]{2,1,0:T(8,128)(2,1)S(1)} async-done(((bf16[64,24,512]{2,1,0:T(8,128)(2,1)}), bf16[64,24,512]{2,1,0:T(8,128)(2,1)S(1)}, u32[]{:S(2)}, u32[]{:S(2)}) %all-to-all-start) | async-done | bytes 1572896 | tf_op jit(solution)/shard_map/all_to_all | solution.py:66
  37.3 3.2 %collective-permute-start.2 = (bf16[64,24,512]{2,1,0:T(8,128)(2,1)S(1)}, bf16[64,24,512]{2,1,0:T(8,128)(2,1)S(1)}, u32[]{:S(2)}, u32[]{:S(2)}) collective-permute-start(bf16[64,24,512]{2,1,0:T(8,128)(2,1)S(1)} %all-to-all-done.bundle), channel_id=1, source_target_pairs={{0,1},{1,0},{2,3},{3,2},{4,5},{5,4},{6,7},{7,6},{8,9},{9,8},{10,11... | collective-permute-start | bytes 4718600 | tf_op jit(solution)/shard_map/ppermute | solution.py:58
  40.4 0.0 collective-permute-start.1
  40.4 2.9 %shard_map.159 = (f32[512,512]{1,0:T(8,128)S(1)}, bf16[512,1024]{1,0:T(8,128)(2,1)S(1)}, bf16[512,512]{1,0:T(8,128)(2,1)S(1)}, f32[512,512]{1,0:T(8,128)S(1)}, f...) custom-call(bf16[512,512]{1,0:T(8,128)(2,1)} %get-tuple-element.46.wide_at, ...), custom_call_target="tpu_custom_call" | custom-call | flops 805306368 | bytes 12587008 | tf_op jit(solution)/shard_map/pallas_call | solution.py:31
  43.4 0.5 collective-permute-done.1.degree_in
  43.8 0.0 copy-start.9
  43.8 0.0 collective-permute-done.ship_in
  43.8 0.7 copy-done.9
  44.5 0.0 collective-permute-done.2.bundle
  44.5 3.0 %shard_map.160 = (bf16[512,512]{1,0:T(8,128)(2,1)}, bf16[256,512]{1,0:T(8,128)(2,1)S(1)}, bf16[768,512]{1,0:T(8,128)(2,1)S(1)}, bf16[1024,512]{1,0:T(8,128)(2,1)...) custom-call(s32[1]{0:T(128)} %bitcast.core, ...), custom_call_target="tpu_custom_call" | custom-call | flops 1073741824 | bytes 15210504 | tf_op jit(solution)/shard_map/pallas_call | solution.py:31
  47.6 0.5 collective-permute-start.3
  48.0 0.4 shard_map.163.weight
  48.5 1.4 %shard_map.161 = (bf16[512,512]{1,0:T(8,128)(2,1)}, f32[1024,512]{1,0:T(8,128)S(1)}, f32[512,512]{1,0:T(8,128)S(1)}) custom-call(bf16[768,512]{1,0:T(8,128)(2,1)S(1)} %get-tuple-element.60.pack, bf16[512,512]{1,0:T(8,128)(2,1)S(1)} %get-tuple-element.57.wneigh, f32[512,1]{1,0:T(8,128)S(1)} %get-tuple-element.55.degree, ...), custom_call_target="tpu_custom_call" | custom-call | flops 1073741824 | bytes 6555648 | tf_op jit(solution)/shard_map/pallas_call | solution.py:31
  49.8 0.1 collective-permute-done.3.pack
  49.9 2.6 %shard_map.164 = bf16[64,32,512]{2,1,0:T(8,128)(2,1)} custom-call(bf16[768,512]{1,0:T(8,128)(2,1)S(1)} %collective-permute-done.3.pack, bf16[512,512]{1,0:T(8,128)(2,1)S(1)} %get-tuple-element.57.wneigh, f32[512,1]{1,0:T(8,128)S(1)} %get-tuple-element.64.degree, bf16[1792,512]{1,0:T(8,128)(2,1)S(1)} %get-tuple-element.65.ship, ...), custom_call_target="tpu_custom_call" | custom-call | flops 1342177280 | bytes 9439232 | tf_op jit(solution)/shard_map/pallas_call | solution.py:31
  52.5 32.7 %all_to_all.15.bundle.parts = bf16[64,32,512]{2,1,0:T(8,128)(2,1)S(1)} all-to-all(bf16[64,32,512]{2,1,0:T(8,128)(2,1)} %shard_map.164), channel_id=1, replica_groups=mesh['dom_0'=4,'dom_1'=4,'dom_2'=4,'dom_3'=2] {'dom_0','dom_1','dom_2'}, dimensions={0} | all-to-all | bytes 4194304 | tf_op jit(solution)/shard_map/all_to_all | solution.py:66
  85.2 0.0 copy-start
  85.2 0.0 copy-start.1
  85.2 0.0 copy-start.2
  85.2 0.9 shard_map.166
  86.1 18.8 %all_to_all.16.source = bf16[64,8,512]{2,1,0:T(8,128)(2,1)S(1)} all-to-all(bf16[64,8,512]{2,1,0:T(8,128)(2,1)} %shard_map.166), channel_id=1, replica_groups=mesh['dom_0'=4,'dom_1'=4,'dom_2'=4,'dom_3'=2] {'dom_0','dom_1','dom_2'}, dimensions={0} | all-to-all | bytes 1048576 | tf_op jit(solution)/shard_map/all_to_all | solution.py:66
  105.0 0.0 copy-start.3
  105.0 0.0 copy-start.5
  105.0 2.6 %collective-permute-start.4 = (bf16[64,8,512]{2,1,0:T(8,128)(2,1)S(1)}, bf16[64,8,512]{2,1,0:T(8,128)(2,1)S(1)}, u32[]{:S(2)}, u32[]{:S(2)}) collective-permute-start(bf16[64,8,512]{2,1,0:T(8,128)(2,1)S(1)} %all_to_all.16.source), channel_id=1, source_target_pairs={{0,1},{1,0},{2,3},{3,2},{4,5},{5,4},{6,7},{7,6},{8,9},{9,8},{10,11... | collective-permute-start | bytes 1572872 | tf_op jit(solution)/shard_map/ppermute | solution.py:58
  107.6 0.0 copy-done
  107.6 0.0 copy-done.1
  107.6 0.0 copy-done.2
  107.6 1.6 %shard_map.162.rows_in = f32[512,512]{1,0:T(8,128)S(1)} custom-call(s32[4,4]{1,0:T(4,128)S(1)} %copy-done.4, bf16[768,512]{1,0:T(8,128)(2,1)S(1)} %get-tuple-element.60.pack, bf16[512,512]{1,0:T(8,128)(2,1)S(1)} %copy-done.1, bf16[512,512]{1,0:T(8,128)(2,1)S(1)} %copy-done, bf16[512,512]{1,0:T(8,128)(2,1)S(1)} %copy-done.2), custom_call_target="tpu_custom_call" | custom-call | flops 805306368 | bytes 3407936 | tf_op jit(solution)/shard_map/pallas_call | solution.py:31
  109.2 0.0 copy-done.3
  109.2 0.0 copy-done.5
  109.2 1.5 %shard_map.165 = bf16[512,512]{1,0:T(8,128)(2,1)} custom-call(s32[1]{0:T(128)S(6)} %copy.25.count, f32[512,512]{1,0:T(8,128)S(1)} %shard_map.162.rows_in, s32[4,128]{1,0:T(4,128)S(1)} %bitcast.7, s32[1,16]{1,0:T(1,128)S(1)} %bitcast.9, bf16[64,32,512]{2,1,0:T(8,128)(2,1)S(1)} %all_to_all.15.bundle.parts), custom_call_target="tpu_custom_call" | custom-call | flops 536870912 | bytes 3672132 | tf_op jit(solution)/shard_map/pallas_call | solution.py:31
  110.7 1.0 shard_map.167
  111.7 0.0 collective-permute-done.4.source
  111.7 1.0 shard_map.168
  (1 shorter events, 0.0 us)
Async XLA Ops:
  3.2 12.8 %copy-start.4 = (s32[4,4]{1,0:T(4,128)S(1)}, s32[4,4]{1,0:T(4,128)}, u32[]{:S(2)}) copy-start(s32[4,4]{1,0:T(4,128)} %cols.3) | copy-start | bytes 196
  3.2 12.8 %copy-start.6 = (s32[512,8]{0,1:T(8,128)S(1)}, s32[512,8]{0,1:T(8,128)}, u32[]{:S(2)}) copy-start(s32[512,8]{0,1:T(8,128)} %param.22) | copy-start | bytes 49156
  3.2 12.8 %copy-start.7 = (bf16[512,8]{0,1:T(8,128)(2,1)S(1)}, bf16[512,8]{0,1:T(8,128)(2,1)}, u32[]{:S(2)}) copy-start(bf16[512,8]{0,1:T(8,128)(2,1)} %param.23) | copy-start | bytes 24580
  3.2 12.8 %copy-start.8 = (s32[128,1]{0,1:T(1,128)S(1)}, s32[128,1]{0,1:T(1,128)}, u32[]{:S(2)}) copy-start(s32[128,1]{0,1:T(1,128)} %param.20) | copy-start | bytes 1540
  3.2 34.1 %all-to-all-start = ((bf16[64,24,512]{2,1,0:T(8,128)(2,1)}), bf16[64,24,512]{2,1,0:T(8,128)(2,1)S(1)}, u32[]{:S(2)}, u32[]{:S(2)}) async-start(bf16[64,24,512]{2,1,0:T(8,128)(2,1)} %shard_map.158), calls=%async_computation | async-start | bytes 3145728 | tf_op jit(solution)/shard_map/all_to_all | solution.py:66
  25.5 18.3 %collective-permute-start = (bf16[1792,512]{1,0:T(8,128)(2,1)S(1)}, bf16[1792,512]{1,0:T(8,128)(2,1)}, u32[]{:S(2)}, u32[]{:S(2)}) collective-permute-start(bf16[1792,512]{1,0:T(8,128)(2,1)S(1)} %get-tuple-element.42), channel_id=1, source_target_pairs={{0,1},{1,0},{2,3},{3,2},{4,5},{5,4},{6,7},{7,6},{8,9},{9,8},{10,11... | collective-permute-start | bytes 5505032 | tf_op jit(solution)/shard_map/ppermute | solution.py:58
  37.3 7.3 %collective-permute-start.2 = (bf16[64,24,512]{2,1,0:T(8,128)(2,1)S(1)}, bf16[64,24,512]{2,1,0:T(8,128)(2,1)S(1)}, u32[]{:S(2)}, u32[]{:S(2)}) collective-permute-start(bf16[64,24,512]{2,1,0:T(8,128)(2,1)S(1)} %all-to-all-done.bundle), channel_id=1, source_target_pairs={{0,1},{1,0},{2,3},{3,2},{4,5},{5,4},{6,7},{7,6},{8,9},{9,8},{10,11... | collective-permute-start | bytes 4718600 | tf_op jit(solution)/shard_map/ppermute | solution.py:58
  40.4 3.4 %collective-permute-start.1 = (f32[512,1]{1,0:T(8,128)}, f32[512,1]{1,0:T(8,128)S(1)}, u32[]{:S(2)}, u32[]{:S(2)}) collective-permute-start(f32[512,1]{1,0:T(8,128)} %get-tuple-element.43.degree_at), channel_id=1, source_target_pairs={{0,1},{1,0},{2,3},{3,2},{4,5},{5,4},{6,7},{7,6},{8,9},{9,8},{10,11... | collective-permute-start | bytes 6152 | tf_op jit(solution)/shard_map/ppermute | solution.py:58
  43.8 0.7 copy-start.9
  47.6 2.4 %collective-permute-start.3 = (bf16[768,512]{1,0:T(8,128)(2,1)S(1)}, bf16[768,512]{1,0:T(8,128)(2,1)S(1)}, u32[]{:S(2)}, u32[]{:S(2)}) collective-permute-start(bf16[768,512]{1,0:T(8,128)(2,1)S(1)} %get-tuple-element.60.pack), channel_id=1, source_target_pairs={{0,1},{1,0},{2,3},{3,2},{4,5},{5,4},{6,7},{7,6},{8,9},{9,8},{10,11... | collective-permute-start | bytes 2359304 | tf_op jit(solution)/shard_map/ppermute | solution.py:58
  85.2 22.4 %copy-start = (bf16[512,512]{1,0:T(8,128)(2,1)S(1)}, bf16[512,512]{1,0:T(8,128)(2,1)}, u32[]{:S(2)}) copy-start(bf16[512,512]{1,0:T(8,128)(2,1)} %lweight.1) | copy-start | bytes 1572868
  85.2 22.4 %copy-start.1 = (bf16[512,512]{1,0:T(8,128)(2,1)S(1)}, bf16[512,512]{1,0:T(8,128)(2,1)}, u32[]{:S(2)}) copy-start(bf16[512,512]{1,0:T(8,128)(2,1)} %wself.1) | copy-start | bytes 1572868
  85.2 22.4 %copy-start.2 = (bf16[512,512]{1,0:T(8,128)(2,1)S(1)}, bf16[512,512]{1,0:T(8,128)(2,1)}, u32[]{:S(2)}) copy-start(bf16[512,512]{1,0:T(8,128)(2,1)} %get-tuple-element.63.gmean) | copy-start | bytes 1572868
  105.0 4.2 %copy-start.3 = (s32[128,4]{0,1:T(4,128)S(1)}, s32[128,4]{0,1:T(4,128)}, u32[]{:S(2)}) copy-start(s32[128,4]{0,1:T(4,128)} %param.19) | copy-start | bytes 6148
  105.0 4.2 %copy-start.5 = (s32[16]{0:T(128)S(1)}, s32[16]{0:T(128)}, u32[]{:S(2)}) copy-start(s32[16]{0:T(128)} %param.21) | copy-start | bytes 196
  105.0 6.8 %collective-permute-start.4 = (bf16[64,8,512]{2,1,0:T(8,128)(2,1)S(1)}, bf16[64,8,512]{2,1,0:T(8,128)(2,1)S(1)}, u32[]{:S(2)}, u32[]{:S(2)}) collective-permute-start(bf16[64,8,512]{2,1,0:T(8,128)(2,1)S(1)} %all_to_all.16.source), channel_id=1, source_target_pairs={{0,1},{1,0},{2,3},{3,2},{4,5},{5,4},{6,7},{7,6},{8,9},{9,8},{10,11... | collective-permute-start | bytes 1572872 | tf_op jit(solution)/shard_map/ppermute | solution.py:58

commit v5 on v4

--- a/solution.py
+++ b/solution.py
@@ -397,31 +397,23 @@
     out[half:, :] = mm(mean_own[...], grad)
 
 
-def back_far(pack, wneigh, degree, ship, hub, cut, weight, out, hubs_out, cuts_out, weights_out, sem):
+def back_far(pack, wneigh, degree, ship, hub, cut, weight, out):
     feat = wneigh.shape[0]
     half = feat // 2
     hubs, slots = hub.shape[0], cut.shape[0]
-    width, deep, share = hubs_out.shape[1], cuts_out.shape[1], weights_out.shape[1]
     peers = out.shape[0]
+    width, deep = hubs // peers, (hubs + slots) // peers
+    share = out.shape[1] - deep
     grad = pack[half:, :]
     far = (mm_nt(grad, wneigh[...]) / degree[...]).astype(BF)
+    low = weight[:half, :] + mm(ship[hubs + slots :, :], grad)
+    out[: peers // 2, deep:, :] = low.astype(BF).reshape(peers // 2, share, feat)
+    high = weight[half:, :] + mm(pack[:half, :], grad)
+    out[peers // 2 :, deep:, :] = high.astype(BF).reshape(peers // 2, share, feat)
     first = hub[...] + mm(ship[:hubs, :], far)
-    hubs_out[...] = first.astype(BF).reshape(hubs_out.shape)
-    one = pltpu.make_async_copy(hubs_out, out.at[:, pl.ds(0, width), :], sem.at[0])
-    one.start()
+    out[:, :width, :] = first.astype(BF).reshape(peers, width, feat)
     second = cut[...] + mm(ship[hubs : hubs + slots, :], far)
-    cuts_out[...] = second.astype(BF).reshape(cuts_out.shape)
-    two = pltpu.make_async_copy(cuts_out, out.at[:, pl.ds(width, deep), :], sem.at[1])
-    two.start()
-    low = weight[:half, :] + mm(ship[hubs + slots :, :], grad)
-    weights_out[: peers // 2] = low.astype(BF).reshape(peers // 2, share, feat)
-    high = weight[half:, :] + mm(pack[:half, :], grad)
-    weights_out[peers // 2 :] = high.astype(BF).reshape(peers // 2, share, feat)
-    three = pltpu.make_async_copy(weights_out, out.at[:, pl.ds(width + deep, share), :], sem.at[2])
-    three.start()
-    one.wait()
-    two.wait()
-    three.wait()
+    out[:, width:deep, :] = second.astype(BF).reshape(peers, deep - width, feat)
 
 
 def row_terms(cols, pack, wself, lweight, gmean, out):
@@ -645,13 +637,6 @@
         hub_part,
         cut_part,
         weight_part,
-        to=[HB],
-        scratch=[
-            pltpu.VMEM((chips, width, feat), BF),
-            pltpu.VMEM((chips, 2 * deep, feat), BF),
-            pltpu.VMEM((chips, share, feat), BF),
-            DMA((3,)),
-        ],
     )
     back = over_chips(back)
     (row_sum,) = call(

time: 113 us -> 111 us (0.982)
  transfers between devices with their start and end apart: 6 -> 6, of which waited for: 3 -> 3; matrix products, arithmetic and copies ran while one was open for 0% -> 0% of each run, Pallas kernels for 16% -> 17%
where the time goes in v5:
time: 111 us
  blocking collectives  50.6 us (46%)
  Pallas kernels  27.4 us (25%)
  starting transfers between devices  19.4 us (17%)
  waiting for transfers between devices  11.3 us (10%)
  between operations  1.46 us (1%)
    all_to_all x2, blocking collectives, over_chips(): return lax.all_to_all(x, CHIPS, 0, 0, tiled=True)  50.6 us
    pallas_call x13, Pallas kernels, call(): pl.pallas_call(body, out_shape=tuple((pltpu.MemorySpace.HBM(o.shape, o.dt...  27.4 us
    all_to_all x1, starting transfers between devices, over_chips(): return lax.all_to_all(x, CHIPS, 0, 0, tiled=True)  12.1 us
    all_to_all x1, waiting for transfers between devices, over_chips(): return lax.all_to_all(x, CHIPS, 0, 0, tiled=True)  10.7 us
    ppermute x5, starting transfers between devices, pair(): return lax.ppermute(x, CORE, [(0, 1), (1, 0)])  7.28 us
  transfers between devices with their start and end apart: 6, of which 3 were waited for; matrix products, arithmetic and copies ran while one was open for 0% of the time, Pallas kernels for 17%

profile of v5, /device:TPU:1, one launch (start us, length us, event | category | flops | bytes accessed | tf_op | source)
XLA Modules:
  0.0 110.8 jit_solution(1827020138154788188)
XLA Ops:
  0.6 2.5 %shard_map.158 = bf16[64,24,512]{2,1,0:T(8,128)(2,1)} custom-call(s32[4,128]{1,0:T(4,128)} %bitcast.6, s32[1,16]{1,0:T(1,128)} %bitcast.8, bf16[512,512]{1,0:T(8,128)(2,1)} %feats_at.3), custom_call_target="tpu_custom_call" | custom-call | flops 268435456 | bytes 2099264 | tf_op jit(solution)/shard_map/pallas_call | solution.py:31
  3.2 0.0 copy-start.4
  3.2 0.0 copy-start.6
  3.2 0.0 copy-start.7
  3.2 0.0 copy-start.8
  3.2 12.1 %all-to-all-start = ((bf16[64,24,512]{2,1,0:T(8,128)(2,1)}), bf16[64,24,512]{2,1,0:T(8,128)(2,1)S(1)}, u32[]{:S(2)}, u32[]{:S(2)}) async-start(bf16[64,24,512]{2,1,0:T(8,128)(2,1)} %shard_map.158), calls=%async_computation | async-start | bytes 3145728 | tf_op jit(solution)/shard_map/all_to_all | solution.py:66
  16.0 0.0 copy-done.4
  16.0 0.0 copy-done.6
  16.0 0.0 copy-done.7
  16.0 0.0 copy-done.8
  16.0 9.5 %shard_map.156 = (f32[512,512]{1,0:T(8,128)}, f32[512,512]{1,0:T(8,128)}, bf16[512,1024]{1,0:T(8,128)(2,1)}, bf16[1024,512]{1,0:T(8,128)(2,1)}, bf16[512,512]{1,...) custom-call(s32[4,4]{1,0:T(4,128)S(1)} %copy-done.4, ...), custom_call_target="tpu_custom_call" | custom-call | flops 10737418240 | bytes 11037256 | tf_op jit(solution)/shard_map/pallas_call | solution.py:31
  25.5 1.0 collective-permute-start
  26.6 10.7 %all-to-all-done.bundle = bf16[64,24,512]{2,1,0:T(8,128)(2,1)S(1)} async-done(((bf16[64,24,512]{2,1,0:T(8,128)(2,1)}), bf16[64,24,512]{2,1,0:T(8,128)(2,1)S(1)}, u32[]{:S(2)}, u32[]{:S(2)}) %all-to-all-start) | async-done | bytes 1572896 | tf_op jit(solution)/shard_map/all_to_all | solution.py:66
  37.3 3.2 %collective-permute-start.2 = (bf16[64,24,512]{2,1,0:T(8,128)(2,1)S(1)}, bf16[64,24,512]{2,1,0:T(8,128)(2,1)S(1)}, u32[]{:S(2)}, u32[]{:S(2)}) collective-permute-start(bf16[64,24,512]{2,1,0:T(8,128)(2,1)S(1)} %all-to-all-done.bundle), channel_id=1, source_target_pairs={{0,1},{1,0},{2,3},{3,2},{4,5},{5,4},{6,7},{7,6},{8,9},{9,8},{10,11... | collective-permute-start | bytes 4718600 | tf_op jit(solution)/shard_map/ppermute | solution.py:58
  40.4 0.0 collective-permute-start.1
  40.4 2.9 %shard_map.159 = (f32[512,512]{1,0:T(8,128)S(1)}, bf16[512,1024]{1,0:T(8,128)(2,1)S(1)}, bf16[512,512]{1,0:T(8,128)(2,1)S(1)}, f32[512,512]{1,0:T(8,128)S(1)}, f...) custom-call(bf16[512,512]{1,0:T(8,128)(2,1)} %get-tuple-element.46.wide_at, ...), custom_call_target="tpu_custom_call" | custom-call | flops 805306368 | bytes 12587008 | tf_op jit(solution)/shard_map/pallas_call | solution.py:31
  43.4 0.5 collective-permute-done.1.degree_in
  43.8 0.0 copy-start.9
  43.8 0.0 collective-permute-done.ship_in
  43.8 0.7 copy-done.9
  44.5 0.0 collective-permute-done.2.bundle
  44.5 3.0 %shard_map.160 = (bf16[512,512]{1,0:T(8,128)(2,1)}, bf16[256,512]{1,0:T(8,128)(2,1)S(1)}, bf16[768,512]{1,0:T(8,128)(2,1)S(1)}, bf16[1024,512]{1,0:T(8,128)(2,1)...) custom-call(s32[1]{0:T(128)} %bitcast.core, ...), custom_call_target="tpu_custom_call" | custom-call | flops 1073741824 | bytes 15210504 | tf_op jit(solution)/shard_map/pallas_call | solution.py:31
  47.6 0.5 collective-permute-start.3
  48.0 0.4 shard_map.163.weight
  48.5 1.4 %shard_map.161 = (bf16[512,512]{1,0:T(8,128)(2,1)}, f32[1024,512]{1,0:T(8,128)S(1)}, f32[512,512]{1,0:T(8,128)S(1)}) custom-call(bf16[768,512]{1,0:T(8,128)(2,1)S(1)} %get-tuple-element.60.pack, bf16[512,512]{1,0:T(8,128)(2,1)S(1)} %get-tuple-element.57.wneigh, f32[512,1]{1,0:T(8,128)S(1)} %get-tuple-element.55.degree, ...), custom_call_target="tpu_custom_call" | custom-call | flops 1073741824 | bytes 6555648 | tf_op jit(solution)/shard_map/pallas_call | solution.py:31
  49.8 0.1 collective-permute-done.3.pack
  49.9 1.6 %shard_map.164 = bf16[64,32,512]{2,1,0:T(8,128)(2,1)S(1)} custom-call(bf16[768,512]{1,0:T(8,128)(2,1)S(1)} %collective-permute-done.3.pack, bf16[512,512]{1,0:T(8,128)(2,1)S(1)} %get-tuple-element.57.wneigh, f32[512,1]{1,0:T(8,128)S(1)} %get-tuple-element.64.degree, bf16[1792,512]{1,0:T(8,128)(2,1)S(1)} %get-tuple-element.65.ship, ...), custom_call_target="tpu_custom_call" | custom-call | flops 1342177280 | bytes 9439232 | tf_op jit(solution)/shard_map/pallas_call | solution.py:31
  51.5 31.8 %all_to_all.15.bundle.parts = bf16[64,32,512]{2,1,0:T(8,128)(2,1)S(1)} all-to-all(bf16[64,32,512]{2,1,0:T(8,128)(2,1)S(1)} %shard_map.164), channel_id=1, replica_groups=mesh['dom_0'=4,'dom_1'=4,'dom_2'=4,'dom_3'=2] {'dom_0','dom_1','dom_2'}, dimensions={0} | all-to-all | bytes 4194304 | tf_op jit(solution)/shard_map/all_to_all | solution.py:66
  83.3 0.0 copy-start
  83.3 0.0 copy-start.1
  83.3 0.0 copy-start.2
  83.3 0.9 shard_map.166
  84.3 18.8 %all_to_all.16.source = bf16[64,8,512]{2,1,0:T(8,128)(2,1)S(1)} all-to-all(bf16[64,8,512]{2,1,0:T(8,128)(2,1)} %shard_map.166), channel_id=1, replica_groups=mesh['dom_0'=4,'dom_1'=4,'dom_2'=4,'dom_3'=2] {'dom_0','dom_1','dom_2'}, dimensions={0} | all-to-all | bytes 1048576 | tf_op jit(solution)/shard_map/all_to_all | solution.py:66
  103.0 0.0 copy-start.3
  103.0 0.0 copy-start.5
  103.0 2.6 %collective-permute-start.4 = (bf16[64,8,512]{2,1,0:T(8,128)(2,1)S(1)}, bf16[64,8,512]{2,1,0:T(8,128)(2,1)S(1)}, u32[]{:S(2)}, u32[]{:S(2)}) collective-permute-start(bf16[64,8,512]{2,1,0:T(8,128)(2,1)S(1)} %all_to_all.16.source), channel_id=1, source_target_pairs={{0,1},{1,0},{2,3},{3,2},{4,5},{5,4},{6,7},{7,6},{8,9},{9,8},{10,11... | collective-permute-start | bytes 1572872 | tf_op jit(solution)/shard_map/ppermute | solution.py:58
  105.6 0.0 copy-done
  105.6 0.0 copy-done.1
  105.6 0.0 copy-done.2
  105.6 1.6 %shard_map.162.rows_in = f32[512,512]{1,0:T(8,128)S(1)} custom-call(s32[4,4]{1,0:T(4,128)S(1)} %copy-done.4, bf16[768,512]{1,0:T(8,128)(2,1)S(1)} %get-tuple-element.60.pack, bf16[512,512]{1,0:T(8,128)(2,1)S(1)} %copy-done.1, bf16[512,512]{1,0:T(8,128)(2,1)S(1)} %copy-done, bf16[512,512]{1,0:T(8,128)(2,1)S(1)} %copy-done.2), custom_call_target="tpu_custom_call" | custom-call | flops 805306368 | bytes 3407936 | tf_op jit(solution)/shard_map/pallas_call | solution.py:31
  107.2 0.0 copy-done.3
  107.2 0.0 copy-done.5
  107.3 1.5 %shard_map.165 = bf16[512,512]{1,0:T(8,128)(2,1)} custom-call(s32[1]{0:T(128)S(6)} %copy.25.count, f32[512,512]{1,0:T(8,128)S(1)} %shard_map.162.rows_in, s32[4,128]{1,0:T(4,128)S(1)} %bitcast.7, s32[1,16]{1,0:T(1,128)S(1)} %bitcast.9, bf16[64,32,512]{2,1,0:T(8,128)(2,1)S(1)} %all_to_all.15.bundle.parts), custom_call_target="tpu_custom_call" | custom-call | flops 536870912 | bytes 3672132 | tf_op jit(solution)/shard_map/pallas_call | solution.py:31
  108.8 1.0 shard_map.167
  109.8 0.0 collective-permute-done.4.source
  109.8 1.0 shard_map.168
  (1 shorter events, 0.0 us)
Async XLA Ops:
  3.2 12.8 %copy-start.4 = (s32[4,4]{1,0:T(4,128)S(1)}, s32[4,4]{1,0:T(4,128)}, u32[]{:S(2)}) copy-start(s32[4,4]{1,0:T(4,128)} %cols.3) | copy-start | bytes 196
  3.2 12.8 %copy-start.6 = (s32[512,8]{0,1:T(8,128)S(1)}, s32[512,8]{0,1:T(8,128)}, u32[]{:S(2)}) copy-start(s32[512,8]{0,1:T(8,128)} %param.22) | copy-start | bytes 49156
  3.2 12.8 %copy-start.7 = (bf16[512,8]{0,1:T(8,128)(2,1)S(1)}, bf16[512,8]{0,1:T(8,128)(2,1)}, u32[]{:S(2)}) copy-start(bf16[512,8]{0,1:T(8,128)(2,1)} %param.23) | copy-start | bytes 24580
  3.2 12.8 %copy-start.8 = (s32[128,1]{0,1:T(1,128)S(1)}, s32[128,1]{0,1:T(1,128)}, u32[]{:S(2)}) copy-start(s32[128,1]{0,1:T(1,128)} %param.20) | copy-start | bytes 1540
  3.2 34.1 %all-to-all-start = ((bf16[64,24,512]{2,1,0:T(8,128)(2,1)}), bf16[64,24,512]{2,1,0:T(8,128)(2,1)S(1)}, u32[]{:S(2)}, u32[]{:S(2)}) async-start(bf16[64,24,512]{2,1,0:T(8,128)(2,1)} %shard_map.158), calls=%async_computation | async-start | bytes 3145728 | tf_op jit(solution)/shard_map/all_to_all | solution.py:66
  25.5 18.3 %collective-permute-start = (bf16[1792,512]{1,0:T(8,128)(2,1)S(1)}, bf16[1792,512]{1,0:T(8,128)(2,1)}, u32[]{:S(2)}, u32[]{:S(2)}) collective-permute-start(bf16[1792,512]{1,0:T(8,128)(2,1)S(1)} %get-tuple-element.42), channel_id=1, source_target_pairs={{0,1},{1,0},{2,3},{3,2},{4,5},{5,4},{6,7},{7,6},{8,9},{9,8},{10,11... | collective-permute-start | bytes 5505032 | tf_op jit(solution)/shard_map/ppermute | solution.py:58
  37.3 7.3 %collective-permute-start.2 = (bf16[64,24,512]{2,1,0:T(8,128)(2,1)S(1)}, bf16[64,24,512]{2,1,0:T(8,128)(2,1)S(1)}, u32[]{:S(2)}, u32[]{:S(2)}) collective-permute-start(bf16[64,24,512]{2,1,0:T(8,128)(2,1)S(1)} %all-to-all-done.bundle), channel_id=1, source_target_pairs={{0,1},{1,0},{2,3},{3,2},{4,5},{5,4},{6,7},{7,6},{8,9},{9,8},{10,11... | collective-permute-start | bytes 4718600 | tf_op jit(solution)/shard_map/ppermute | solution.py:58
  40.4 3.4 %collective-permute-start.1 = (f32[512,1]{1,0:T(8,128)}, f32[512,1]{1,0:T(8,128)S(1)}, u32[]{:S(2)}, u32[]{:S(2)}) collective-permute-start(f32[512,1]{1,0:T(8,128)} %get-tuple-element.43.degree_at), channel_id=1, source_target_pairs={{0,1},{1,0},{2,3},{3,2},{4,5},{5,4},{6,7},{7,6},{8,9},{9,8},{10,11... | collective-permute-start | bytes 6152 | tf_op jit(solution)/shard_map/ppermute | solution.py:58
  43.8 0.7 copy-start.9
  47.6 2.4 %collective-permute-start.3 = (bf16[768,512]{1,0:T(8,128)(2,1)S(1)}, bf16[768,512]{1,0:T(8,128)(2,1)S(1)}, u32[]{:S(2)}, u32[]{:S(2)}) collective-permute-start(bf16[768,512]{1,0:T(8,128)(2,1)S(1)} %get-tuple-element.60.pack), channel_id=1, source_target_pairs={{0,1},{1,0},{2,3},{3,2},{4,5},{5,4},{6,7},{7,6},{8,9},{9,8},{10,11... | collective-permute-start | bytes 2359304 | tf_op jit(solution)/shard_map/ppermute | solution.py:58
  83.3 22.3 %copy-start = (bf16[512,512]{1,0:T(8,128)(2,1)S(1)}, bf16[512,512]{1,0:T(8,128)(2,1)}, u32[]{:S(2)}) copy-start(bf16[512,512]{1,0:T(8,128)(2,1)} %lweight.1) | copy-start | bytes 1572868
  83.3 22.3 %copy-start.1 = (bf16[512,512]{1,0:T(8,128)(2,1)S(1)}, bf16[512,512]{1,0:T(8,128)(2,1)}, u32[]{:S(2)}) copy-start(bf16[512,512]{1,0:T(8,128)(2,1)} %wself.1) | copy-start | bytes 1572868
  83.3 22.3 %copy-start.2 = (bf16[512,512]{1,0:T(8,128)(2,1)S(1)}, bf16[512,512]{1,0:T(8,128)(2,1)}, u32[]{:S(2)}) copy-start(bf16[512,512]{1,0:T(8,128)(2,1)} %get-tuple-element.63.gmean) | copy-start | bytes 1572868
  103.0 4.2 %copy-start.3 = (s32[128,4]{0,1:T(4,128)S(1)}, s32[128,4]{0,1:T(4,128)}, u32[]{:S(2)}) copy-start(s32[128,4]{0,1:T(4,128)} %param.19) | copy-start | bytes 6148
  103.0 4.2 %copy-start.5 = (s32[16]{0:T(128)S(1)}, s32[16]{0:T(128)}, u32[]{:S(2)}) copy-start(s32[16]{0:T(128)} %param.21) | copy-start | bytes 196
  103.0 6.8 %collective-permute-start.4 = (bf16[64,8,512]{2,1,0:T(8,128)(2,1)S(1)}, bf16[64,8,512]{2,1,0:T(8,128)(2,1)S(1)}, u32[]{:S(2)}, u32[]{:S(2)}) collective-permute-start(bf16[64,8,512]{2,1,0:T(8,128)(2,1)S(1)} %all_to_all.16.source), channel_id=1, source_target_pairs={{0,1},{1,0},{2,3},{3,2},{4,5},{5,4},{6,7},{7,6},{8,9},{9,8},{10,11... | collective-permute-start | bytes 1572872 | tf_op jit(solution)/shard_map/ppermute | solution.py:58

commit v6 on v5

--- a/solution.py
+++ b/solution.py
@@ -361,23 +361,25 @@
         read.start()
     rows, feat = near.shape
     half = feat // 2
-    me = core[0]
+    me = core[0] % 2
     table, cut = sides(bundle, dense.shape[1] // bundle.shape[0], feat)
-    total = near[...] + mm(wide_far[...], cut) + mm(dense[...], table)
-    mean = (total / degree[...]).astype(BF)
-    mean_own[...] = jnp.transpose(jnp.where(me == 0, mean[:, :half], mean[:, half:]))
-    pack[:half, :] = jnp.transpose(jnp.where(me == 0, mean[:, half:], mean[:, :half]))
-    live = iota((rows, feat), 0) < count[0]
-    pre = self_term[...] + mm(mean, wneigh[...])
-    sig = jax.nn.sigmoid(pre)
-    act[...] = jnp.where(live, pre * sig, 0.0).astype(BF)
-    away = pltpu.make_async_copy(act, act_at, sem.at[len(reads)])
-    away.start()
-    grad = cot[...].astype(F32) * sig * (1.0 + pre * (1.0 - sig))
-    pack[half:, :] = jnp.where(live, grad, 0.0).astype(BF)
+    step = rows // 4
+    for i in range(4):
+        at = pl.ds(i * step, step)
+        total = near[at, :] + mm(wide_far[at, :], cut) + mm(dense[at, :], table)
+        mean = (total / degree[at, :]).astype(BF)
+        mean_own[:, at] = jnp.transpose(jnp.where(me == 0, mean[:, :half], mean[:, half:]))
+        pack[:half, at] = jnp.transpose(jnp.where(me == 0, mean[:, half:], mean[:, :half]))
+        live = iota((step, feat), 0) + i * step < count[0]
+        pre = self_term[at, :] + mm(mean, wneigh[...])
+        sig = jax.nn.sigmoid(pre)
+        act[at, :] = jnp.where(live, pre * sig, 0.0).astype(BF)
+        reads.append(pltpu.make_async_copy(act.at[at], act_at.at[at], sem.at[len(reads)]))
+        reads[-1].start()
+        grad = cot[at, :].astype(F32) * sig * (1.0 + pre * (1.0 - sig))
+        pack[pl.ds(half + i * step, step), :] = jnp.where(live, grad, 0.0).astype(BF)
     for read in reads:
         read.wait()
-    away.wait()
 
 
 def back_near(pack, wneigh, degree, flip_own, cut_own, gmean, hub, cut, near, sem):
@@ -608,7 +610,7 @@
         weight_neigh,
         cotangent,
         to=[HB] + [VM] * 7,
-        scratch=[pltpu.VMEM((rows, feat), BF), DMA((6,))],
+        scratch=[pltpu.VMEM((rows, feat), BF), DMA((9,))],
     )
     pack_far = pair(pack)
     gmean, hub_part, cut_part = call(

time: 111 us -> 111 us (level)
  no operation moved by 1% of the time
where the time goes in v6:
time: 111 us
  blocking collectives  50.6 us (46%)
  Pallas kernels  27.2 us (25%)
  starting transfers between devices  19.4 us (17%)
  waiting for transfers between devices  11.2 us (10%)
  between operations  1.46 us (1%)
    all_to_all x2, blocking collectives, over_chips(): return lax.all_to_all(x, CHIPS, 0, 0, tiled=True)  50.6 us
    pallas_call x13, Pallas kernels, call(): pl.pallas_call(body, out_shape=tuple((pltpu.MemorySpace.HBM(o.shape, o.dt...  27.2 us
    all_to_all x1, starting transfers between devices, over_chips(): return lax.all_to_all(x, CHIPS, 0, 0, tiled=True)  12.1 us
    all_to_all x1, waiting for transfers between devices, over_chips(): return lax.all_to_all(x, CHIPS, 0, 0, tiled=True)  10.7 us
    ppermute x5, starting transfers between devices, pair(): return lax.ppermute(x, CORE, [(0, 1), (1, 0)])  7.29 us
  transfers between devices with their start and end apart: 6, of which 3 were waited for; matrix products, arithmetic and copies ran while one was open for 0% of the time, Pallas kernels for 17%

profile of v6, /device:TPU:1, one launch (start us, length us, event | category | flops | bytes accessed | tf_op | source)
XLA Modules:
  0.0 110.6 jit_solution(5424769749497270466)
XLA Ops:
  0.6 2.5 %shard_map.158 = bf16[64,24,512]{2,1,0:T(8,128)(2,1)} custom-call(s32[4,128]{1,0:T(4,128)} %bitcast.6, s32[1,16]{1,0:T(1,128)} %bitcast.8, bf16[512,512]{1,0:T(8,128)(2,1)} %feats_at.3), custom_call_target="tpu_custom_call" | custom-call | flops 268435456 | bytes 2099264 | tf_op jit(solution)/shard_map/pallas_call | solution.py:31
  3.2 0.0 copy-start.4
  3.2 0.0 copy-start.6
  3.2 0.0 copy-start.7
  3.2 0.0 copy-start.8
  3.2 12.1 %all-to-all-start = ((bf16[64,24,512]{2,1,0:T(8,128)(2,1)}), bf16[64,24,512]{2,1,0:T(8,128)(2,1)S(1)}, u32[]{:S(2)}, u32[]{:S(2)}) async-start(bf16[64,24,512]{2,1,0:T(8,128)(2,1)} %shard_map.158), calls=%async_computation | async-start | bytes 3145728 | tf_op jit(solution)/shard_map/all_to_all | solution.py:66
  16.0 0.0 copy-done.4
  16.0 0.0 copy-done.6
  16.0 0.0 copy-done.7
  16.0 0.0 copy-done.8
  16.0 9.5 %shard_map.156 = (f32[512,512]{1,0:T(8,128)}, f32[512,512]{1,0:T(8,128)}, bf16[512,1024]{1,0:T(8,128)(2,1)}, bf16[1024,512]{1,0:T(8,128)(2,1)}, bf16[512,512]{1,...) custom-call(s32[4,4]{1,0:T(4,128)S(1)} %copy-done.4, ...), custom_call_target="tpu_custom_call" | custom-call | flops 10737418240 | bytes 11037256 | tf_op jit(solution)/shard_map/pallas_call | solution.py:31
  25.5 1.0 collective-permute-start
  26.6 10.7 %all-to-all-done.bundle = bf16[64,24,512]{2,1,0:T(8,128)(2,1)S(1)} async-done(((bf16[64,24,512]{2,1,0:T(8,128)(2,1)}), bf16[64,24,512]{2,1,0:T(8,128)(2,1)S(1)}, u32[]{:S(2)}, u32[]{:S(2)}) %all-to-all-start) | async-done | bytes 1572896 | tf_op jit(solution)/shard_map/all_to_all | solution.py:66
  37.3 3.2 %collective-permute-start.2 = (bf16[64,24,512]{2,1,0:T(8,128)(2,1)S(1)}, bf16[64,24,512]{2,1,0:T(8,128)(2,1)S(1)}, u32[]{:S(2)}, u32[]{:S(2)}) collective-permute-start(bf16[64,24,512]{2,1,0:T(8,128)(2,1)S(1)} %all-to-all-done.bundle), channel_id=1, source_target_pairs={{0,1},{1,0},{2,3},{3,2},{4,5},{5,4},{6,7},{7,6},{8,9},{9,8},{10,11... | collective-permute-start | bytes 4718600 | tf_op jit(solution)/shard_map/ppermute | solution.py:58
  40.4 0.0 collective-permute-start.1
  40.4 2.9 %shard_map.159 = (f32[512,512]{1,0:T(8,128)S(1)}, bf16[512,1024]{1,0:T(8,128)(2,1)S(1)}, bf16[512,512]{1,0:T(8,128)(2,1)S(1)}, f32[512,512]{1,0:T(8,128)S(1)}, f...) custom-call(bf16[512,512]{1,0:T(8,128)(2,1)} %get-tuple-element.46.wide_at, ...), custom_call_target="tpu_custom_call" | custom-call | flops 805306368 | bytes 12587008 | tf_op jit(solution)/shard_map/pallas_call | solution.py:31
  43.4 0.5 collective-permute-done.1.degree_in
  43.8 0.0 copy-start.9
  43.8 0.0 collective-permute-done.ship_in
  43.8 0.7 copy-done.9
  44.5 0.0 collective-permute-done.2.bundle
  44.5 2.9 %shard_map.160 = (bf16[512,512]{1,0:T(8,128)(2,1)}, bf16[256,512]{1,0:T(8,128)(2,1)S(1)}, bf16[768,512]{1,0:T(8,128)(2,1)S(1)}, bf16[1024,512]{1,0:T(8,128)(2,1)...) custom-call(s32[1]{0:T(128)} %bitcast.core, ...), custom_call_target="tpu_custom_call" | custom-call | flops 1073741824 | bytes 15210504 | tf_op jit(solution)/shard_map/pallas_call | solution.py:31
  47.4 0.5 collective-permute-start.3
  47.9 0.4 shard_map.163.weight
  48.3 1.4 %shard_map.161 = (bf16[512,512]{1,0:T(8,128)(2,1)}, f32[1024,512]{1,0:T(8,128)S(1)}, f32[512,512]{1,0:T(8,128)S(1)}) custom-call(bf16[768,512]{1,0:T(8,128)(2,1)S(1)} %get-tuple-element.60.pack, bf16[512,512]{1,0:T(8,128)(2,1)S(1)} %get-tuple-element.57.wneigh, f32[512,1]{1,0:T(8,128)S(1)} %get-tuple-element.55.degree, ...), custom_call_target="tpu_custom_call" | custom-call | flops 1073741824 | bytes 6555648 | tf_op jit(solution)/shard_map/pallas_call | solution.py:31
  49.7 0.1 collective-permute-done.3.pack
  49.8 1.6 %shard_map.164 = bf16[64,32,512]{2,1,0:T(8,128)(2,1)S(1)} custom-call(bf16[768,512]{1,0:T(8,128)(2,1)S(1)} %collective-permute-done.3.pack, bf16[512,512]{1,0:T(8,128)(2,1)S(1)} %get-tuple-element.57.wneigh, f32[512,1]{1,0:T(8,128)S(1)} %get-tuple-element.64.degree, bf16[1792,512]{1,0:T(8,128)(2,1)S(1)} %get-tuple-element.65.ship, ...), custom_call_target="tpu_custom_call" | custom-call | flops 1342177280 | bytes 9439232 | tf_op jit(solution)/shard_map/pallas_call | solution.py:31
  51.3 31.8 %all_to_all.15.bundle.parts = bf16[64,32,512]{2,1,0:T(8,128)(2,1)S(1)} all-to-all(bf16[64,32,512]{2,1,0:T(8,128)(2,1)S(1)} %shard_map.164), channel_id=1, replica_groups=mesh['dom_0'=4,'dom_1'=4,'dom_2'=4,'dom_3'=2] {'dom_0','dom_1','dom_2'}, dimensions={0} | all-to-all | bytes 4194304 | tf_op jit(solution)/shard_map/all_to_all | solution.py:66
  83.2 0.0 copy-start
  83.2 0.0 copy-start.1
  83.2 0.0 copy-start.2
  83.2 0.9 shard_map.166
  84.1 18.8 %all_to_all.16.source = bf16[64,8,512]{2,1,0:T(8,128)(2,1)S(1)} all-to-all(bf16[64,8,512]{2,1,0:T(8,128)(2,1)} %shard_map.166), channel_id=1, replica_groups=mesh['dom_0'=4,'dom_1'=4,'dom_2'=4,'dom_3'=2] {'dom_0','dom_1','dom_2'}, dimensions={0} | all-to-all | bytes 1048576 | tf_op jit(solution)/shard_map/all_to_all | solution.py:66
  102.8 0.0 copy-start.3
  102.8 0.0 copy-start.5
  102.8 2.6 %collective-permute-start.4 = (bf16[64,8,512]{2,1,0:T(8,128)(2,1)S(1)}, bf16[64,8,512]{2,1,0:T(8,128)(2,1)S(1)}, u32[]{:S(2)}, u32[]{:S(2)}) collective-permute-start(bf16[64,8,512]{2,1,0:T(8,128)(2,1)S(1)} %all_to_all.16.source), channel_id=1, source_target_pairs={{0,1},{1,0},{2,3},{3,2},{4,5},{5,4},{6,7},{7,6},{8,9},{9,8},{10,11... | collective-permute-start | bytes 1572872 | tf_op jit(solution)/shard_map/ppermute | solution.py:58
  105.5 0.0 copy-done
  105.5 0.0 copy-done.1
  105.5 0.0 copy-done.2
  105.5 1.6 %shard_map.162.rows_in = f32[512,512]{1,0:T(8,128)S(1)} custom-call(s32[4,4]{1,0:T(4,128)S(1)} %copy-done.4, bf16[768,512]{1,0:T(8,128)(2,1)S(1)} %get-tuple-element.60.pack, bf16[512,512]{1,0:T(8,128)(2,1)S(1)} %copy-done.1, bf16[512,512]{1,0:T(8,128)(2,1)S(1)} %copy-done, bf16[512,512]{1,0:T(8,128)(2,1)S(1)} %copy-done.2), custom_call_target="tpu_custom_call" | custom-call | flops 805306368 | bytes 3407936 | tf_op jit(solution)/shard_map/pallas_call | solution.py:31
  107.1 0.0 copy-done.3
  107.1 0.0 copy-done.5
  107.1 1.5 %shard_map.165 = bf16[512,512]{1,0:T(8,128)(2,1)} custom-call(s32[1]{0:T(128)S(6)} %copy.25.count, f32[512,512]{1,0:T(8,128)S(1)} %shard_map.162.rows_in, s32[4,128]{1,0:T(4,128)S(1)} %bitcast.7, s32[1,16]{1,0:T(1,128)S(1)} %bitcast.9, bf16[64,32,512]{2,1,0:T(8,128)(2,1)S(1)} %all_to_all.15.bundle.parts), custom_call_target="tpu_custom_call" | custom-call | flops 536870912 | bytes 3672132 | tf_op jit(solution)/shard_map/pallas_call | solution.py:31
  108.6 1.0 shard_map.167
  109.6 0.0 collective-permute-done.4.source
  109.6 1.0 shard_map.168
  (1 shorter events, 0.0 us)
Async XLA Ops:
  3.2 12.8 %copy-start.4 = (s32[4,4]{1,0:T(4,128)S(1)}, s32[4,4]{1,0:T(4,128)}, u32[]{:S(2)}) copy-start(s32[4,4]{1,0:T(4,128)} %cols.3) | copy-start | bytes 196
  3.2 12.8 %copy-start.6 = (s32[512,8]{0,1:T(8,128)S(1)}, s32[512,8]{0,1:T(8,128)}, u32[]{:S(2)}) copy-start(s32[512,8]{0,1:T(8,128)} %param.22) | copy-start | bytes 49156
  3.2 12.8 %copy-start.7 = (bf16[512,8]{0,1:T(8,128)(2,1)S(1)}, bf16[512,8]{0,1:T(8,128)(2,1)}, u32[]{:S(2)}) copy-start(bf16[512,8]{0,1:T(8,128)(2,1)} %param.23) | copy-start | bytes 24580
  3.2 12.8 %copy-start.8 = (s32[128,1]{0,1:T(1,128)S(1)}, s32[128,1]{0,1:T(1,128)}, u32[]{:S(2)}) copy-start(s32[128,1]{0,1:T(1,128)} %param.20) | copy-start | bytes 1540
  3.2 34.1 %all-to-all-start = ((bf16[64,24,512]{2,1,0:T(8,128)(2,1)}), bf16[64,24,512]{2,1,0:T(8,128)(2,1)S(1)}, u32[]{:S(2)}, u32[]{:S(2)}) async-start(bf16[64,24,512]{2,1,0:T(8,128)(2,1)} %shard_map.158), calls=%async_computation | async-start | bytes 3145728 | tf_op jit(solution)/shard_map/all_to_all | solution.py:66
  25.5 18.3 %collective-permute-start = (bf16[1792,512]{1,0:T(8,128)(2,1)S(1)}, bf16[1792,512]{1,0:T(8,128)(2,1)}, u32[]{:S(2)}, u32[]{:S(2)}) collective-permute-start(bf16[1792,512]{1,0:T(8,128)(2,1)S(1)} %get-tuple-element.42), channel_id=1, source_target_pairs={{0,1},{1,0},{2,3},{3,2},{4,5},{5,4},{6,7},{7,6},{8,9},{9,8},{10,11... | collective-permute-start | bytes 5505032 | tf_op jit(solution)/shard_map/ppermute | solution.py:58
  37.3 7.3 %collective-permute-start.2 = (bf16[64,24,512]{2,1,0:T(8,128)(2,1)S(1)}, bf16[64,24,512]{2,1,0:T(8,128)(2,1)S(1)}, u32[]{:S(2)}, u32[]{:S(2)}) collective-permute-start(bf16[64,24,512]{2,1,0:T(8,128)(2,1)S(1)} %all-to-all-done.bundle), channel_id=1, source_target_pairs={{0,1},{1,0},{2,3},{3,2},{4,5},{5,4},{6,7},{7,6},{8,9},{9,8},{10,11... | collective-permute-start | bytes 4718600 | tf_op jit(solution)/shard_map/ppermute | solution.py:58
  40.4 3.4 %collective-permute-start.1 = (f32[512,1]{1,0:T(8,128)}, f32[512,1]{1,0:T(8,128)S(1)}, u32[]{:S(2)}, u32[]{:S(2)}) collective-permute-start(f32[512,1]{1,0:T(8,128)} %get-tuple-element.43.degree_at), channel_id=1, source_target_pairs={{0,1},{1,0},{2,3},{3,2},{4,5},{5,4},{6,7},{7,6},{8,9},{9,8},{10,11... | collective-permute-start | bytes 6152 | tf_op jit(solution)/shard_map/ppermute | solution.py:58
  43.8 0.7 copy-start.9
  47.4 2.4 %collective-permute-start.3 = (bf16[768,512]{1,0:T(8,128)(2,1)S(1)}, bf16[768,512]{1,0:T(8,128)(2,1)S(1)}, u32[]{:S(2)}, u32[]{:S(2)}) collective-permute-start(bf16[768,512]{1,0:T(8,128)(2,1)S(1)} %get-tuple-element.60.pack), channel_id=1, source_target_pairs={{0,1},{1,0},{2,3},{3,2},{4,5},{5,4},{6,7},{7,6},{8,9},{9,8},{10,11... | collective-permute-start | bytes 2359304 | tf_op jit(solution)/shard_map/ppermute | solution.py:58
  83.2 22.3 %copy-start = (bf16[512,512]{1,0:T(8,128)(2,1)S(1)}, bf16[512,512]{1,0:T(8,128)(2,1)}, u32[]{:S(2)}) copy-start(bf16[512,512]{1,0:T(8,128)(2,1)} %lweight.1) | copy-start | bytes 1572868
  83.2 22.3 %copy-start.1 = (bf16[512,512]{1,0:T(8,128)(2,1)S(1)}, bf16[512,512]{1,0:T(8,128)(2,1)}, u32[]{:S(2)}) copy-start(bf16[512,512]{1,0:T(8,128)(2,1)} %wself.1) | copy-start | bytes 1572868
  83.2 22.3 %copy-start.2 = (bf16[512,512]{1,0:T(8,128)(2,1)S(1)}, bf16[512,512]{1,0:T(8,128)(2,1)}, u32[]{:S(2)}) copy-start(bf16[512,512]{1,0:T(8,128)(2,1)} %get-tuple-element.63.gmean) | copy-start | bytes 1572868
  102.8 4.2 %copy-start.3 = (s32[128,4]{0,1:T(4,128)S(1)}, s32[128,4]{0,1:T(4,128)}, u32[]{:S(2)}) copy-start(s32[128,4]{0,1:T(4,128)} %param.19) | copy-start | bytes 6148
  102.8 4.2 %copy-start.5 = (s32[16]{0:T(128)S(1)}, s32[16]{0:T(128)}, u32[]{:S(2)}) copy-start(s32[16]{0:T(128)} %param.21) | copy-start | bytes 196
  102.8 6.8 %collective-permute-start.4 = (bf16[64,8,512]{2,1,0:T(8,128)(2,1)S(1)}, bf16[64,8,512]{2,1,0:T(8,128)(2,1)S(1)}, u32[]{:S(2)}, u32[]{:S(2)}) collective-permute-start(bf16[64,8,512]{2,1,0:T(8,128)(2,1)S(1)} %all_to_all.16.source), channel_id=1, source_target_pairs={{0,1},{1,0},{2,3},{3,2},{4,5},{5,4},{6,7},{7,6},{8,9},{9,8},{10,11... | collective-permute-start | bytes 1572872 | tf_op jit(solution)/shard_map/ppermute | solution.py:58
